TPU v7x, 32 devices: a whole 2x2x4 slice. The times are simulated.
32 devices in a mesh: dp: 8 (over y, x, core), mp: 4 (over z).
Axes of the slice: x: 2, y: 2, z: 4, core: 2. Of those that a mesh axis runs over, the one named last changes fastest.
Arguments:
- tokens: bfloat16 [512, 32, 1024], P('mp', 'dp'), may hold values from -6 to 6
- timesteps: int32 [32], P('dp'), may hold values from 0 to 4999
- buckets: int32 [32], P('dp'), may hold values from 0 to 31
- counts: int32 [8], replicated, may hold values from 1 to 4, as said below
- w_time: bfloat16 [1024, 1024], replicated, may hold values from -0.1875 to 0.1875
- table: float32 [32, 1024], replicated, may hold values from -3 to 3
- w_qkv: bfloat16 [3, 1024, 1024], P(None, None, 'mp'), may hold values from -0.1875 to 0.1875
- b_qv: float32 [2, 1024], P(None, 'mp'), may hold values from -0.6 to 0.6
- w_out: bfloat16 [1024, 1024], P('mp'), may hold values from -0.5 to 0.5
- b_out: float32 [1024], replicated, may hold values from -2 to 2
- gain1: float32 [1024], replicated, may hold values from 0.5 to 1.5
- shift1: float32 [1024], replicated, may hold values from -1.2 to 1.2
- w_up: bfloat16 [1024, 4096], P(None, 'mp'), may hold values from -0.1875 to 0.1875
- b_up: float32 [4096], P('mp'), may hold values from -3 to 3
- w_down: bfloat16 [4096, 1024], P('mp'), may hold values from -0.09375 to 0.09375
- b_down: float32 [1024], replicated, may hold values from -2 to 2
- gain2: float32 [1024], replicated, may hold values from 0.5 to 1.5
- shift2: float32 [1024], replicated, may hold values from -1.2 to 1.2
- cotangent: bfloat16 [512, 32, 1024], P('mp', 'dp'), may hold values from -6 to 6
Outputs:
- output: bfloat16 [512, 32, 1024], P('mp', 'dp')
- grad_tokens: float32 [512, 32, 1024], P('mp', 'dp')
- grad_w_time: float32 [1024, 1024], P(None, ('dp', 'mp'))
- grad_table: float32 [32, 1024], P(None, ('dp', 'mp'))
- grad_w_qkv: float32 [3, 1024, 1024], P(None, 'dp', 'mp')
- grad_b_qv: float32 [2, 1024], P(None, ('dp', 'mp'))
- grad_w_out: float32 [1024, 1024], P('mp', 'dp')
- grad_b_out: float32 [1024], P(('dp', 'mp'))
- grad_gain1: float32 [1024], P(('dp', 'mp'))
- grad_shift1: float32 [1024], P(('dp', 'mp'))
- grad_w_up: float32 [1024, 4096], P('dp', 'mp')
- grad_b_up: float32 [4096], P(('dp', 'mp'))
- grad_w_down: float32 [4096, 1024], P('mp', 'dp')
- grad_b_down: float32 [1024], P(('dp', 'mp'))
- grad_gain2: float32 [1024], P(('dp', 'mp'))
- grad_shift2: float32 [1024], P(('dp', 'mp'))
Inputs may be any that keep to these rules, and one draw needn't show every extreme that they name: Slot s of group g holds a live item iff s < counts[g]; in every draw some group has all 4 slots live.
All inputs are finite; a program needn't handle non-finite values.
Results may differ from a plain program's by a relative error of at most 0.025.
Values may be sent and summed in bfloat16 or wider, within the bound.
No kernel may reach another device: no remote copies, remote signals or barrier semaphores. Data moves between devices by JAX's collectives and lax.ppermute only.
A program may use at most 192 MiB of HBM per device.

v0:
```python
import functools
import math

import jax
import jax.numpy as jnp
from jax import lax
from jax.experimental import pallas as pl
from jax.experimental.pallas import tpu as pltpu
from jax.sharding import PartitionSpec as P

HD = 64
f32 = jnp.float32
bf16 = jnp.bfloat16
VMEM_LIMIT = 56 * 2**20


def params(**more):
    return pltpu.CompilerParams(vmem_limit_bytes=VMEM_LIMIT, **more)


def dot(a, b, dims):
    return lax.dot_general(a, b, (dims, ((), ())), preferred_element_type=f32)


def sinusoid(steps, model_width):
    half_width = model_width // 2
    freqs = jnp.exp(-math.log(10000.0) * jnp.arange(half_width, dtype=f32) / half_width)
    angles = steps[:, None] * freqs[None, :]
    return jnp.concatenate([jnp.sin(angles), jnp.cos(angles)], axis=-1).astype(bf16)


def masks(place):
    first = 2 + 2 * (place & 1)
    return first, 6 - first


class Gathered:
    def __init__(self, own, pieces, lead, start):
        self.arrays = [own] + pieces
        self.lead = lead
        self.start = start
        self.dims = own.shape

    def scratch(self, shards):
        return [pltpu.VMEM((shards,) + self.dims, bf16), pltpu.SemaphoreType.DMA((shards, 8))]

    def copies_of(self, refs, place, into, sems, shard, slot):
        if isinstance(shard, int) and shard == 0:
            return [pltpu.make_async_copy(refs[0], into.at[slot], sems.at[slot, 0])]
        lead = (slice(None),) * self.lead
        first, second = masks(place)
        held = (place, place ^ first)
        far = (place ^ second, place ^ 6)
        held2 = (place ^ 1, place ^ 1 ^ second)
        far2 = (place ^ 1 ^ first, place ^ 7)
        made = []
        for ref, chunks in zip(refs[1:], (held, far, held2, far2)):
            for i, chunk in enumerate(chunks):
                at = lead + (pl.ds(self.start, self.dims[-2]),)
                made.append(
                    pltpu.make_async_copy(
                        ref.at[i, shard - 1].at[at],
                        into.at[(slot,) + lead + (chunk,)],
                        sems.at[slot, len(made)],
                    )
                )
        return made

    def start_all(self, refs, place, into, sems, shards):
        for shard in range(shards):
            for copy in self.copies_of(refs, place, into, sems, shard, shard):
                copy.start()

    def wait(self, refs, place, into, sems, shard):
        @pl.when(shard == 0)
        def _():
            for copy in self.copies_of(refs, place, into, sems, 0, 0):
                copy.wait()

        @pl.when(shard > 0)
        def _():
            for copy in self.copies_of(refs, place, into, sems, shard, shard):
                copy.wait()


HBM = pl.BlockSpec(memory_space=pl.ANY)
SMEM = pl.BlockSpec(memory_space=pltpu.SMEM)


def whole(shape):
    return pl.BlockSpec(shape, lambda *_: (0,) * len(shape))


def cost(micros):
    return pl.CostEstimate(flops=int(micros * 1.15e9), transcendentals=0, bytes_accessed=0)


def over_rows(length, step, body, init):
    def one(i, carry):
        return body(pl.ds(pl.multiple_of(i * step, step), step), carry)

    return lax.fori_loop(0, length // step, one, init)


def row_sum(v):
    return jnp.sum(v, axis=0, keepdims=True)


def pack_body(rows, n, with_sum, *refs):
    parts, out_ref = refs[:n], refs[n]
    sems = refs[-1]
    lead = (slice(None),) * (len(parts[0].shape) - 2)
    copies = []
    for i, ref in enumerate(parts):
        at = lead + (pl.ds(0, rows),)
        copies.append(pltpu.make_async_copy(ref.at[at], out_ref.at[i], sems.at[len(copies)]))
        if with_sum:
            at = lead + (pl.ds(rows, 8),)
            copies.append(pltpu.make_async_copy(ref.at[at], refs[-2].at[i], sems.at[len(copies)]))
    for copy in copies:
        copy.start()
    for copy in copies:
        copy.wait()
    if with_sum:
        extra = refs[-2][...].astype(f32)
        refs[n + 1][...] = sum(extra[..., i : i + 1, :] for i in range(3))


def pack(covers, parts, rows=None):
    dims = parts[0].shape
    n = len(parts)
    lead = (n,) + dims[:-2]
    out = [jax.ShapeDtypeStruct(lead + (rows or dims[-2], dims[-1]), bf16)]
    scratch = []
    if rows:
        out.append(jax.ShapeDtypeStruct(lead + (1, dims[-1]), f32))
        scratch.append(pltpu.VMEM(lead + (8, dims[-1]), bf16))
    made = pl.pallas_call(
        functools.partial(pack_body, rows or dims[-2], n, bool(rows)),
        out_shape=out,
        in_specs=[HBM] * n,
        out_specs=[pl.BlockSpec(memory_space=pltpu.VMEM)] * len(out),
        scratch_shapes=scratch + [pltpu.SemaphoreType.DMA((2 * n,))],
        compiler_params=params(),
        cost_estimate=cost(covers),
        name="pack",
    )(*parts)
    return made if rows else made[0]


def in_three(v):
    parts = []
    for _ in range(3):
        parts.append(lax.reduce_precision(v, 8, 7))
        v = v - parts[-1]
    return jnp.concatenate(parts + [jnp.zeros_like(v)] * 5, axis=-2).astype(bf16)


def embed_body(sinus_ref, w_ref, row_ref, out_ref):
    out_ref[...] = dot(sinus_ref[...], w_ref[...], ((1,), (0,)))[:1] + row_ref[...]


def embed(covers, sinus, w, row):
    return pl.pallas_call(
        embed_body,
        out_shape=jax.ShapeDtypeStruct(row.shape, f32),
        compiler_params=params(),
        cost_estimate=cost(covers),
        name="embed",
    )(jnp.broadcast_to(sinus, (16,) + sinus.shape[1:]), w, row)


def attend_body(shard, gathered, place_ref, x_hbm, bias_ref, *refs):
    n = len(gathered.arrays)
    w_refs = refs[:n]
    qkv_ref, p_ref, c_ref, w, sems, x_ref, x_sem = refs[-7:]
    pair = pl.program_id(0)
    place = place_ref[0]
    cols = w.shape[-1]

    @pl.when(pair == 0)
    def _():
        copies = [pltpu.make_async_copy(x_hbm, x_ref, x_sem.at[0])]
        copies += gathered.copies_of(w_refs, place, w, sems, shard, 0)
        for copy in copies:
            copy.start()
        for copy in copies:
            copy.wait()
        for c in range(3):
            wide = w[0, c].reshape(x_ref.shape[1], cols)
            out = dot(x_ref[...], wide, ((1,), (0,))) + bias_ref[0, c]
            qkv_ref[0, :, c * cols : (c + 1) * cols] = out.astype(bf16)

    at = pl.multiple_of(pair * 2 * HD, 2 * HD)
    q = qkv_ref[0, :, pl.ds(at, 2 * HD)]
    k = qkv_ref[0, :, pl.ds(cols + at, 2 * HD)]
    v = qkv_ref[0, :, pl.ds(2 * cols + at, 2 * HD)]
    lane = lax.broadcasted_iota(jnp.int32, q.shape, 1)
    joined = None
    for hh in range(2):
        mine = (lane // HD) == hh
        kh = jnp.where(mine, k, jnp.zeros_like(k))
        st = dot(kh, q, ((1,), (1,))) * 0.125
        top = jnp.max(st, axis=0, keepdims=True)
        e = jnp.exp(st - top)
        p = (e * (1.0 / jnp.sum(e, axis=0, keepdims=True))).astype(bf16)
        p_ref[0, hh] = p
        c = dot(p, v, ((0,), (0,)))
        joined = c if joined is None else jnp.where(mine, c, joined)
    c_ref[0] = joined.astype(bf16)


def attend(covers, shard, shards, gathered, place, x, bias, old):
    length, width = x.shape
    cols = gathered.dims[-1]
    pairs = cols // (2 * HD)
    n_w = len(gathered.arrays)
    return pl.pallas_call(
        functools.partial(attend_body, shard, gathered),
        grid=(pairs,),
        out_shape=[
            jax.ShapeDtypeStruct((shards, length, 3 * cols), bf16),
            jax.ShapeDtypeStruct((shards, 2 * pairs, length, length), bf16),
            jax.ShapeDtypeStruct((shards, length, cols), bf16),
        ],
        in_specs=[SMEM, HBM, pl.BlockSpec((1, 3, 1, cols), lambda i: (max(shard - 1, 0), 0, 0, 0))]
        + [HBM] * (n_w + len(old)),
        out_specs=[
            pl.BlockSpec((1, length, 3 * cols), lambda i: (shard, 0, 0)),
            pl.BlockSpec((1, 2, length, length), lambda i: (shard, i, 0, 0)),
            pl.BlockSpec((1, length, 2 * HD), lambda i: (shard, 0, i)),
        ],
        input_output_aliases={3 + n_w + i: i for i in range(len(old))},
        scratch_shapes=gathered.scratch(1) + [pltpu.VMEM(x.shape, bf16), pltpu.SemaphoreType.DMA((1,))],
        compiler_params=params(),
        cost_estimate=cost(covers),
        name="attend",
    )(place, x, bias, *gathered.arrays, *old)


def norm_stats(values):
    center = values - jnp.mean(values, axis=-1, keepdims=True)
    inv = lax.rsqrt(jnp.mean(center * center, axis=-1, keepdims=True) + 1e-05)
    return center * inv, inv


def norm_back(grad, n, inv, gain):
    gn = grad * gain
    return (gn - jnp.mean(gn, -1, keepdims=True) - n * jnp.mean(gn * n, -1, keepdims=True)) * inv


def up_body(
    shards, g_out, g_up, place_ref, ctx_ref, x_ref, te_ref, b_ref, gain_ref, shift_ref, bias_ref, *refs
):
    n_out = len(g_out.arrays)
    out_refs = list(refs[:n_out])
    up_refs = [refs[n_out]] + list(refs[1:n_out])
    n1_ref, inv_ref, low_ref, act_ref, slope_ref, wo_full = refs[n_out + 1 : n_out + 7]
    wo, o_sems, wu, u_sems, acc, keep_o = refs[n_out + 7 :]
    s = pl.program_id(0)
    place = place_ref[0]
    length, width = acc.shape

    def keep_out(shard):
        return pltpu.make_async_copy(wo.at[shard], wo_full.at[shard], keep_o.at[shard])

    @pl.when(s == 0)
    def _():
        g_out.start_all(out_refs, place, wo, o_sems, shards)
        g_up.start_all(up_refs, place, wu, u_sems, shards)
        for shard in range(shards):
            g_out.wait(out_refs, place, wo, o_sems, shard)
            keep_out(shard).start()
            part = dot(ctx_ref[shard], wo[shard].reshape(-1, width), ((1,), (0,)))
            if shard == 0:
                acc[...] = part
            else:
                acc[...] += part

        def rows(at, _):
            start = x_ref[at, :].astype(f32) + te_ref[...]
            n1, inv = norm_stats(start + (acc[at, :] + b_ref[...]))
            n1_ref[at, :] = n1
            inv_ref[at, :] = jnp.broadcast_to(inv, (64, inv_ref.shape[1]))
            low_ref[at, :] = (n1 * gain_ref[...] + shift_ref[...]).astype(bf16)
            return 0

        over_rows(length, 64, rows, 0)

    g_up.wait(up_refs, place, wu, u_sems, s)
    units = wu.shape[-1]

    def columns(n, _):
        span = pl.ds(pl.multiple_of(n * 256, 256), 256)
        u = dot(low_ref[...], wu[s, :, :, span].reshape(width, 256), ((1,), (0,)))
        u = u + bias_ref[0, :, span]
        phi = 0.5 + 0.5 * lax.erf(u * (2.0**-0.5))
        act_ref[0, :, span] = (u * phi).astype(bf16)
        slope = phi + u * jnp.exp(-0.5 * u * u) * (2.0 * math.pi) ** -0.5
        slope_ref[0, :, span] = slope.astype(bf16)
        return 0

    lax.fori_loop(0, units // 256, columns, 0)

    @pl.when(s == shards - 1)
    def _():
        for shard in range(shards):
            keep_out(shard).wait()


def up_project(g_out, g_up, place, ctx, x, time_embed, b_out, gain, shift, bias):
    length, width = x.shape
    shards = ctx.shape[0]
    units = g_up.dims[-1]
    block = pl.BlockSpec((1, length, units), lambda s: (s, 0, 0))
    row = whole((1, width))
    return pl.pallas_call(
        functools.partial(up_body, shards, g_out, g_up),
        grid=(shards,),
        out_shape=[
            jax.ShapeDtypeStruct((length, width), f32),
            jax.ShapeDtypeStruct((length, 128), f32),
            jax.ShapeDtypeStruct((length, width), bf16),
            jax.ShapeDtypeStruct((shards, length, units), bf16),
            jax.ShapeDtypeStruct((shards, length, units), bf16),
            jax.ShapeDtypeStruct((shards,) + g_out.dims, bf16),
        ],
        in_specs=[
            SMEM,
            whole(ctx.shape),
            whole(x.shape),
            row,
            row,
            row,
            row,
            pl.BlockSpec((1, 1, units), lambda s: (s, 0, 0)),
        ]
        + [HBM] * (len(g_out.arrays) + 1),
        out_specs=[
            whole((length, width)),
            whole((length, 128)),
            whole((length, width)),
            block,
            block,
            HBM,
        ],
        scratch_shapes=g_out.scratch(shards)
        + g_up.scratch(shards)
        + [pltpu.VMEM((length, width), f32)]
        + [pltpu.SemaphoreType.DMA((shards,))],
        compiler_params=params(),
        cost_estimate=cost(300),
        name="up_project",
    )(place, ctx, x, time_embed, b_out, gain, shift, bias, *g_out.arrays, g_up.arrays[0])


def down_body(
    shards, gathered, place_ref, live_ref, act_ref, b_ref, gain1_ref, shift1_ref, gain2_ref, shift2_ref,
    n1_hbm, cot_hbm, *refs
):
    n = len(gathered.arrays)
    w_refs, (out_hbm, bg_hbm, sums_ref) = refs[:n], refs[n : n + 3]
    w, sems, acc, n1_ref, cot_ref, late, out_ref, bg_ref, done = refs[n + 3 :]
    s = pl.program_id(0)
    place = place_ref[0]
    length, width = acc.shape

    def fetch(i):
        return pltpu.make_async_copy((n1_hbm, cot_hbm)[i], (n1_ref, cot_ref)[i], late.at[i])

    @pl.when(s == 0)
    def _():
        gathered.start_all(w_refs, place, w, sems, shards)
        fetch(0).start()
        fetch(1).start()

    gathered.wait(w_refs, place, w, sems, s)
    part = dot(act_ref[0], w[s].reshape(-1, width), ((1,), (0,)))

    @pl.when(s == 0)
    def _():
        acc[...] = part

    @pl.when(s > 0)
    def _():
        acc[...] += part

    @pl.when(s == shards - 1)
    def _():
        live = live_ref[0]
        fetch(0).wait()
        fetch(1).wait()

        def leave(i):
            at = pl.ds(i * 64, 64)
            return [
                pltpu.make_async_copy(out_ref.at[at], out_hbm.at[at], done.at[0, i]),
                pltpu.make_async_copy(bg_ref.at[at], bg_hbm.at[at], done.at[1, i]),
            ]

        def rows(i, sums):
            at = pl.ds(pl.multiple_of(i * 64, 64), 64)
            normed = n1_ref[at, :] * gain1_ref[...] + shift1_ref[...]
            n2, inv = norm_stats(normed + (acc[at, :] + b_ref[...]))
            out_ref[at, :] = (n2 * gain2_ref[...] + shift2_ref[...]).astype(bf16)
            grad = cot_ref[at, :].astype(f32) * live
            second = norm_back(grad, n2, inv, gain2_ref[...])
            low = second.astype(bf16)
            bg_ref[at, :] = low
            for copy in leave(i):
                copy.start()
            add = (low.astype(f32), grad * n2, grad)
            return tuple(a + row_sum(b) for a, b in zip(sums, add))

        zero = jnp.zeros((1, width), f32)
        sums = lax.fori_loop(0, length // 64, rows, (zero, zero, zero))
        for i, v in enumerate(sums):
            sums_ref[i : i + 1, :] = v
        for i in range(length // 64):
            for copy in leave(i):
                copy.wait()


def down_project(gathered, place, live, act, n1, cot, b_down, gain1, shift1, gain2, shift2):
    shards, length, units = act.shape
    width = n1.shape[1]
    row = whole((1, width))
    return pl.pallas_call(
        functools.partial(down_body, shards, gathered),
        grid=(shards,),
        out_shape=[
            jax.ShapeDtypeStruct((length, width), bf16),
            jax.ShapeDtypeStruct((length, width), bf16),
            jax.ShapeDtypeStruct((3, width), f32),
        ],
        in_specs=[SMEM, SMEM, pl.BlockSpec((1, length, units), lambda s: (s, 0, 0))]
        + [row] * 5
        + [HBM] * (2 + len(gathered.arrays)),
        out_specs=[HBM] * 2 + [whole((3, width))],
        scratch_shapes=gathered.scratch(shards)
        + [
            pltpu.VMEM((length, width), f32),
            pltpu.VMEM((length, width), f32),
            pltpu.VMEM((length, width), bf16),
            pltpu.SemaphoreType.DMA((2,)),
            pltpu.VMEM((length, width), bf16),
            pltpu.VMEM((length, width), bf16),
            pltpu.SemaphoreType.DMA((2, length // 64)),
        ],
        compiler_params=params(),
        cost_estimate=cost(300),
        name="down_project",
    )(place, live, act, b_down, gain1, shift1, gain2, shift2, n1, cot, *gathered.arrays)


def up_back_body(
    shards, g_down, g_up, place_ref, bg_ref, slope_ref, inv_ref, gain_ref, n1_hbm, *refs
):
    n = len(g_down.arrays)
    d_refs, u_refs = list(refs[:n]), [refs[n]] + list(refs[n + 1 : 2 * n])
    ug_ref, bias_ref, gf_ref, mg_ref, sums_ref = refs[2 * n : 2 * n + 5]
    wd, d_sems, wu, u_sems, acc, n1_ref, late = refs[2 * n + 5 :]
    s = pl.program_id(0)
    place = place_ref[0]
    length, width = acc.shape

    fetch = pltpu.make_async_copy(n1_hbm, n1_ref, late.at[0])

    @pl.when(s == 0)
    def _():
        for shard in range(shards):
            for copy in g_down.copies_of(d_refs, place, wd, d_sems, shard, shard):
                copy.start()
            for copy in g_up.copies_of(u_refs, place, wu, u_sems, shard, shard):
                copy.start()
        fetch.start()

    g_down.wait(d_refs, place, wd, d_sems, s)
    units = ug_ref.shape[2]

    def columns(n, _):
        span = pl.ds(pl.multiple_of(n * 256, 256), 256)
        rows = wd[s, pl.ds(2 * n, 2)].reshape(256, width)
        grad = dot(bg_ref[...], rows, ((1,), (1,)))
        low = (grad * slope_ref[0, :, span].astype(f32)).astype(bf16)
        ug_ref[0, :, span] = low
        bias_ref[0, :, span] = row_sum(low.astype(f32))
        return 0

    lax.fori_loop(0, units // 256, columns, 0)
    g_up.wait(u_refs, place, wu, u_sems, s)
    part = dot(ug_ref[0], wu[s].reshape(width, units), ((1,), (1,)))

    @pl.when(s == 0)
    def _():
        acc[...] = part

    @pl.when(s > 0)
    def _():
        acc[...] += part

    @pl.when(s == shards - 1)
    def _():
        fetch.wait()

        def rows(at, sums):
            n1, grad = n1_ref[at, :], acc[at, :] + bg_ref[at, :].astype(f32)
            first = norm_back(grad, n1, inv_ref[at, 0:1], gain_ref[...])
            gf_ref[at, :] = first
            low = first.astype(bf16)
            mg_ref[at, :] = low
            add = (low.astype(f32), grad * n1, grad)
            return tuple(a + row_sum(b) for a, b in zip(sums, add))

        zero = jnp.zeros((1, width), f32)
        sums = over_rows(length, 64, rows, (zero, zero, zero))
        for i, v in enumerate(sums):
            sums_ref[i : i + 1, :] = v


def up_back(g_down, g_up, place, bg, slope, n1, inv, gain):
    shards, length, units = slope.shape
    width = n1.shape[1]
    block = pl.BlockSpec((1, length, units), lambda s: (s, 0, 0))
    return pl.pallas_call(
        functools.partial(up_back_body, shards, g_down, g_up),
        grid=(shards,),
        out_shape=[
            jax.ShapeDtypeStruct((shards, length, units), bf16),
            jax.ShapeDtypeStruct((shards, 1, units), f32),
            jax.ShapeDtypeStruct((length, width), f32),
            jax.ShapeDtypeStruct((length, width), bf16),
            jax.ShapeDtypeStruct((3, width), f32),
        ],
        in_specs=[SMEM, whole(bg.shape), block, whole(inv.shape), whole((1, width))]
        + [HBM] * (1 + len(g_down.arrays) + len(g_up.arrays)),
        out_specs=[
            block,
            pl.BlockSpec((1, 1, units), lambda s: (s, 0, 0)),
            whole((length, width)),
            whole((length, width)),
            whole((3, width)),
        ],
        scratch_shapes=g_down.scratch(shards)
        + g_up.scratch(shards)
        + [pltpu.VMEM((length, width), f32)] * 2
        + [pltpu.SemaphoreType.DMA((1,))],
        compiler_params=params(),
        cost_estimate=cost(300),
        name="up_back",
    )(place, bg, slope, inv, gain, n1, *g_down.arrays, *g_up.arrays)


def attend_back_body(mg_ref, wo_ref, qkv, p_of, *refs):
    pg_ref, bias_ref, cg = refs[-3:]
    pair = pl.program_id(1)
    cols = cg.shape[1]

    @pl.when(pair == 0)
    def _():
        cg[...] = dot(mg_ref[...], wo_ref[0], ((1,), (1,))).astype(bf16)

    at = pl.multiple_of(pair * 2 * HD, 2 * HD)
    q = qkv[0, :, pl.ds(at, 2 * HD)]
    k = qkv[0, :, pl.ds(cols + at, 2 * HD)]
    v = qkv[0, :, pl.ds(2 * cols + at, 2 * HD)]
    g = cg[:, pl.ds(at, 2 * HD)]
    lane = lax.broadcasted_iota(jnp.int32, q.shape, 1)
    dq = dk = dv = None
    for hh in range(2):
        mine = (lane // HD) == hh
        zero = jnp.zeros_like(q)
        gh = jnp.where(mine, g, zero)
        kh = jnp.where(mine, k, zero)
        qh = jnp.where(mine, q, zero)
        p = p_of[0, hh]
        dpt = dot(v, gh, ((1,), (1,)))
        pf = p.astype(f32)
        row = row_sum(pf * dpt)
        ds = (pf * (dpt - row)).astype(bf16)
        a = dot(p, gh, ((1,), (0,)))
        b = dot(ds, qh, ((1,), (0,)))
        c = dot(ds, kh, ((0,), (0,)))
        dv = a if dv is None else dv + a
        dk = b if dk is None else dk + b
        dq = c if dq is None else dq + c
    for c, g in enumerate((dq * 0.125, dk * 0.125, dv)):
        low = g.astype(bf16)
        pg_ref[0, :, pl.ds(c * cols + at, 2 * HD)] = low
        bias_ref[0, :, pl.ds(c * cols + at, 2 * HD)] = row_sum(low.astype(f32))


def attend_back(covers, base, count, w_out, mg, qkv, p, pg):
    length, width = mg.shape
    shards, cols = w_out.shape[:2]
    pairs = cols // (2 * HD)
    old = [] if pg is None else [pg]
    return pl.pallas_call(
        attend_back_body,
        grid=(count, pairs),
        out_shape=[
            jax.ShapeDtypeStruct((shards, length, 3 * cols), bf16),
            jax.ShapeDtypeStruct((count, 1, 3 * cols), f32),
        ],
        in_specs=[
            whole(mg.shape),
            pl.BlockSpec((1, cols, width), lambda s, i: (s + base, 0, 0)),
            pl.BlockSpec((1, length, 3 * cols), lambda s, i: (s + base, 0, 0)),
            pl.BlockSpec((1, 2, length, length), lambda s, i: (s + base, i, 0, 0)),
        ]
        + [HBM] * len(old),
        out_specs=[
            pl.BlockSpec((1, length, 3 * cols), lambda s, i: (s + base, 0, 0)),
            pl.BlockSpec((1, 1, 3 * cols), lambda s, i: (s, 0, 0)),
        ],
        input_output_aliases={4: 0} if old else {},
        scratch_shapes=[pltpu.VMEM((length, cols), bf16)],
        compiler_params=params(),
        cost_estimate=cost(covers),
        name="attend_back",
    )(mg, w_out, qkv, p, *old)


def input_back_body(shards, gathered, place_ref, pg_ref, gf_hbm, *refs):
    n = len(gathered.arrays)
    w_refs, (gt_ref, tg_ref, w, sems, acc, gf_ref, late) = refs[:n], refs[n:]
    s = pl.program_id(0)
    place = place_ref[0]
    cols = w.shape[-1]
    length, width = acc.shape
    fetch = pltpu.make_async_copy(gf_hbm, gf_ref, late.at[0])

    @pl.when(s == 0)
    def _():
        gathered.start_all(w_refs, place, w, sems, shards)
        fetch.start()
        acc[...] = jnp.zeros_like(acc)

    gathered.wait(w_refs, place, w, sems, s)
    part = None
    for c in range(3):
        new = dot(pg_ref[0, :, c * cols : (c + 1) * cols], w[s, c].reshape(width, cols), ((1,), (1,)))
        part = new if part is None else part + new
    acc[...] += part

    @pl.when(s == shards - 1)
    def _():
        fetch.wait()

        def rows(at, total):
            grad = acc[at, :] + gf_ref[at, :]
            gt_ref[at, :] = grad.astype(bf16)
            return total + row_sum(grad)

        tg_ref[...] = over_rows(length, 64, rows, jnp.zeros((1, width), f32))


def input_back(gathered, place, pg, gf):
    shards, length, cols3 = pg.shape
    width = gf.shape[1]
    return pl.pallas_call(
        functools.partial(input_back_body, shards, gathered),
        grid=(shards,),
        out_shape=[
            jax.ShapeDtypeStruct((length, width), bf16),
            jax.ShapeDtypeStruct((1, width), f32),
        ],
        in_specs=[SMEM, pl.BlockSpec((1, length, cols3), lambda s: (s, 0, 0)), HBM]
        + [HBM] * len(gathered.arrays),
        out_specs=[whole((length, width)), whole((1, width))],
        scratch_shapes=gathered.scratch(shards)
        + [pltpu.VMEM((length, width), f32)] * 2
        + [pltpu.SemaphoreType.DMA((1,))],
        compiler_params=params(),
        cost_estimate=cost(1),
        name="input_back",
    )(place, pg, gf, *gathered.arrays)


def weight_grad_body(n_pairs, looped, place_ref, *refs):
    ins = refs[: 4 * n_pairs]
    keep_ref, send_ref = refs[4 * n_pairs : 4 * n_pairs + 2]
    turned = refs[4 * n_pairs + 2 :]
    place = place_ref[0]
    rows = keep_ref.shape[2]
    first, second = masks(place)

    @pl.when(pl.program_id(0) == 0)
    def _():
        for p in range(n_pairs):
            for core in range(2):
                feature_ref = ins[4 * p + core]
                length = feature_ref.shape[0]
                for j, mask in enumerate((0, second, first, 6)):
                    at = pl.multiple_of((place ^ mask) * rows, rows)
                    block = feature_ref[:, pl.ds(at, rows)]
                    turned[p][j * rows : (j + 1) * rows, core * length : (core + 1) * length] = block.T

    at = 0
    for p in range(n_pairs):
        b_ref, b2_ref = ins[4 * p + 2 : 4 * p + 4]
        length, cols = b_ref.shape[1:]

        def columns(n, _, p=p, b_ref=b_ref, b2_ref=b2_ref, length=length, at=at):
            start = n * 256 if isinstance(n, int) else pl.multiple_of(n * 256, 256)
            g = dot(turned[p][:, :length], b_ref[0, :, pl.ds(start, 256)], ((1,), (0,)))
            g += dot(turned[p][:, length:], b2_ref[0, :, pl.ds(start, 256)], ((1,), (0,)))
            g = g.astype(bf16)
            to = pl.ds(at + start if isinstance(n, int) else pl.multiple_of(at + start, 256), 256)
            for i in range(2):
                keep_ref[i, 0, :, to] = g[i * rows : (i + 1) * rows]
                send_ref[i, 0, :, to] = g[(i + 2) * rows : (i + 3) * rows]
            return 0

        if looped:
            lax.fori_loop(0, cols // 256, columns, 0)
        else:
            for n in range(cols // 256):
                columns(n, 0)
        at += cols


def weight_grad(covers, place, groups, looped=False):
    shards, length, _ = groups[0][2].shape
    rows = groups[0][0].shape[1] // 8
    cols = sum(g[2].shape[2] for g in groups)
    specs, args, scratch = [], [], []
    for feature, feature2, b, b2 in groups:
        block = pl.BlockSpec((1,) + b.shape[1:], lambda s: (s, 0, 0))
        specs += [whole(feature.shape)] * 2 + [block] * 2
        args += [feature, feature2, b, b2]
        scratch.append(pltpu.VMEM((4 * rows, 2 * length), bf16))
    out = jax.ShapeDtypeStruct((2, shards, rows, cols), bf16)
    return pl.pallas_call(
        functools.partial(weight_grad_body, len(groups), looped),
        grid=(shards,),
        out_shape=[out] * 2,
        in_specs=[SMEM] + specs,
        out_specs=[pl.BlockSpec((2, 1, rows, cols), lambda s: (0, s, 0, 0))] * 2,
        scratch_shapes=scratch,
        compiler_params=params(),
        cost_estimate=cost(covers),
        name="weight_grad",
    )(place, *args)


def pass_on_body(keep_ref, came_ref, out_ref):
    def rows(at, _):
        total = keep_ref[0, 0, at, :].astype(f32) + came_ref[0, 0, at, :].astype(f32)
        out_ref[0, at, :] = total.astype(bf16)
        return 0

    over_rows(out_ref.shape[1], 32, rows, 0)


def pass_on(keep, came):
    _, shards, rows, cols = keep.shape
    half = pl.BlockSpec((1, 1, rows, cols), lambda s: (1, s, 0, 0))
    return pl.pallas_call(
        pass_on_body,
        grid=(shards,),
        out_shape=jax.ShapeDtypeStruct((shards, rows, cols), bf16),
        in_specs=[half, half],
        out_specs=pl.BlockSpec((1, rows, cols), lambda s: (s, 0, 0)),
        compiler_params=params(),
        cost_estimate=cost(300),
        name="pass_on",
    )(keep, came)


def gather_up_body(keep_ref, came_ref, last_ref, own_ref, *out_refs):
    s = pl.program_id(0)

    def rows(at, _):
        part = keep_ref[0, 0, at, :].astype(f32) + came_ref[0, 0, at, :].astype(f32)
        part += last_ref[0, at, :].astype(f32)

        @pl.when(s == 0)
        def _():
            own_ref[at, :] = part

        low = part.astype(bf16)
        for i, ref in enumerate(out_refs):

            @pl.when(s == i + 1)
            def _():
                ref[at, :] = low

        return 0

    over_rows(own_ref.shape[0], 32, rows, 0)


def gather_up(covers, keep, came, last):
    _, shards, rows, cols = keep.shape
    half = pl.BlockSpec((1, 1, rows, cols), lambda s: (0, s, 0, 0))
    out = pl.BlockSpec((rows, cols), lambda s: (0, 0))
    return pl.pallas_call(
        gather_up_body,
        grid=(shards,),
        out_shape=[jax.ShapeDtypeStruct((rows, cols), f32)]
        + [jax.ShapeDtypeStruct((rows, cols), bf16)] * (shards - 1),
        in_specs=[half, half, pl.BlockSpec((1, rows, cols), lambda s: (s, 0, 0))],
        out_specs=[out] * shards,
        compiler_params=params(),
        cost_estimate=cost(covers),
        name="gather_up",
    )(keep, came, last)


def finish_body(pieces, scale_ref, *refs):
    n = len(refs) - len(pieces)
    total = refs[0][...]
    for ref in refs[1:n]:
        total += ref[...].astype(f32)
    total *= scale_ref[0]
    for ref, (kind, low, high) in zip(refs[n:], pieces):
        part = total[:, low:high]
        if kind == "turned":
            ref[...] = part.T
        elif kind == "plain":
            ref[...] = part
        else:
            cols = ref.shape[2]
            for c in range(ref.shape[0]):
                ref[c] = part[:, c * cols : (c + 1) * cols]


def finish_all(scale, parts, pieces):
    rows = parts[0].shape[0]
    shapes = []
    for kind, low, high in pieces:
        cols = high - low
        shapes.append({"turned": (cols, rows), "plain": (rows, cols), "three": (3, rows, cols // 3)}[kind])
    return pl.pallas_call(
        functools.partial(finish_body, pieces),
        out_shape=[jax.ShapeDtypeStruct(v, f32) for v in shapes],
        in_specs=[SMEM] + [pl.BlockSpec(memory_space=pltpu.VMEM)] * len(parts),
        compiler_params=params(),
        cost_estimate=cost(300),
        name="finish",
    )(scale, *parts)


def after(x, *deps):
    return lax.optimization_barrier((x, deps))[0]


def on_device(
    tokens,
    timesteps,
    buckets,
    counts,
    w_time,
    table,
    w_qkv,
    b_qv,
    w_out,
    b_out,
    gain1,
    shift1,
    w_up,
    b_up,
    w_down,
    b_down,
    gain2,
    shift2,
    cotangent,
):
    mpn = lax.axis_size("mp")
    dpn = lax.axis_size("dp")
    extra = dpn.bit_length() - 4
    me = lax.axis_index("dp")
    z = lax.axis_index("mp")
    q8 = me >> extra
    width = w_time.shape[0]
    positions, slots = tokens.shape[:2]
    length = positions * mpn
    head_cols = w_qkv.shape[2]
    units = w_up.shape[1]

    def exchange(x, partner):
        low = (1 << extra) - 1
        pairs = [(i, (partner(i >> extra) << extra) | (i & low)) for i in range(dpn)]
        return lax.ppermute(x, "dp", pairs)

    def cores(x):
        return exchange(x, lambda p: p ^ 1)

    def first_link(x):
        return exchange(x, lambda p: p ^ masks(p)[0])

    def second_link(x):
        return exchange(x, lambda p: p ^ masks(p)[1])

    def shift(x, s):
        return lax.ppermute(x, "mp", [(i, (i + s) % mpn) for i in range(mpn)])

    def to_items(x):
        x = lax.all_to_all(jnp.moveaxis(x, 1, 0), "mp", 0, 0, tiled=False)
        return x.reshape(length, width)

    def to_positions(x):
        return lax.all_to_all(x.reshape(mpn, positions, width), "mp", 0, 0, tiled=False)

    def split(shard, axis):
        dims = shard.shape
        return shard.reshape(dims[:axis] + (8, dims[axis] // 8) + dims[axis + 1 :])

    def eighth(shaped, axis):
        return lax.dynamic_index_in_dim(shaped, q8, axis, False)

    def along_z(part):
        return [shift(part, s) for s in range(1, mpn)]

    place = q8.astype(jnp.int32)[None]
    own_qkv, own_out, own_up, own_down = split(w_qkv, 1), split(w_out, 0), split(w_up, 0), split(w_down, 0)
    b_out, gain1, shift1, b_down, gain2, shift2 = [
        v[None] for v in (b_out, gain1, shift1, b_down, gain2, shift2)
    ]

    own_bias = jnp.stack([b_qv[0], jnp.zeros_like(b_qv[0]), b_qv[1]])[:, None]
    z_qkv = along_z(jnp.concatenate([eighth(own_qkv, 1), in_three(own_bias)], axis=1))
    part_up = jnp.concatenate([eighth(own_out, 0), eighth(own_up, 0), in_three(b_up[None])])
    part_down = eighth(own_down, 0)
    mine_qkv, far_bias = pack(300, after(z_qkv, part_up, part_down), own_qkv.shape[2])
    came_qkv = first_link(mine_qkv)
    z_up = along_z(after(part_up, mine_qkv))

    x = to_items(after(tokens, mine_qkv))
    held_qkv = pack(300, [mine_qkv, came_qkv])
    far_qkv = second_link(held_qkv)
    held2_qkv = cores(held_qkv)
    mine_up, far_up_bias = pack(300, after(z_up, held_qkv), own_out.shape[1] + own_up.shape[1])
    came_up = first_link(mine_up)

    timesteps, buckets, counts = after((timesteps, buckets, counts), mine_up)
    total_live = jnp.sum(counts).astype(f32)
    weighting = 1.0 / total_live
    live = (z < lax.dynamic_index_in_dim(counts, me, 0, True)).astype(f32)
    my_step = lax.dynamic_index_in_dim(timesteps, z, 0, True)
    my_bucket = lax.dynamic_index_in_dim(buckets, z, 0, False)
    time_embed = embed(
        300,
        sinusoid(my_step.astype(f32), width), w_time, lax.dynamic_index_in_dim(table, my_bucket, 0, True)
    )

    far2_qkv = cores(after(far_qkv, mine_up))
    g_qkv = Gathered(own_qkv, [held_qkv, far_qkv, held2_qkv, far2_qkv], 1, 0)
    held_up = pack(300, [mine_up, after(came_up, far2_qkv, held2_qkv, time_embed)])
    far_up = second_link(held_up)
    held2_up = cores(held_up)
    x = after(x, held_up)
    hidden = (x.astype(f32) + time_embed).astype(bf16)
    z_down = along_z(after(part_down, hidden))

    done = attend(300, 0, mpn, Gathered(own_qkv, [], 1, 0), place, hidden, own_bias[None], [])
    done = attend(300, 1, mpn, g_qkv, place, after(hidden, held2_up), far_bias, done)
    far2_up = cores(after(far_up, done))
    done = attend(300, 2, mpn, g_qkv, place, hidden, far_bias, done)
    mine_down = pack(300, after(z_down, done, far2_up))
    came_down = first_link(mine_down)
    qkv, probs, ctx = attend(300, 3, mpn, g_qkv, place, after(hidden, mine_down), far_bias, done)
    cot = to_items(after(cotangent, ctx))
    held_down = pack(300, [mine_down, after(came_down, ctx)])
    far_down = second_link(held_down)
    held2_down = cores(held_down)
    ctx2, hidden2 = cores(after(ctx, held_down)), cores(after(hidden, held_down))
    up_pieces = [held_up, far_up, held2_up, far2_up]
    g_out = Gathered(own_out, up_pieces, 0, 0)
    g_up = Gathered(own_up, up_pieces, 0, own_out.shape[1])
    n1, inv1, normed_low, active, slope, full_out = up_project(
        g_out,
        g_up,
        place,
        after(ctx, held_down),
        x,
        time_embed,
        b_out,
        gain1,
        shift1,
        jnp.concatenate([b_up[None, None], far_up_bias]),
    )
    full_out = full_out.reshape(mpn, head_cols, width)
    far2_down = cores(after(far_down, normed_low, held2_down, ctx2, hidden2))
    g_down = Gathered(own_down, [held_down, far_down, held2_down, far2_down], 0, 0)
    cot = after(cot, normed_low)
    active2 = cores(active)
    output, branch_grad, sums2 = down_project(
        g_down, place, live, active, n1, cot, b_down, gain1, shift1, gain2, shift2
    )
    def send_home(covers, keep, came, last):
        sums = gather_up(covers, keep, came, last)
        return [sums[0]] + [shift(v, -s - 1) for s, v in enumerate(sums[1:])], sums

    def finish(arrived, pieces):
        if extra == 0:
            return finish_all(weighting[None], arrived, pieces)
        total = sum(a.astype(f32) for a in arrived) * weighting
        for t in reversed(range(extra)):
            half = total.shape[0] // 2
            bit = (me >> t) & 1
            keep = lax.dynamic_slice_in_dim(total, bit * half, half, 0)
            sent = lax.dynamic_slice_in_dim(total, (1 - bit) * half, half, 0)
            total = keep + lax.ppermute(sent, "dp", [(i, i ^ (1 << t)) for i in range(dpn)])
        made = []
        for kind, low, high in pieces:
            part = total[:, low:high]
            if kind == "turned":
                part = part.T
            elif kind == "three":
                part = jnp.moveaxis(part.reshape(part.shape[0], 3, -1), 1, 0)
            made.append(part)
        return made

    devices = dpn * mpn
    both = ("dp", "mp")

    def in_order(parts):
        turned = jnp.stack([parts[-i % mpn] for i in range(mpn)] * 2)
        return lax.dynamic_slice_in_dim(turned, (mpn - z) % mpn, mpn, 0).reshape(-1)

    keep_d, send_d = weight_grad(300, place, [(branch_grad, cores(branch_grad), active, active2)])
    came_d = first_link(send_d)
    low2 = cores(after(normed_low, keep_d))
    up_grad, bias_up, grad_first, mixing_grad, sums1 = up_back(
        g_down, g_up, place, after(branch_grad, keep_d), slope, n1, inv1, gain1
    )
    up_grad2, mixing_grad2 = cores(up_grad), cores(mixing_grad)
    pass_d = pass_on(keep_d, after(came_d, mixing_grad, low2))
    last_d = second_link(pass_d)
    out_items = to_positions(after(output, mixing_grad))
    keep_u, send_u = weight_grad(
        300,
        place,
        after([(normed_low, low2, up_grad, up_grad2), (mixing_grad, mixing_grad2, ctx, ctx2)], pass_d),
    )
    came_u = first_link(send_u)
    pg, bias_near = attend_back(300, 0, mpn // 2, full_out, after(mixing_grad, keep_u), qkv, probs, None)
    home_d, sent_d = send_home(1, keep_d, came_d, after(last_d, pg))
    pg, bias_far = attend_back(
        1, mpn // 2, mpn - mpn // 2, full_out, after(mixing_grad, sent_d, out_items), qkv, probs, pg
    )
    pg2 = cores(pg)
    pass_u = pass_on(keep_u, after(came_u, pg))
    last_u = second_link(pass_u)
    grad_tokens, time_grad = input_back(g_qkv, place, after(pg, pass_u), grad_first)
    back_items = to_positions(grad_tokens)
    keep_q, send_q = weight_grad(300, place, [(hidden, hidden2, after(pg, grad_tokens), pg2)], looped=True)
    bias_proj = jnp.concatenate([bias_near, bias_far])
    vectors = [
        in_order(bias_proj[:, 0, :head_cols]),
        in_order(bias_proj[:, 0, 2 * head_cols :]),
        sums1[0],
        sums1[1],
        sums1[2],
        sums2[0],
        sums2[1],
        sums2[2],
        in_order(bias_up[:, 0]),
        after(time_grad, keep_q),
    ]
    facts = jnp.stack([my_step[0].astype(f32), my_bucket.astype(f32)])
    facts = jnp.broadcast_to(facts[None], (devices, 2))
    vectors = jnp.concatenate([facts] + [v.reshape(devices, -1) for v in vectors], axis=1)
    came_q = first_link(send_q)
    home_u, sent_u = send_home(300, keep_u, came_u, after(last_u, keep_q, home_d))
    pass_q = pass_on(keep_q, after(came_q, sent_u))
    last_q = second_link(pass_q)
    back_items = after(back_items, pass_q)
    gathered = lax.all_to_all(after(vectors, back_items), both, 0, 0, tiled=True)
    home_u = after(home_u, pass_q)
    (grad_w_down,) = finish(after(home_d, pass_q), [("turned", 0, units)])
    home_q, sent_q = send_home(300, keep_q, came_q, after(last_q, grad_w_down))
    grad_tokens = jnp.moveaxis(after(back_items, sent_q), 0, 1).astype(f32)
    output = jnp.moveaxis(after(out_items, sent_q), 0, 1)
    grad_w_up, grad_w_out = finish(
        after(home_u, sent_q), [("plain", 0, units), ("turned", units, units + head_cols)]
    )
    (grad_w_qkv,) = finish(home_q, [("three", 0, 3 * head_cols)])
    per = width // devices

    gathered = after(gathered, sent_q)
    grads = gathered[:, -per:]
    summed = jnp.sum(gathered[:, 2:-per], axis=0) * weighting
    steps, rows_of = gathered[:, 0], gathered[:, 1]
    small = [summed[i * per : (i + 1) * per] for i in range(8)]
    grad_b_up = summed[8 * per :]
    high = lax.Precision.HIGHEST
    grad_w_time = (
        jnp.einsum("nd,ne->de", sinusoid(steps, width).astype(f32), grads, precision=high)
        * weighting
    )
    onehot = (rows_of[:, None] == jnp.arange(table.shape[0], dtype=f32)[None, :]).astype(f32)
    grad_table = jnp.einsum("nb,nd->bd", onehot, grads, precision=high) * weighting
    return (
        output,
        grad_tokens,
        grad_w_time,
        grad_table,
        grad_w_qkv,
        jnp.stack(small[:2]),
        grad_w_out,
        small[2],
        small[3],
        small[4],
        grad_w_up,
        grad_b_up,
        grad_w_down,
        small[5],
        small[6],
        small[7],
    )


def solution(mesh):
    return jax.shard_map(
        on_device,
        mesh=mesh,
        in_specs=(
            P("mp", "dp", None),
            P("dp"),
            P("dp"),
            P(),
            P(),
            P(),
            P(None, None, "mp"),
            P(None, "mp"),
            P("mp", None),
            P(),
            P(),
            P(),
            P(None, "mp"),
            P("mp"),
            P("mp", None),
            P(),
            P(),
            P(),
            P("mp", "dp", None),
        ),
        out_specs=(
            P("mp", "dp", None),
            P("mp", "dp", None),
            P(None, ("dp", "mp")),
            P(None, ("dp", "mp")),
            P(None, "dp", "mp"),
            P(None, ("dp", "mp")),
            P("mp", "dp"),
            P(("dp", "mp")),
            P(("dp", "mp")),
            P(("dp", "mp")),
            P("dp", "mp"),
            P(("dp", "mp")),
            P("mp", "dp"),
            P(("dp", "mp")),
            P(("dp", "mp")),
            P(("dp", "mp")),
        ),
        check_vma=False,
    )
```

profile of v0, /device:TPU:0, one launch (start us, length us, event | category | flops | bytes accessed | tf_op | source)
XLA Modules:
  0.0 389.7 jit_solution(9976300583224384672)
XLA Ops:
  3.7 3.1 collective-permute-start
  6.8 2.6 collective-permute-start.1
  12.3 1.8 dynamic-slice_bitcast_fusion
  14.1 2.0 concatenate.63
  16.1 7.0 %collective-permute-done.1.refs_1_ = bf16[3,136,256]{2,1,0:T(8,128)(2,1)S(1)} collective-permute-done((bf16[3,136,256]{2,1,0:T(8,128)(2,1)S(1)}, bf16[3,136,256]{2,1,0:T(8,128)(2,1)S(1)}, u32[]{:S(2)}, u32[]{:S(2)}) %collective-permute-start.1) | collective-permute-done | bytes 208928 | tf_op jit(solution)/shard_map/ppermute | solution.py:897
  23.8 2.1 pack.6
  25.9 1.5 collective-permute-start.6
  28.2 4.9 %collective-permute-start.3 = (bf16[168,1024]{1,0:T(8,128)(2,1)}, bf16[168,1024]{1,0:T(8,128)(2,1)}, u32[]{:S(2)}, u32[]{:S(2)}) collective-permute-start(bf16[168,1024]{1,0:T(8,128)(2,1)} %concatenate.63), channel_id=1, source_target_pairs={{0,1},{1,2},{2,3},{3,0},{4,5},{5,6},{6,7},{7,4},{8,9},{9,10},{10,1... | collective-permute-start | bytes 1032200 | tf_op jit(solution)/shard_map/ppermute | solution.py:897
  33.0 1.7 collective-permute-start.4
  36.7 4.3 %all-to-all-start = ((bf16[4,128,1024]{2,1,0:T(8,128)(2,1)}), bf16[4,128,1024]{2,1,0:T(8,128)(2,1)}, u32[]{:S(2)}, u32[]{:S(2)}) async-start(bf16[4,128,1024]{2,1,0:T(8,128)(2,1)} %bitcast.76), calls=%async_computation | async-start | bytes 2097152 | tf_op jit(solution)/shard_map/all_to_all | solution.py:900
  41.8 2.3 pack.7.refs_1_
  44.1 1.6 collective-permute-start.8
  45.7 12.7 %collective-permute-done.4.refs_1_ = bf16[168,1024]{1,0:T(8,128)(2,1)} collective-permute-done((bf16[168,1024]{1,0:T(8,128)(2,1)}, bf16[168,1024]{1,0:T(8,128)(2,1)}, u32[]{:S(2)}, u32[]{:S(2)}) %collective-permute-start.4) | collective-permute-done | bytes 344096 | tf_op jit(solution)/shard_map/ppermute | solution.py:897
  58.4 2.2 pack.8
  66.7 2.6 embed.1.te_ref
  70.0 5.1 %collective-permute-done.7.refs_1_ = bf16[3,160,1024]{2,1,0:T(8,128)(2,1)} collective-permute-done((bf16[3,160,1024]{2,1,0:T(8,128)(2,1)}, bf16[3,160,1024]{2,1,0:T(8,128)(2,1)}, u32[]{:S(2)}, u32[]{:S(2)}) %collective-permute-start.7) | collective-permute-done | bytes 983072 | tf_op jit(solution)/shard_map/ppermute | solution.py:885
  75.1 2.8 pack.9.refs_1_.refs_6_
  78.0 2.1 collective-permute-start.15
  80.2 5.9 %all-to-all-done = bf16[4,128,1024]{2,1,0:T(8,128)(2,1)} async-done(((bf16[4,128,1024]{2,1,0:T(8,128)(2,1)}), bf16[4,128,1024]{2,1,0:T(8,128)(2,1)}, u32[]{:S(2)}, u32[]{:S(2)}) %all-to-all-start) | async-done | bytes 1048608 | tf_op jit(solution)/shard_map/all_to_all | solution.py:900
  86.1 2.4 add_convert_fusion.x_hbm.refs_0_
  88.5 10.4 %collective-permute-start.11 = (bf16[128,1024]{1,0:T(8,128)(2,1)}, bf16[128,1024]{1,0:T(8,128)(2,1)}, u32[]{:S(2)}, u32[]{:S(2)}) collective-permute-start(bf16[128,1024]{1,0:T(8,128)(2,1)} %get-tuple-element.154), channel_id=1, source_target_pairs={{0,1},{1,2},{2,3},{3,0},{4,5},{5,6},{6,7},{7,4},{8,9},{9,10},{10,1... | collective-permute-start | bytes 786440 | tf_op jit(solution)/shard_map/ppermute | solution.py:897
  98.9 3.4 collective-permute-start.12
  102.3 7.0 %attend.4 = (bf16[4,512,768]{2,1,0:T(8,128)(2,1)}, bf16[4,4,512,512]{3,2,1,0:T(8,128)(2,1)}, bf16[4,512,256]{2,1,0:T(8,128)(2,1)}) custom-call(s32[1]{0:T(128)} %bitcast.place_ref, bf16[512,1024]{1,0:T(8,128)(2,1)} %add_convert_fusion.x_hbm.refs_0_, f32[1,3,1,256]{3,2,1,0:T(1,128)} %broadcast_in_dim_broadcast_in_dim.3.bias_ref, bf16[3,8,128,256]{3,2,1,0:T(8,128)(2,1)} %bitcast.81), custom_call_target="tpu_custom_call" | custom-call | flops 344999985152 | tf_op jit(solution)/shard_map/attend/pallas_call | solution.py:218
  109.3 7.1 %attend.5 = (bf16[4,512,768]{2,1,0:T(8,128)(2,1)}, bf16[4,4,512,512]{3,2,1,0:T(8,128)(2,1)}, bf16[4,512,256]{2,1,0:T(8,128)(2,1)}) custom-call(s32[1]{0:T(128)} %bitcast.place_ref, bf16[512,1024]{1,0:T(8,128)(2,1)} %add_convert_fusion.x_hbm.refs_0_, ...), custom_call_target="tpu_custom_call", output_to_operand_aliasing={{0}: (8, {}), {1}: (9, {}), {2}: (10, {})} | custom-call | flops 344999985152 | tf_op jit(solution)/shard_map/attend/pallas_call | solution.py:218
  116.5 7.1 %attend.6 = (bf16[4,512,768]{2,1,0:T(8,128)(2,1)}, bf16[4,4,512,512]{3,2,1,0:T(8,128)(2,1)}, bf16[4,512,256]{2,1,0:T(8,128)(2,1)}) custom-call(s32[1]{0:T(128)} %bitcast.place_ref, bf16[512,1024]{1,0:T(8,128)(2,1)} %add_convert_fusion.x_hbm.refs_0_, ...), custom_call_target="tpu_custom_call", output_to_operand_aliasing={{0}: (8, {}), {1}: (9, {}), {2}: (10, {})} | custom-call | flops 344999985152 | tf_op jit(solution)/shard_map/attend/pallas_call | solution.py:218
  123.6 2.0 pack.10.refs_0_
  126.2 7.1 %attend.7 = (bf16[4,512,768]{2,1,0:T(8,128)(2,1)}, bf16[4,4,512,512]{3,2,1,0:T(8,128)(2,1)}, bf16[4,512,256]{2,1,0:T(8,128)(2,1)}) custom-call(s32[1]{0:T(128)} %bitcast.place_ref, bf16[512,1024]{1,0:T(8,128)(2,1)} %add_convert_fusion.x_hbm.refs_0_, ...), custom_call_target="tpu_custom_call", output_to_operand_aliasing={{0}: (8, {}), {1}: (9, {}), {2}: (10, {})} | custom-call | flops 344999985152 | tf_op jit(solution)/shard_map/attend/pallas_call | solution.py:218
  134.6 7.6 %all-to-all-start.1 = ((bf16[4,128,1024]{2,1,0:T(8,128)(2,1)}), bf16[4,128,1024]{2,1,0:T(8,128)(2,1)}, u32[]{:S(2)}, u32[]{:S(2)}) async-start(bf16[4,128,1024]{2,1,0:T(8,128)(2,1)} %bitcast.75), calls=%async_computation.1 | async-start | bytes 2097152 | tf_op jit(solution)/shard_map/all_to_all | solution.py:900
  142.3 2.6 pack.11.refs_1_
  144.9 1.6 collective-permute-start.18
  147.0 20.9 %up_project.1 = (f32[512,1024]{1,0:T(8,128)}, f32[512,128]{1,0:T(8,128)}, bf16[512,1024]{1,0:T(8,128)(2,1)}, bf16[4,512,1024]{2,1,0:T(8,128)(2,1)}, bf16[4,512,1...) custom-call(s32[1]{0:T(128)} %bitcast.place_ref, bf16[4,512,256]{2,1,0:T(8,128)(2,1)} %get-tuple-element.200.ctx_ref.refs_6_, ...), custom_call_target="tpu_custom_call" | custom-call | flops 344999985152 | tf_op jit(solution)/shard_map/up_project/pallas_call | solution.py:317
  169.8 1.9 collective-permute-done.22.refs_4_
  172.9 13.6 %down_project.1 = (bf16[512,1024]{1,0:T(8,128)(2,1)}, bf16[512,1024]{1,0:T(8,128)(2,1)}, f32[3,1024]{1,0:T(4,128)}) custom-call(s32[1]{0:T(128)} %bitcast.place_ref, f32[1]{0:T(128)S(6)} %convert_element_type.37.live_ref, bf16[4,512,1024]{2,1,0:T(8,128)(2,1)} %get-tuple-element.175.act_ref.refs_2_, f32[1,1024]{1,0:T(1,128)} %bitcast.105, ...), custom_call_target="tpu_custom_call" | custom-call | flops 344999985152 | tf_op jit(solution)/shard_map/down_project/pallas_call | solution.py:428
  193.9 9.4 %weight_grad.3 = (bf16[2,4,128,1024]{3,2,1,0:T(8,128)(2,1)}, bf16[2,4,128,1024]{3,2,1,0:T(8,128)(2,1)}) custom-call(s32[1]{0:T(128)} %bitcast.place_ref, bf16[512,1024]{1,0:T(8,128)(2,1)} %get-tuple-element.185.refs_0_.bg_ref, bf16[512,1024]{1,0:T(8,128)(2,1)} %copy-done.30, bf16[4,512,1024]{2,1,0:T(8,128)(2,1)} %get-tuple-element.175.act_ref.refs_2_, ...), custom_call_target="tpu_custom_call" | custom-call | flops 344999985152 | tf_op jit(solution)/shard_map/weight_grad/pallas_call | solution.py:734
  203.4 1.6 collective-permute-start.25
  205.0 21.8 %up_back.1 = (bf16[4,512,1024]{2,1,0:T(8,128)(2,1)}, f32[4,1,1024]{2,1,0:T(1,128)}, f32[512,1024]{1,0:T(8,128)}, bf16[512,1024]{1,0:T(8,128)(2,1)}, f32[3,1024]{1,0:T(4,128)}) custom-call(s32[1]{0:T(128)} %bitcast.place_ref, bf16[512,1024]{1,0:T(8,128)(2,1)} %get-tuple-element.185.refs_0_.bg_ref, bf16[4,512,1024]{2,1,0:T(8,128)(2,1)} %get-tuple-element.186.slope_ref, ...), custom_call_target="tpu_custom_call" | custom-call | flops 344999985152 | tf_op jit(solution)/shard_map/up_back/pallas_call | solution.py:525
  227.5 5.1 %all-to-all-start.2 = ((bf16[4,128,1024]{2,1,0:T(8,128)(2,1)}), bf16[4,128,1024]{2,1,0:T(8,128)(2,1)}, u32[]{:S(2)}, u32[]{:S(2)}) async-start(bf16[4,128,1024]{2,1,0:T(8,128)(2,1)} %bitcast.26), calls=%async_computation.2 | async-start | bytes 2097152 | tf_op jit(solution)/shard_map/all_to_all | solution.py:904
  235.3 3.7 pass_on.3
  239.4 11.9 %weight_grad.4 = (bf16[2,4,128,1280]{3,2,1,0:T(8,128)(2,1)}, bf16[2,4,128,1280]{3,2,1,0:T(8,128)(2,1)}) custom-call(s32[1]{0:T(128)} %bitcast.place_ref, bf16[512,1024]{1,0:T(8,128)(2,1)} %get-tuple-element.194.refs_0_, bf16[512,1024]{1,0:T(8,128)(2,1)} %collective-permute-done.26.refs_1_, bf16[4,512,1024]{2,1,0:T(8,128)(2,1)} %get-tuple-element.196.refs_2_, ...), custom_call_target="tpu_custom_call" | custom-call | flops 344999985152 | tf_op jit(solution)/shard_map/weight_grad/pallas_call | solution.py:734
  252.6 11.5 %attend_back.2 = (bf16[4,512,768]{2,1,0:T(8,128)(2,1)}, f32[2,1,768]{2,1,0:T(1,128)}) custom-call(bf16[512,1024]{1,0:T(8,128)(2,1)} %get-tuple-element.213.refs_4_.mg_ref, bf16[4,256,1024]{2,1,0:T(8,128)(2,1)} %bitcast.78, bf16[4,512,768]{2,1,0:T(8,128)(2,1)} %get-tuple-element.205.qkv, bf16[4,4,512,512]{3,2,1,0:T(8,128)(2,1)} %get-tuple-element.206.p_of), custom_call_target="tpu_custom_call" | custom-call | flops 344999985152 | tf_op jit(solution)/shard_map/attend_back/pallas_call | solution.py:598
  264.1 4.0 %gather_up.3 = (f32[128,1024]{1,0:T(8,128)}, bf16[128,1024]{1,0:T(8,128)(2,1)}, bf16[128,1024]{1,0:T(8,128)(2,1)}, bf16[128,1024]{1,0:T(8,128)(2,1)}) custom-call(bf16[2,4,128,1024]{3,2,1,0:T(8,128)(2,1)} %get-tuple-element.184.keep_ref, bf16[2,4,128,1024]{3,2,1,0:T(8,128)(2,1)} %collective-permute-done.25.came_ref, ...), custom_call_target="tpu_custom_call" | custom-call | flops 1150000000 | tf_op jit(solution)/shard_map/gather_up/pallas_call | solution.py:798
  268.1 3.8 collective-permute-start.34
  273.1 11.6 %attend_back.3 = (bf16[4,512,768]{2,1,0:T(8,128)(2,1)}, f32[2,1,768]{2,1,0:T(1,128)}) custom-call(bf16[512,1024]{1,0:T(8,128)(2,1)} %get-tuple-element.213.refs_4_.mg_ref, bf16[4,256,1024]{2,1,0:T(8,128)(2,1)} %bitcast.79, bf16[4,512,768]{2,1,0:T(8,128)(2,1)} %get-tuple-element.205.qkv, ...), custom_call_target="tpu_custom_call", output_to_operand_aliasing={{0}: (4, {})} | custom-call | flops 1150000000 | tf_op jit(solution)/shard_map/attend_back/pallas_call | solution.py:598
  286.9 3.8 pass_on.4
  291.5 8.7 %input_back.1 = (bf16[512,1024]{1,0:T(8,128)(2,1)}, f32[1,1024]{1,0:T(1,128)}) custom-call(s32[1]{0:T(128)} %bitcast.place_ref, bf16[4,512,768]{2,1,0:T(8,128)(2,1)} %get-tuple-element.220.pg_ref.refs_2_, f32[512,1024]{1,0:T(8,128)} %get-tuple-element.218.gf_hbm, bf16[3,8,128,256]{3,2,1,0:T(8,128)(2,1)} %bitcast.85, ...), custom_call_target="tpu_custom_call" | custom-call | flops 1150000000 | tf_op jit(solution)/shard_map/input_back/pallas_call | solution.py:661
  300.2 4.2 %all-to-all-start.3 = ((bf16[4,128,1024]{2,1,0:T(8,128)(2,1)}), bf16[4,128,1024]{2,1,0:T(8,128)(2,1)}, u32[]{:S(2)}, u32[]{:S(2)}) async-start(bf16[4,128,1024]{2,1,0:T(8,128)(2,1)} %bitcast.86), calls=%async_computation.3 | async-start | bytes 2097152 | tf_op jit(solution)/shard_map/all_to_all | solution.py:904
  304.6 9.0 %weight_grad.5 = (bf16[2,4,128,768]{3,2,1,0:T(8,128)(2,1)}, bf16[2,4,128,768]{3,2,1,0:T(8,128)(2,1)}) custom-call(s32[1]{0:T(128)} %bitcast.place_ref, bf16[512,1024]{1,0:T(8,128)(2,1)} %add_convert_fusion.x_hbm.refs_0_, bf16[512,1024]{1,0:T(8,128)(2,1)} %collective-permute-done.21.refs_1_, bf16[4,512,768]{2,1,0:T(8,128)(2,1)} %get-tuple-element.220.pg_ref.refs_2_, ...), custom_call_target="tpu_custom_call" | custom-call | flops 344999985152 | tf_op jit(solution)/shard_map/weight_grad/pallas_call | solution.py:734
  313.6 1.6 collective-permute-start.32
  317.3 4.4 %gather_up.4 = (f32[128,1280]{1,0:T(8,128)}, bf16[128,1280]{1,0:T(8,128)(2,1)}, bf16[128,1280]{1,0:T(8,128)(2,1)}, bf16[128,1280]{1,0:T(8,128)(2,1)}) custom-call(bf16[2,4,128,1280]{3,2,1,0:T(8,128)(2,1)} %get-tuple-element.202.keep_ref, bf16[2,4,128,1280]{3,2,1,0:T(8,128)(2,1)} %collective-permute-done.30.came_ref, ...), custom_call_target="tpu_custom_call" | custom-call | flops 344999985152 | tf_op jit(solution)/shard_map/gather_up/pallas_call | solution.py:798
  321.7 3.8 collective-permute-start.41
  326.6 7.8 %collective-permute-done.32.came_ref = bf16[2,4,128,768]{3,2,1,0:T(8,128)(2,1)} collective-permute-done((bf16[2,4,128,768]{3,2,1,0:T(8,128)(2,1)}, bf16[2,4,128,768]{3,2,1,0:T(8,128)(2,1)}, u32[]{:S(2)}, u32[]{:S(2)}) %collective-permute-start.32) | collective-permute-done | bytes 1572896 | tf_op jit(solution)/shard_map/ppermute | solution.py:885
  334.4 3.6 pass_on.5
  339.9 9.8 %all-to-all-start.4 = ((f32[32,1,418]{2,1,0:T(1,128)}), f32[32,1,418]{2,1,0:T(1,128)}, u32[]{:S(2)}, u32[]{:S(2)}) async-start(f32[32,1,418]{2,1,0:T(1,128)} %copy.66), calls=%async_computation.4 | async-start | bytes 131072 | tf_op jit(solution)/shard_map/all_to_all | solution.py:1071
  349.7 2.3 finish.3
  352.0 8.1 %collective-permute-done.42.refs_2_ = bf16[128,1280]{1,0:T(8,128)(2,1)} collective-permute-done((bf16[128,1280]{1,0:T(8,128)(2,1)}, bf16[128,1280]{1,0:T(8,128)(2,1)}, u32[]{:S(2)}, u32[]{:S(2)}) %collective-permute-start.42) | collective-permute-done | bytes 327712 | tf_op jit(solution)/shard_map/ppermute | solution.py:897
  361.2 1.5 copy.75
  362.7 3.8 gather_up.5
  367.7 2.2 collective-permute-start.38
  373.1 2.7 copy.68
  375.8 3.0 copy.67
  380.6 2.4 finish.5
  383.1 1.6 convolution_multiply_fusion.1
  384.7 2.9 collective-permute-done.39.refs_2_
  387.6 2.1 finish.4
  (212 shorter events, 47.0 us)
Async XLA Ops:
  0.6 64.4 %copy-start = (f32[32,1024]{1,0:T(8,128)S(1)}, f32[32,1024]{1,0:T(8,128)}, u32[]{:S(2)}) copy-start(f32[32,1024]{1,0:T(8,128)} %param.24) | copy-start | bytes 393220
  3.7 12.4 %collective-permute-start = (bf16[3,136,256]{2,1,0:T(8,128)(2,1)S(1)}, bf16[3,136,256]{2,1,0:T(8,128)(2,1)S(1)}, u32[]{:S(2)}, u32[]{:S(2)}) collective-permute-start(bf16[3,136,256]{2,1,0:T(8,128)(2,1)S(1)} %concatenate.65), channel_id=1, source_target_pairs={{0,1},{1,2},{2,3},{3,0},{4,5},{5,6},{6,7},{7,4},{8,9},{9,10},{10,1... | collective-permute-start | bytes 626696 | tf_op jit(solution)/shard_map/ppermute | solution.py:897
  6.8 16.3 %collective-permute-start.1 = (bf16[3,136,256]{2,1,0:T(8,128)(2,1)S(1)}, bf16[3,136,256]{2,1,0:T(8,128)(2,1)S(1)}, u32[]{:S(2)}, u32[]{:S(2)}) collective-permute-start(bf16[3,136,256]{2,1,0:T(8,128)(2,1)S(1)} %concatenate.65), channel_id=1, source_target_pairs={{0,2},{1,3},{2,0},{3,1},{4,6},{5,7},{6,4},{7,5},{8,10},{9,11},{10,... | collective-permute-start | bytes 626696 | tf_op jit(solution)/shard_map/ppermute | solution.py:897
  9.4 13.7 %collective-permute-start.2 = (bf16[3,136,256]{2,1,0:T(8,128)(2,1)S(1)}, bf16[3,136,256]{2,1,0:T(8,128)(2,1)S(1)}, u32[]{:S(2)}, u32[]{:S(2)}) collective-permute-start(bf16[3,136,256]{2,1,0:T(8,128)(2,1)S(1)} %concatenate.65), channel_id=1, source_target_pairs={{0,3},{1,0},{2,1},{3,2},{4,7},{5,4},{6,5},{7,6},{8,11},{9,8},{10,9... | collective-permute-start | bytes 626696 | tf_op jit(solution)/shard_map/ppermute | solution.py:897
  23.8 11.6 %copy-start.2 = (bf16[128,4,1024]{2,1,0:T(4,128)(2,1)S(1)}, bf16[128,4,1024]{2,1,0:T(4,128)(2,1)}, u32[]{:S(2)}) copy-start(bf16[128,4,1024]{2,1,0:T(4,128)(2,1)} %param.19) | copy-start | bytes 3145732
  25.9 15.0 %collective-permute-start.6 = (bf16[3,3,128,256]{3,2,1,0:T(8,128)(2,1)}, bf16[3,3,128,256]{3,2,1,0:T(8,128)(2,1)S(1)}, u32[]{:S(2)}, u32[]{:S(2)}) collective-permute-start(bf16[3,3,128,256]{3,2,1,0:T(8,128)(2,1)} %get-tuple-element.141.refs_0_), channel_id=1, source_target_pairs={{0,8},{4,20},{8,0},{12,28},{16,24},{20,4},{24,16},{28,12},{1,9},{5... | collective-permute-start | bytes 1769480 | tf_op jit(solution)/shard_map/ppermute | solution.py:885
  28.2 17.5 %collective-permute-start.3 = (bf16[168,1024]{1,0:T(8,128)(2,1)}, bf16[168,1024]{1,0:T(8,128)(2,1)}, u32[]{:S(2)}, u32[]{:S(2)}) collective-permute-start(bf16[168,1024]{1,0:T(8,128)(2,1)} %concatenate.63), channel_id=1, source_target_pairs={{0,1},{1,2},{2,3},{3,0},{4,5},{5,6},{6,7},{7,4},{8,9},{9,10},{10,1... | collective-permute-start | bytes 1032200 | tf_op jit(solution)/shard_map/ppermute | solution.py:897
  33.0 25.3 %collective-permute-start.4 = (bf16[168,1024]{1,0:T(8,128)(2,1)}, bf16[168,1024]{1,0:T(8,128)(2,1)}, u32[]{:S(2)}, u32[]{:S(2)}) collective-permute-start(bf16[168,1024]{1,0:T(8,128)(2,1)} %concatenate.63), channel_id=1, source_target_pairs={{0,2},{1,3},{2,0},{3,1},{4,6},{5,7},{6,4},{7,5},{8,10},{9,11},{10,... | collective-permute-start | bytes 1032200 | tf_op jit(solution)/shard_map/ppermute | solution.py:897
  34.7 23.7 %collective-permute-start.5 = (bf16[168,1024]{1,0:T(8,128)(2,1)}, bf16[168,1024]{1,0:T(8,128)(2,1)}, u32[]{:S(2)}, u32[]{:S(2)}) collective-permute-start(bf16[168,1024]{1,0:T(8,128)(2,1)} %concatenate.63), channel_id=1, source_target_pairs={{0,3},{1,0},{2,1},{3,2},{4,7},{5,4},{6,5},{7,6},{8,11},{9,8},{10,9... | collective-permute-start | bytes 1032200 | tf_op jit(solution)/shard_map/ppermute | solution.py:897
  36.7 49.4 %all-to-all-start = ((bf16[4,128,1024]{2,1,0:T(8,128)(2,1)}), bf16[4,128,1024]{2,1,0:T(8,128)(2,1)}, u32[]{:S(2)}, u32[]{:S(2)}) async-start(bf16[4,128,1024]{2,1,0:T(8,128)(2,1)} %bitcast.76), calls=%async_computation | async-start | bytes 2097152 | tf_op jit(solution)/shard_map/all_to_all | solution.py:900
  44.1 21.6 %collective-permute-start.8 = (bf16[2,3,3,128,256]{4,3,2,1,0:T(8,128)(2,1)}, bf16[2,3,3,128,256]{4,3,2,1,0:T(8,128)(2,1)}, u32[]{:S(2)}, u32[]{:S(2)}) collective-permute-start(bf16[2,3,3,128,256]{4,3,2,1,0:T(8,128)(2,1)} %pack.7.refs_1_), channel_id=1, source_target_pairs={{0,16},{4,12},{8,24},{12,4},{16,0},{20,28},{24,8},{28,20},{1,17},{... | collective-permute-start | bytes 3538952 | tf_op jit(solution)/shard_map/ppermute | solution.py:885
  45.7 29.4 %collective-permute-start.10 = (bf16[2,3,3,128,256]{4,3,2,1,0:T(8,128)(2,1)}, bf16[2,3,3,128,256]{4,3,2,1,0:T(8,128)(2,1)}, u32[]{:S(2)}, u32[]{:S(2)}) collective-permute-start(bf16[2,3,3,128,256]{4,3,2,1,0:T(8,128)(2,1)} %pack.7.refs_1_), channel_id=1, source_target_pairs={{0,4},{4,0},{8,12},{12,8},{16,20},{20,16},{24,28},{28,24},{1,5},{5... | collective-permute-start | bytes 3538952 | tf_op jit(solution)/shard_map/ppermute | solution.py:885
  60.6 14.5 %collective-permute-start.7 = (bf16[3,160,1024]{2,1,0:T(8,128)(2,1)}, bf16[3,160,1024]{2,1,0:T(8,128)(2,1)}, u32[]{:S(2)}, u32[]{:S(2)}) collective-permute-start(bf16[3,160,1024]{2,1,0:T(8,128)(2,1)} %get-tuple-element.146.refs_0_), channel_id=1, source_target_pairs={{0,8},{4,20},{8,0},{12,28},{16,24},{20,4},{24,16},{28,12},{1,9},{5... | collective-permute-start | bytes 2949128 | tf_op jit(solution)/shard_map/ppermute | solution.py:885
  65.7 9.4 %collective-permute-start.9 = (bf16[2,3,3,128,256]{4,3,2,1,0:T(8,128)(2,1)}, bf16[2,3,3,128,256]{4,3,2,1,0:T(8,128)(2,1)}, u32[]{:S(2)}, u32[]{:S(2)}) collective-permute-start(bf16[2,3,3,128,256]{4,3,2,1,0:T(8,128)(2,1)} %collective-permute-done.8.refs_2_), channel_id=1, source_target_pairs={{0,4},{4,0},{8,12},{12,8},{16,20},{20,16},{24,28},{28,24},{1,5},{5... | collective-permute-start | bytes 3538952 | tf_op jit(solution)/shard_map/ppermute | solution.py:885
  77.9 31.3 %collective-permute-start.14 = (bf16[2,3,160,1024]{3,2,1,0:T(8,128)(2,1)}, bf16[2,3,160,1024]{3,2,1,0:T(8,128)(2,1)}, u32[]{:S(2)}, u32[]{:S(2)}) collective-permute-start(bf16[2,3,160,1024]{3,2,1,0:T(8,128)(2,1)} %pack.9.refs_1_.refs_6_), channel_id=1, source_target_pairs={{0,4},{4,0},{8,12},{12,8},{16,20},{20,16},{24,28},{28,24},{1,5},{5... | collective-permute-start | bytes 5898248 | tf_op jit(solution)/shard_map/ppermute | solution.py:885
  78.0 38.4 %collective-permute-start.15 = (bf16[2,3,160,1024]{3,2,1,0:T(8,128)(2,1)}, bf16[2,3,160,1024]{3,2,1,0:T(8,128)(2,1)}, u32[]{:S(2)}, u32[]{:S(2)}) collective-permute-start(bf16[2,3,160,1024]{3,2,1,0:T(8,128)(2,1)} %pack.9.refs_1_.refs_6_), channel_id=1, source_target_pairs={{0,16},{4,12},{8,24},{12,4},{16,0},{20,28},{24,8},{28,20},{1,17},{... | collective-permute-start | bytes 5898248 | tf_op jit(solution)/shard_map/ppermute | solution.py:885
  88.5 35.1 %collective-permute-start.11 = (bf16[128,1024]{1,0:T(8,128)(2,1)}, bf16[128,1024]{1,0:T(8,128)(2,1)}, u32[]{:S(2)}, u32[]{:S(2)}) collective-permute-start(bf16[128,1024]{1,0:T(8,128)(2,1)} %get-tuple-element.154), channel_id=1, source_target_pairs={{0,1},{1,2},{2,3},{3,0},{4,5},{5,6},{6,7},{7,4},{8,9},{9,10},{10,1... | collective-permute-start | bytes 786440 | tf_op jit(solution)/shard_map/ppermute | solution.py:897
  98.9 24.7 %collective-permute-start.12 = (bf16[128,1024]{1,0:T(8,128)(2,1)}, bf16[128,1024]{1,0:T(8,128)(2,1)}, u32[]{:S(2)}, u32[]{:S(2)}) collective-permute-start(bf16[128,1024]{1,0:T(8,128)(2,1)} %get-tuple-element.154), channel_id=1, source_target_pairs={{0,2},{1,3},{2,0},{3,1},{4,6},{5,7},{6,4},{7,5},{8,10},{9,11},{10,... | collective-permute-start | bytes 786440 | tf_op jit(solution)/shard_map/ppermute | solution.py:897
  102.3 21.3 %collective-permute-start.13 = (bf16[128,1024]{1,0:T(8,128)(2,1)}, bf16[128,1024]{1,0:T(8,128)(2,1)}, u32[]{:S(2)}, u32[]{:S(2)}) collective-permute-start(bf16[128,1024]{1,0:T(8,128)(2,1)} %get-tuple-element.154), channel_id=1, source_target_pairs={{0,3},{1,0},{2,1},{3,2},{4,7},{5,4},{6,5},{7,6},{8,11},{9,8},{10,9... | collective-permute-start | bytes 786440 | tf_op jit(solution)/shard_map/ppermute | solution.py:897
  116.4 7.2 %collective-permute-start.16 = (bf16[2,3,160,1024]{3,2,1,0:T(8,128)(2,1)}, bf16[2,3,160,1024]{3,2,1,0:T(8,128)(2,1)}, u32[]{:S(2)}, u32[]{:S(2)}) collective-permute-start(bf16[2,3,160,1024]{3,2,1,0:T(8,128)(2,1)} %collective-permute-done.15.refs_2_.refs_7_), channel_id=1, source_target_pairs={{0,4},{4,0},{8,12},{12,8},{16,20},{20,16},{24,28},{28,24},{1,5},{5... | collective-permute-start | bytes 5898248 | tf_op jit(solution)/shard_map/ppermute | solution.py:885
  125.7 16.6 %collective-permute-start.17 = (bf16[3,128,1024]{2,1,0:T(8,128)(2,1)}, bf16[3,128,1024]{2,1,0:T(8,128)(2,1)}, u32[]{:S(2)}, u32[]{:S(2)}) collective-permute-start(bf16[3,128,1024]{2,1,0:T(8,128)(2,1)} %pack.10.refs_0_), channel_id=1, source_target_pairs={{0,8},{4,20},{8,0},{12,28},{16,24},{20,4},{24,16},{28,12},{1,9},{5... | collective-permute-start | bytes 2359304 | tf_op jit(solution)/shard_map/ppermute | solution.py:885
  134.6 35.2 %all-to-all-start.1 = ((bf16[4,128,1024]{2,1,0:T(8,128)(2,1)}), bf16[4,128,1024]{2,1,0:T(8,128)(2,1)}, u32[]{:S(2)}, u32[]{:S(2)}) async-start(bf16[4,128,1024]{2,1,0:T(8,128)(2,1)} %bitcast.75), calls=%async_computation.1 | async-start | bytes 2097152 | tf_op jit(solution)/shard_map/all_to_all | solution.py:900
  144.9 23.0 %collective-permute-start.18 = (bf16[2,3,128,1024]{3,2,1,0:T(8,128)(2,1)}, bf16[2,3,128,1024]{3,2,1,0:T(8,128)(2,1)}, u32[]{:S(2)}, u32[]{:S(2)}) collective-permute-start(bf16[2,3,128,1024]{3,2,1,0:T(8,128)(2,1)} %pack.11.refs_1_), channel_id=1, source_target_pairs={{0,16},{4,12},{8,24},{12,4},{16,0},{20,28},{24,8},{28,20},{1,17},{... | collective-permute-start | bytes 4718600 | tf_op jit(solution)/shard_map/ppermute | solution.py:885
  146.4 21.5 %collective-permute-start.19 = (bf16[2,3,128,1024]{3,2,1,0:T(8,128)(2,1)}, bf16[2,3,128,1024]{3,2,1,0:T(8,128)(2,1)}, u32[]{:S(2)}, u32[]{:S(2)}) collective-permute-start(bf16[2,3,128,1024]{3,2,1,0:T(8,128)(2,1)} %pack.11.refs_1_), channel_id=1, source_target_pairs={{0,4},{4,0},{8,12},{12,8},{16,20},{20,16},{24,28},{28,24},{1,5},{5... | collective-permute-start | bytes 4718600 | tf_op jit(solution)/shard_map/ppermute | solution.py:885
  146.4 21.4 %collective-permute-start.21 = (bf16[512,1024]{1,0:T(8,128)(2,1)}, bf16[512,1024]{1,0:T(8,128)(2,1)}, u32[]{:S(2)}, u32[]{:S(2)}) collective-permute-start(bf16[512,1024]{1,0:T(8,128)(2,1)} %add_convert_fusion.x_hbm.refs_0_), channel_id=1, source_target_pairs={{0,4},{4,0},{8,12},{12,8},{16,20},{20,16},{24,28},{28,24},{1,5},{5... | collective-permute-start | bytes 3145736 | tf_op jit(solution)/shard_map/ppermute | solution.py:885
  147.0 20.9 %collective-permute-start.20 = (bf16[4,512,256]{2,1,0:T(8,128)(2,1)}, bf16[4,512,256]{2,1,0:T(8,128)(2,1)}, u32[]{:S(2)}, u32[]{:S(2)}) collective-permute-start(bf16[4,512,256]{2,1,0:T(8,128)(2,1)} %get-tuple-element.200.ctx_ref.refs_6_), channel_id=1, source_target_pairs={{0,4},{4,0},{8,12},{12,8},{16,20},{20,16},{24,28},{28,24},{1,5},{5... | collective-permute-start | bytes 3145736 | tf_op jit(solution)/shard_map/ppermute | solution.py:885
  147.0 21.5 %copy-start.37 = (s32[8]{0:T(128)S(1)}, s32[8]{0:T(128)}, u32[]{:S(2)}) copy-start(s32[8]{0:T(128)} %param.22) | copy-start | bytes 100
  167.9 3.8 collective-permute-start.22
  169.7 23.2 %collective-permute-start.24 = (bf16[4,512,1024]{2,1,0:T(8,128)(2,1)}, bf16[4,512,1024]{2,1,0:T(8,128)(2,1)}, u32[]{:S(2)}, u32[]{:S(2)}) collective-permute-start(bf16[4,512,1024]{2,1,0:T(8,128)(2,1)} %get-tuple-element.175.act_ref.refs_2_), channel_id=1, source_target_pairs={{0,4},{4,0},{8,12},{12,8},{16,20},{20,16},{24,28},{28,24},{1,5},{5... | collective-permute-start | bytes 12582920 | tf_op jit(solution)/shard_map/ppermute | solution.py:885
  172.9 14.6 %copy-start.38 = (s32[8]{0:T(128)S(1)}, s32[8]{0:T(128)}, u32[]{:S(2)}) copy-start(s32[8]{0:T(128)} %param.22) | copy-start | bytes 100
  186.5 6.5 %collective-permute-start.23 = (bf16[512,1024]{1,0:T(8,128)(2,1)}, bf16[512,1024]{1,0:T(8,128)(2,1)S(1)}, u32[]{:S(2)}, u32[]{:S(2)}) collective-permute-start(bf16[512,1024]{1,0:T(8,128)(2,1)} %get-tuple-element.185.refs_0_.bg_ref), channel_id=1, source_target_pairs={{0,4},{4,0},{8,12},{12,8},{16,20},{20,16},{24,28},{28,24},{1,5},{5... | collective-permute-start | bytes 3145736 | tf_op jit(solution)/shard_map/ppermute | solution.py:885
  203.3 32.0 %collective-permute-start.26 = (bf16[512,1024]{1,0:T(8,128)(2,1)}, bf16[512,1024]{1,0:T(8,128)(2,1)}, u32[]{:S(2)}, u32[]{:S(2)}) collective-permute-start(bf16[512,1024]{1,0:T(8,128)(2,1)} %get-tuple-element.194.refs_0_), channel_id=1, source_target_pairs={{0,4},{4,0},{8,12},{12,8},{16,20},{20,16},{24,28},{28,24},{1,5},{5... | collective-permute-start | bytes 3145736 | tf_op jit(solution)/shard_map/ppermute | solution.py:885
  203.4 31.9 %collective-permute-start.25 = (bf16[2,4,128,1024]{3,2,1,0:T(8,128)(2,1)}, bf16[2,4,128,1024]{3,2,1,0:T(8,128)(2,1)}, u32[]{:S(2)}, u32[]{:S(2)}) collective-permute-start(bf16[2,4,128,1024]{3,2,1,0:T(8,128)(2,1)} %get-tuple-element.190), channel_id=1, source_target_pairs={{0,8},{4,20},{8,0},{12,28},{16,24},{20,4},{24,16},{28,12},{1,9},{5... | collective-permute-start | bytes 6291464 | tf_op jit(solution)/shard_map/ppermute | solution.py:885
  226.9 12.5 %collective-permute-start.28 = (bf16[4,512,1024]{2,1,0:T(8,128)(2,1)}, bf16[4,512,1024]{2,1,0:T(8,128)(2,1)}, u32[]{:S(2)}, u32[]{:S(2)}) collective-permute-start(bf16[4,512,1024]{2,1,0:T(8,128)(2,1)} %get-tuple-element.196.refs_2_), channel_id=1, source_target_pairs={{0,4},{4,0},{8,12},{12,8},{16,20},{20,16},{24,28},{28,24},{1,5},{5... | collective-permute-start | bytes 12582920 | tf_op jit(solution)/shard_map/ppermute | solution.py:885
  227.0 12.4 %collective-permute-start.29 = (bf16[512,1024]{1,0:T(8,128)(2,1)}, bf16[512,1024]{1,0:T(8,128)(2,1)}, u32[]{:S(2)}, u32[]{:S(2)}) collective-permute-start(bf16[512,1024]{1,0:T(8,128)(2,1)} %get-tuple-element.213.refs_4_.mg_ref), channel_id=1, source_target_pairs={{0,4},{4,0},{8,12},{12,8},{16,20},{20,16},{24,28},{28,24},{1,5},{5... | collective-permute-start | bytes 3145736 | tf_op jit(solution)/shard_map/ppermute | solution.py:885
  227.5 45.6 %all-to-all-start.2 = ((bf16[4,128,1024]{2,1,0:T(8,128)(2,1)}), bf16[4,128,1024]{2,1,0:T(8,128)(2,1)}, u32[]{:S(2)}, u32[]{:S(2)}) async-start(bf16[4,128,1024]{2,1,0:T(8,128)(2,1)} %bitcast.26), calls=%async_computation.2 | async-start | bytes 2097152 | tf_op jit(solution)/shard_map/all_to_all | solution.py:904
  239.0 25.1 %collective-permute-start.27 = (bf16[4,128,1024]{2,1,0:T(8,128)(2,1)}, bf16[4,128,1024]{2,1,0:T(8,128)(2,1)}, u32[]{:S(2)}, u32[]{:S(2)}) collective-permute-start(bf16[4,128,1024]{2,1,0:T(8,128)(2,1)} %pass_on.3), channel_id=1, source_target_pairs={{0,16},{4,12},{8,24},{12,4},{16,0},{20,28},{24,8},{28,20},{1,17},{... | collective-permute-start | bytes 3145736 | tf_op jit(solution)/shard_map/ppermute | solution.py:885
  251.3 35.5 %collective-permute-start.30 = (bf16[2,4,128,1280]{3,2,1,0:T(8,128)(2,1)}, bf16[2,4,128,1280]{3,2,1,0:T(8,128)(2,1)}, u32[]{:S(2)}, u32[]{:S(2)}) collective-permute-start(bf16[2,4,128,1280]{3,2,1,0:T(8,128)(2,1)} %get-tuple-element.215), channel_id=1, source_target_pairs={{0,8},{4,20},{8,0},{12,28},{16,24},{20,4},{24,16},{28,12},{1,9},{5... | collective-permute-start | bytes 7864328 | tf_op jit(solution)/shard_map/ppermute | solution.py:885
  268.1 49.2 %collective-permute-start.34 = (bf16[128,1024]{1,0:T(8,128)(2,1)}, bf16[128,1024]{1,0:T(8,128)(2,1)}, u32[]{:S(2)}, u32[]{:S(2)}) collective-permute-start(bf16[128,1024]{1,0:T(8,128)(2,1)} %get-tuple-element.210), channel_id=1, source_target_pairs={{0,3},{1,0},{2,1},{3,2},{4,7},{5,4},{6,5},{7,6},{8,11},{9,8},{10,9... | collective-permute-start | bytes 786440 | tf_op jit(solution)/shard_map/ppermute | solution.py:897
  271.9 45.4 %collective-permute-start.35 = (bf16[128,1024]{1,0:T(8,128)(2,1)}, bf16[128,1024]{1,0:T(8,128)(2,1)}, u32[]{:S(2)}, u32[]{:S(2)}) collective-permute-start(bf16[128,1024]{1,0:T(8,128)(2,1)} %get-tuple-element.211), channel_id=1, source_target_pairs={{0,2},{1,3},{2,0},{3,1},{4,6},{5,7},{6,4},{7,5},{8,10},{9,11},{10,... | collective-permute-start | bytes 786440 | tf_op jit(solution)/shard_map/ppermute | solution.py:897
  271.9 45.4 %collective-permute-start.36 = (bf16[128,1024]{1,0:T(8,128)(2,1)}, bf16[128,1024]{1,0:T(8,128)(2,1)}, u32[]{:S(2)}, u32[]{:S(2)}) collective-permute-start(bf16[128,1024]{1,0:T(8,128)(2,1)} %get-tuple-element.212), channel_id=1, source_target_pairs={{0,1},{1,2},{2,3},{3,0},{4,5},{5,6},{6,7},{7,4},{8,9},{9,10},{10,1... | collective-permute-start | bytes 786440 | tf_op jit(solution)/shard_map/ppermute | solution.py:897
  273.1 12.3 %copy-start.24 = (f32[2,1,768]{2,1,0:T(1,128)S(1)}, f32[2,1,768]{2,1,0:T(1,128)}, u32[]{:S(2)}) copy-start(f32[2,1,768]{2,1,0:T(1,128)} %get-tuple-element.241) | copy-start | bytes 18436
  284.7 19.8 %collective-permute-start.31 = (bf16[4,512,768]{2,1,0:T(8,128)(2,1)}, bf16[4,512,768]{2,1,0:T(8,128)(2,1)}, u32[]{:S(2)}, u32[]{:S(2)}) collective-permute-start(bf16[4,512,768]{2,1,0:T(8,128)(2,1)} %get-tuple-element.220.pg_ref.refs_2_), channel_id=1, source_target_pairs={{0,4},{4,0},{8,12},{12,8},{16,20},{20,16},{24,28},{28,24},{1,5},{5... | collective-permute-start | bytes 9437192 | tf_op jit(solution)/shard_map/ppermute | solution.py:885
  290.7 26.6 %collective-permute-start.33 = (bf16[4,128,1280]{2,1,0:T(8,128)(2,1)}, bf16[4,128,1280]{2,1,0:T(8,128)(2,1)}, u32[]{:S(2)}, u32[]{:S(2)}) collective-permute-start(bf16[4,128,1280]{2,1,0:T(8,128)(2,1)} %pass_on.4), channel_id=1, source_target_pairs={{0,16},{4,12},{8,24},{12,4},{16,0},{20,28},{24,8},{28,20},{1,17},{... | collective-permute-start | bytes 3932168 | tf_op jit(solution)/shard_map/ppermute | solution.py:885
  300.2 39.0 %all-to-all-start.3 = ((bf16[4,128,1024]{2,1,0:T(8,128)(2,1)}), bf16[4,128,1024]{2,1,0:T(8,128)(2,1)}, u32[]{:S(2)}, u32[]{:S(2)}) async-start(bf16[4,128,1024]{2,1,0:T(8,128)(2,1)} %bitcast.86), calls=%async_computation.3 | async-start | bytes 2097152 | tf_op jit(solution)/shard_map/all_to_all | solution.py:904
  304.5 12.0 %copy-start.28 = (f32[2]{0:T(128)S(1)}, f32[2]{0:T(128)}, u32[]{:S(2)}) copy-start(f32[2]{0:T(128)} %pad_maximum_fusion.5) | copy-start | bytes 28
  304.5 12.0 %copy-start.6 = (f32[32,32]{1,0:T(8,128)S(1)}, f32[32,32]{1,0:T(8,128)}, u32[]{:S(2)}) copy-start(f32[32,32]{1,0:T(8,128)} %reshape_squeeze.21) | copy-start | bytes 12292
  304.5 12.0 %copy-start.7 = (f32[32,32]{1,0:T(8,128)S(1)}, f32[32,32]{1,0:T(8,128)}, u32[]{:S(2)}) copy-start(f32[32,32]{1,0:T(8,128)} %reshape_squeeze.22) | copy-start | bytes 12292
  304.5 12.0 %copy-start.8 = (f32[32,32]{1,0:T(8,128)S(1)}, f32[32,32]{1,0:T(8,128)}, u32[]{:S(2)}) copy-start(f32[32,32]{1,0:T(8,128)} %reshape_squeeze.23) | copy-start | bytes 12292
  304.5 12.0 %copy-start.9 = (f32[32,32]{1,0:T(8,128)S(1)}, f32[32,32]{1,0:T(8,128)}, u32[]{:S(2)}) copy-start(f32[32,32]{1,0:T(8,128)} %reshape_squeeze.18) | copy-start | bytes 12292
  304.5 12.0 %copy-start.10 = (f32[32,32]{1,0:T(8,128)S(1)}, f32[32,32]{1,0:T(8,128)}, u32[]{:S(2)}) copy-start(f32[32,32]{1,0:T(8,128)} %reshape_squeeze.19) | copy-start | bytes 12292
  304.5 12.0 %copy-start.11 = (f32[32,32]{1,0:T(8,128)S(1)}, f32[32,32]{1,0:T(8,128)}, u32[]{:S(2)}) copy-start(f32[32,32]{1,0:T(8,128)} %reshape_squeeze.20) | copy-start | bytes 12292
  304.5 12.0 %copy-start.12 = (f32[32,32]{1,0:T(8,128)S(1)}, f32[32,32]{1,0:T(8,128)}, u32[]{:S(2)}) copy-start(f32[32,32]{1,0:T(8,128)} %reshape_reshape.10) | copy-start | bytes 12292
  304.6 12.0 %copy-start.13 = (f32[32,32]{1,0:T(8,128)S(1)}, f32[32,32]{1,0:T(8,128)}, u32[]{:S(2)}) copy-start(f32[32,32]{1,0:T(8,128)} %reshape_reshape.9) | copy-start | bytes 12292
  304.6 12.0 %copy-start.14 = (f32[32,128]{1,0:T(8,128)S(1)}, f32[32,128]{1,0:T(8,128)}, u32[]{:S(2)}) copy-start(f32[32,128]{1,0:T(8,128)} %reshape_reshape.11) | copy-start | bytes 49156
  313.6 20.7 %collective-permute-start.32 = (bf16[2,4,128,768]{3,2,1,0:T(8,128)(2,1)}, bf16[2,4,128,768]{3,2,1,0:T(8,128)(2,1)}, u32[]{:S(2)}, u32[]{:S(2)}) collective-permute-start(bf16[2,4,128,768]{3,2,1,0:T(8,128)(2,1)} %get-tuple-element.222), channel_id=1, source_target_pairs={{0,8},{4,20},{8,0},{12,28},{16,24},{20,4},{24,16},{28,12},{1,9},{5... | collective-permute-start | bytes 4718600 | tf_op jit(solution)/shard_map/ppermute | solution.py:885
  321.7 30.3 %collective-permute-start.41 = (bf16[128,1280]{1,0:T(8,128)(2,1)}, bf16[128,1280]{1,0:T(8,128)(2,1)}, u32[]{:S(2)}, u32[]{:S(2)}) collective-permute-start(bf16[128,1280]{1,0:T(8,128)(2,1)} %get-tuple-element.225), channel_id=1, source_target_pairs={{0,3},{1,0},{2,1},{3,2},{4,7},{5,4},{6,5},{7,6},{8,11},{9,8},{10,9... | collective-permute-start | bytes 983048 | tf_op jit(solution)/shard_map/ppermute | solution.py:897
  325.5 34.7 %collective-permute-start.42 = (bf16[128,1280]{1,0:T(8,128)(2,1)}, bf16[128,1280]{1,0:T(8,128)(2,1)}, u32[]{:S(2)}, u32[]{:S(2)}) collective-permute-start(bf16[128,1280]{1,0:T(8,128)(2,1)} %get-tuple-element.226), channel_id=1, source_target_pairs={{0,2},{1,3},{2,0},{3,1},{4,6},{5,7},{6,4},{7,5},{8,10},{9,11},{10,... | collective-permute-start | bytes 983048 | tf_op jit(solution)/shard_map/ppermute | solution.py:897
  325.5 34.6 %collective-permute-start.43 = (bf16[128,1280]{1,0:T(8,128)(2,1)}, bf16[128,1280]{1,0:T(8,128)(2,1)}, u32[]{:S(2)}, u32[]{:S(2)}) collective-permute-start(bf16[128,1280]{1,0:T(8,128)(2,1)} %get-tuple-element.227), channel_id=1, source_target_pairs={{0,1},{1,2},{2,3},{3,0},{4,5},{5,6},{6,7},{7,4},{8,9},{9,10},{10,1... | collective-permute-start | bytes 983048 | tf_op jit(solution)/shard_map/ppermute | solution.py:897
  338.0 24.7 %collective-permute-start.37 = (bf16[4,128,768]{2,1,0:T(8,128)(2,1)}, bf16[4,128,768]{2,1,0:T(8,128)(2,1)}, u32[]{:S(2)}, u32[]{:S(2)}) collective-permute-start(bf16[4,128,768]{2,1,0:T(8,128)(2,1)} %pass_on.5), channel_id=1, source_target_pairs={{0,16},{4,12},{8,24},{12,4},{16,0},{20,28},{24,8},{28,20},{1,17},{... | collective-permute-start | bytes 2359304 | tf_op jit(solution)/shard_map/ppermute | solution.py:885
  339.9 21.4 %all-to-all-start.4 = ((f32[32,1,418]{2,1,0:T(1,128)}), f32[32,1,418]{2,1,0:T(1,128)}, u32[]{:S(2)}, u32[]{:S(2)}) async-start(f32[32,1,418]{2,1,0:T(1,128)} %copy.66), calls=%async_computation.4 | async-start | bytes 131072 | tf_op jit(solution)/shard_map/all_to_all | solution.py:1071
  367.7 16.9 %collective-permute-start.38 = (bf16[128,768]{1,0:T(8,128)(2,1)}, bf16[128,768]{1,0:T(8,128)(2,1)}, u32[]{:S(2)}, u32[]{:S(2)}) collective-permute-start(bf16[128,768]{1,0:T(8,128)(2,1)} %get-tuple-element.235), channel_id=1, source_target_pairs={{0,3},{1,0},{2,1},{3,2},{4,7},{5,4},{6,5},{7,6},{8,11},{9,8},{10,9... | collective-permute-start | bytes 589832 | tf_op jit(solution)/shard_map/ppermute | solution.py:897
  369.9 17.6 %collective-permute-start.39 = (bf16[128,768]{1,0:T(8,128)(2,1)}, bf16[128,768]{1,0:T(8,128)(2,1)}, u32[]{:S(2)}, u32[]{:S(2)}) collective-permute-start(bf16[128,768]{1,0:T(8,128)(2,1)} %get-tuple-element.236), channel_id=1, source_target_pairs={{0,2},{1,3},{2,0},{3,1},{4,6},{5,7},{6,4},{7,5},{8,10},{9,11},{10,... | collective-permute-start | bytes 589832 | tf_op jit(solution)/shard_map/ppermute | solution.py:897
  370.0 17.6 %collective-permute-start.40 = (bf16[128,768]{1,0:T(8,128)(2,1)}, bf16[128,768]{1,0:T(8,128)(2,1)}, u32[]{:S(2)}, u32[]{:S(2)}) collective-permute-start(bf16[128,768]{1,0:T(8,128)(2,1)} %get-tuple-element.237), channel_id=1, source_target_pairs={{0,1},{1,2},{2,3},{3,0},{4,5},{5,6},{6,7},{7,4},{8,9},{9,10},{10,1... | collective-permute-start | bytes 589832 | tf_op jit(solution)/shard_map/ppermute | solution.py:897
  (24 other events, 93.6 us)
where the time goes:
time: 392 us; the launch traced here: 390 us
  Pallas kernels  193 us (49%)
  starting transfers between devices  89.8 us (23%)
  waiting for transfers between devices  52.6 us (13%)
  local copies, waits for them, and re-layouts  36.3 us (9%)
  other arithmetic  8.93 us (2%)
  between operations  5.93 us (2%)
    ppermute x18, starting transfers between devices, shift(): return lax.ppermute(x, 'mp', [(i, (i + s) % mpn) for i in range(mpn)])  41.1 us
    ppermute x18, waiting for transfers between devices, shift(): return lax.ppermute(x, 'mp', [(i, (i + s) % mpn) for i in range(mpn)])  30.7 us
    pallas_call x3, Pallas kernels, weight_grad(): pl.pallas_call(functools.partial(weight_grad_body, len(groups), looped),...  30.3 us
    pallas_call x4, Pallas kernels, attend(): pl.pallas_call(functools.partial(attend_body, shard, gathered), grid=(pai...  28.3 us
    pallas_call x2, Pallas kernels, attend_back(): pl.pallas_call(attend_back_body, grid=(count, pairs), out_shape=[jax.Shap...  23.1 us
    pallas_call x1, Pallas kernels, up_back(): pl.pallas_call(functools.partial(up_back_body, shards, g_down, g_up), gri...  21.8 us
    pallas_call x1, Pallas kernels, up_project(): pl.pallas_call(functools.partial(up_body, shards, g_out, g_up), grid=(sha...  20.9 us
    ppermute x26, starting transfers between devices, exchange(): return lax.ppermute(x, 'dp', pairs)  17.7 us
  transfers between devices with their start and end apart: 49, of which 9 were waited for; matrix products, arithmetic and copies ran while one was open for 10% of the time, Pallas kernels for 45%

commit v1 on v0

--- a/solution.py
+++ b/solution.py
@@ -291,8 +291,8 @@
     units = wu.shape[-1]
 
     def columns(n, _):
-        span = pl.ds(pl.multiple_of(n * 256, 256), 256)
-        u = dot(low_ref[...], wu[s, :, :, span].reshape(width, 256), ((1,), (0,)))
+        span = pl.ds(pl.multiple_of(n * 512, 512), 512)
+        u = dot(low_ref[...], wu[s, :, :, span].reshape(width, 512), ((1,), (0,)))
         u = u + bias_ref[0, :, span]
         phi = 0.5 + 0.5 * lax.erf(u * (2.0**-0.5))
         act_ref[0, :, span] = (u * phi).astype(bf16)
@@ -300,7 +300,7 @@
         slope_ref[0, :, span] = slope.astype(bf16)
         return 0
 
-    lax.fori_loop(0, units // 256, columns, 0)
+    lax.fori_loop(0, units // 512, columns, 0)
 
     @pl.when(s == shards - 1)
     def _():

time: 392 us -> 391 us (level)
  transfers between devices with their start and end apart: 49 -> 49, of which waited for: 9 -> 10; matrix products, arithmetic and copies ran while one was open for 10% -> 10% of each run, Pallas kernels for 45% -> 45%
where the time goes in v1:
time: 391 us; the launch traced here: 389 us
  Pallas kernels  193 us (49%)
  starting transfers between devices  89.8 us (23%)
  waiting for transfers between devices  52.7 us (13%)
  local copies, waits for them, and re-layouts  36.3 us (9%)
  other arithmetic  8.93 us (2%)
  between operations  5.93 us (2%)
    ppermute x18, starting transfers between devices, shift(): return lax.ppermute(x, 'mp', [(i, (i + s) % mpn) for i in range(mpn)])  41.1 us
    ppermute x18, waiting for transfers between devices, shift(): return lax.ppermute(x, 'mp', [(i, (i + s) % mpn) for i in range(mpn)])  30.8 us
    pallas_call x3, Pallas kernels, weight_grad(): pl.pallas_call(functools.partial(weight_grad_body, len(groups), looped),...  30.3 us
    pallas_call x4, Pallas kernels, attend(): pl.pallas_call(functools.partial(attend_body, shard, gathered), grid=(pai...  28.3 us
    pallas_call x2, Pallas kernels, attend_back(): pl.pallas_call(attend_back_body, grid=(count, pairs), out_shape=[jax.Shap...  23.1 us
    pallas_call x1, Pallas kernels, up_back(): pl.pallas_call(functools.partial(up_back_body, shards, g_down, g_up), gri...  21.8 us
    pallas_call x1, Pallas kernels, up_project(): pl.pallas_call(functools.partial(up_body, shards, g_out, g_up), grid=(sha...  20.1 us
    ppermute x26, starting transfers between devices, exchange(): return lax.ppermute(x, 'dp', pairs)  17.7 us
  transfers between devices with their start and end apart: 49, of which 10 were waited for; matrix products, arithmetic and copies ran while one was open for 10% of the time, Pallas kernels for 45%

profile of v1, /device:TPU:0, one launch (start us, length us, event | category | flops | bytes accessed | tf_op | source)
XLA Modules:
  0.0 388.9 jit_solution(10590842896023735841)
XLA Ops:
  3.7 3.1 collective-permute-start
  6.8 2.6 collective-permute-start.1
  12.3 1.8 dynamic-slice_bitcast_fusion
  14.1 2.0 concatenate.63
  16.1 7.0 %collective-permute-done.1.refs_1_ = bf16[3,136,256]{2,1,0:T(8,128)(2,1)S(1)} collective-permute-done((bf16[3,136,256]{2,1,0:T(8,128)(2,1)S(1)}, bf16[3,136,256]{2,1,0:T(8,128)(2,1)S(1)}, u32[]{:S(2)}, u32[]{:S(2)}) %collective-permute-start.1) | collective-permute-done | bytes 208928 | tf_op jit(solution)/shard_map/ppermute | solution.py:897
  23.8 2.1 pack.6
  25.9 1.5 collective-permute-start.6
  28.2 4.9 %collective-permute-start.3 = (bf16[168,1024]{1,0:T(8,128)(2,1)}, bf16[168,1024]{1,0:T(8,128)(2,1)}, u32[]{:S(2)}, u32[]{:S(2)}) collective-permute-start(bf16[168,1024]{1,0:T(8,128)(2,1)} %concatenate.63), channel_id=1, source_target_pairs={{0,1},{1,2},{2,3},{3,0},{4,5},{5,6},{6,7},{7,4},{8,9},{9,10},{10,1... | collective-permute-start | bytes 1032200 | tf_op jit(solution)/shard_map/ppermute | solution.py:897
  33.0 1.7 collective-permute-start.4
  36.7 4.3 %all-to-all-start = ((bf16[4,128,1024]{2,1,0:T(8,128)(2,1)}), bf16[4,128,1024]{2,1,0:T(8,128)(2,1)}, u32[]{:S(2)}, u32[]{:S(2)}) async-start(bf16[4,128,1024]{2,1,0:T(8,128)(2,1)} %bitcast.76), calls=%async_computation | async-start | bytes 2097152 | tf_op jit(solution)/shard_map/all_to_all | solution.py:900
  41.8 2.3 pack.7.refs_1_
  44.1 1.6 collective-permute-start.8
  45.7 12.7 %collective-permute-done.4.refs_1_ = bf16[168,1024]{1,0:T(8,128)(2,1)} collective-permute-done((bf16[168,1024]{1,0:T(8,128)(2,1)}, bf16[168,1024]{1,0:T(8,128)(2,1)}, u32[]{:S(2)}, u32[]{:S(2)}) %collective-permute-start.4) | collective-permute-done | bytes 344096 | tf_op jit(solution)/shard_map/ppermute | solution.py:897
  58.4 2.2 pack.8
  66.7 2.6 embed.1.te_ref
  70.0 5.1 %collective-permute-done.7.refs_1_ = bf16[3,160,1024]{2,1,0:T(8,128)(2,1)} collective-permute-done((bf16[3,160,1024]{2,1,0:T(8,128)(2,1)}, bf16[3,160,1024]{2,1,0:T(8,128)(2,1)}, u32[]{:S(2)}, u32[]{:S(2)}) %collective-permute-start.7) | collective-permute-done | bytes 983072 | tf_op jit(solution)/shard_map/ppermute | solution.py:885
  75.1 2.8 pack.9.refs_1_.refs_6_
  78.0 2.1 collective-permute-start.15
  80.2 5.9 %all-to-all-done = bf16[4,128,1024]{2,1,0:T(8,128)(2,1)} async-done(((bf16[4,128,1024]{2,1,0:T(8,128)(2,1)}), bf16[4,128,1024]{2,1,0:T(8,128)(2,1)}, u32[]{:S(2)}, u32[]{:S(2)}) %all-to-all-start) | async-done | bytes 1048608 | tf_op jit(solution)/shard_map/all_to_all | solution.py:900
  86.1 2.4 add_convert_fusion.x_hbm.refs_0_
  88.5 10.4 %collective-permute-start.11 = (bf16[128,1024]{1,0:T(8,128)(2,1)}, bf16[128,1024]{1,0:T(8,128)(2,1)}, u32[]{:S(2)}, u32[]{:S(2)}) collective-permute-start(bf16[128,1024]{1,0:T(8,128)(2,1)} %get-tuple-element.154), channel_id=1, source_target_pairs={{0,1},{1,2},{2,3},{3,0},{4,5},{5,6},{6,7},{7,4},{8,9},{9,10},{10,1... | collective-permute-start | bytes 786440 | tf_op jit(solution)/shard_map/ppermute | solution.py:897
  98.9 3.4 collective-permute-start.12
  102.3 7.0 %attend.4 = (bf16[4,512,768]{2,1,0:T(8,128)(2,1)}, bf16[4,4,512,512]{3,2,1,0:T(8,128)(2,1)}, bf16[4,512,256]{2,1,0:T(8,128)(2,1)}) custom-call(s32[1]{0:T(128)} %bitcast.place_ref, bf16[512,1024]{1,0:T(8,128)(2,1)} %add_convert_fusion.x_hbm.refs_0_, f32[1,3,1,256]{3,2,1,0:T(1,128)} %broadcast_in_dim_broadcast_in_dim.3.bias_ref, bf16[3,8,128,256]{3,2,1,0:T(8,128)(2,1)} %bitcast.81), custom_call_target="tpu_custom_call" | custom-call | flops 344999985152 | tf_op jit(solution)/shard_map/attend/pallas_call | solution.py:218
  109.3 7.1 %attend.5 = (bf16[4,512,768]{2,1,0:T(8,128)(2,1)}, bf16[4,4,512,512]{3,2,1,0:T(8,128)(2,1)}, bf16[4,512,256]{2,1,0:T(8,128)(2,1)}) custom-call(s32[1]{0:T(128)} %bitcast.place_ref, bf16[512,1024]{1,0:T(8,128)(2,1)} %add_convert_fusion.x_hbm.refs_0_, ...), custom_call_target="tpu_custom_call", output_to_operand_aliasing={{0}: (8, {}), {1}: (9, {}), {2}: (10, {})} | custom-call | flops 344999985152 | tf_op jit(solution)/shard_map/attend/pallas_call | solution.py:218
  116.5 7.1 %attend.6 = (bf16[4,512,768]{2,1,0:T(8,128)(2,1)}, bf16[4,4,512,512]{3,2,1,0:T(8,128)(2,1)}, bf16[4,512,256]{2,1,0:T(8,128)(2,1)}) custom-call(s32[1]{0:T(128)} %bitcast.place_ref, bf16[512,1024]{1,0:T(8,128)(2,1)} %add_convert_fusion.x_hbm.refs_0_, ...), custom_call_target="tpu_custom_call", output_to_operand_aliasing={{0}: (8, {}), {1}: (9, {}), {2}: (10, {})} | custom-call | flops 344999985152 | tf_op jit(solution)/shard_map/attend/pallas_call | solution.py:218
  123.6 2.0 pack.10.refs_0_
  126.2 7.1 %attend.7 = (bf16[4,512,768]{2,1,0:T(8,128)(2,1)}, bf16[4,4,512,512]{3,2,1,0:T(8,128)(2,1)}, bf16[4,512,256]{2,1,0:T(8,128)(2,1)}) custom-call(s32[1]{0:T(128)} %bitcast.place_ref, bf16[512,1024]{1,0:T(8,128)(2,1)} %add_convert_fusion.x_hbm.refs_0_, ...), custom_call_target="tpu_custom_call", output_to_operand_aliasing={{0}: (8, {}), {1}: (9, {}), {2}: (10, {})} | custom-call | flops 344999985152 | tf_op jit(solution)/shard_map/attend/pallas_call | solution.py:218
  134.6 7.6 %all-to-all-start.1 = ((bf16[4,128,1024]{2,1,0:T(8,128)(2,1)}), bf16[4,128,1024]{2,1,0:T(8,128)(2,1)}, u32[]{:S(2)}, u32[]{:S(2)}) async-start(bf16[4,128,1024]{2,1,0:T(8,128)(2,1)} %bitcast.75), calls=%async_computation.1 | async-start | bytes 2097152 | tf_op jit(solution)/shard_map/all_to_all | solution.py:900
  142.3 2.6 pack.11.refs_1_
  144.9 1.6 collective-permute-start.18
  147.0 20.1 %up_project.1 = (f32[512,1024]{1,0:T(8,128)}, f32[512,128]{1,0:T(8,128)}, bf16[512,1024]{1,0:T(8,128)(2,1)}, bf16[4,512,1024]{2,1,0:T(8,128)(2,1)}, bf16[4,512,1...) custom-call(s32[1]{0:T(128)} %bitcast.place_ref, bf16[4,512,256]{2,1,0:T(8,128)(2,1)} %get-tuple-element.200.ctx_ref.refs_6_, ...), custom_call_target="tpu_custom_call" | custom-call | flops 344999985152 | tf_op jit(solution)/shard_map/up_project/pallas_call | solution.py:317
  169.5 1.5 collective-permute-done.22.refs_4_
  172.1 13.6 %down_project.1 = (bf16[512,1024]{1,0:T(8,128)(2,1)}, bf16[512,1024]{1,0:T(8,128)(2,1)}, f32[3,1024]{1,0:T(4,128)}) custom-call(s32[1]{0:T(128)} %bitcast.place_ref, f32[1]{0:T(128)S(6)} %convert_element_type.37.live_ref, bf16[4,512,1024]{2,1,0:T(8,128)(2,1)} %get-tuple-element.175.act_ref.refs_2_, f32[1,1024]{1,0:T(1,128)} %bitcast.105, ...), custom_call_target="tpu_custom_call" | custom-call | flops 344999985152 | tf_op jit(solution)/shard_map/down_project/pallas_call | solution.py:428
  193.2 9.4 %weight_grad.3 = (bf16[2,4,128,1024]{3,2,1,0:T(8,128)(2,1)}, bf16[2,4,128,1024]{3,2,1,0:T(8,128)(2,1)}) custom-call(s32[1]{0:T(128)} %bitcast.place_ref, bf16[512,1024]{1,0:T(8,128)(2,1)} %get-tuple-element.185.refs_0_.bg_ref, bf16[512,1024]{1,0:T(8,128)(2,1)} %copy-done.30, bf16[4,512,1024]{2,1,0:T(8,128)(2,1)} %get-tuple-element.175.act_ref.refs_2_, ...), custom_call_target="tpu_custom_call" | custom-call | flops 344999985152 | tf_op jit(solution)/shard_map/weight_grad/pallas_call | solution.py:734
  202.7 1.6 collective-permute-start.25
  204.2 21.8 %up_back.1 = (bf16[4,512,1024]{2,1,0:T(8,128)(2,1)}, f32[4,1,1024]{2,1,0:T(1,128)}, f32[512,1024]{1,0:T(8,128)}, bf16[512,1024]{1,0:T(8,128)(2,1)}, f32[3,1024]{1,0:T(4,128)}) custom-call(s32[1]{0:T(128)} %bitcast.place_ref, bf16[512,1024]{1,0:T(8,128)(2,1)} %get-tuple-element.185.refs_0_.bg_ref, bf16[4,512,1024]{2,1,0:T(8,128)(2,1)} %get-tuple-element.186.slope_ref, ...), custom_call_target="tpu_custom_call" | custom-call | flops 344999985152 | tf_op jit(solution)/shard_map/up_back/pallas_call | solution.py:525
  226.7 5.1 %all-to-all-start.2 = ((bf16[4,128,1024]{2,1,0:T(8,128)(2,1)}), bf16[4,128,1024]{2,1,0:T(8,128)(2,1)}, u32[]{:S(2)}, u32[]{:S(2)}) async-start(bf16[4,128,1024]{2,1,0:T(8,128)(2,1)} %bitcast.26), calls=%async_computation.2 | async-start | bytes 2097152 | tf_op jit(solution)/shard_map/all_to_all | solution.py:904
  234.6 3.7 pass_on.3
  238.6 11.9 %weight_grad.4 = (bf16[2,4,128,1280]{3,2,1,0:T(8,128)(2,1)}, bf16[2,4,128,1280]{3,2,1,0:T(8,128)(2,1)}) custom-call(s32[1]{0:T(128)} %bitcast.place_ref, bf16[512,1024]{1,0:T(8,128)(2,1)} %get-tuple-element.194.refs_0_, bf16[512,1024]{1,0:T(8,128)(2,1)} %collective-permute-done.26.refs_1_, bf16[4,512,1024]{2,1,0:T(8,128)(2,1)} %get-tuple-element.196.refs_2_, ...), custom_call_target="tpu_custom_call" | custom-call | flops 344999985152 | tf_op jit(solution)/shard_map/weight_grad/pallas_call | solution.py:734
  251.8 11.5 %attend_back.2 = (bf16[4,512,768]{2,1,0:T(8,128)(2,1)}, f32[2,1,768]{2,1,0:T(1,128)}) custom-call(bf16[512,1024]{1,0:T(8,128)(2,1)} %get-tuple-element.213.refs_4_.mg_ref, bf16[4,256,1024]{2,1,0:T(8,128)(2,1)} %bitcast.78, bf16[4,512,768]{2,1,0:T(8,128)(2,1)} %get-tuple-element.205.qkv, bf16[4,4,512,512]{3,2,1,0:T(8,128)(2,1)} %get-tuple-element.206.p_of), custom_call_target="tpu_custom_call" | custom-call | flops 344999985152 | tf_op jit(solution)/shard_map/attend_back/pallas_call | solution.py:598
  263.4 4.0 %gather_up.3 = (f32[128,1024]{1,0:T(8,128)}, bf16[128,1024]{1,0:T(8,128)(2,1)}, bf16[128,1024]{1,0:T(8,128)(2,1)}, bf16[128,1024]{1,0:T(8,128)(2,1)}) custom-call(bf16[2,4,128,1024]{3,2,1,0:T(8,128)(2,1)} %get-tuple-element.184.keep_ref, bf16[2,4,128,1024]{3,2,1,0:T(8,128)(2,1)} %collective-permute-done.25.came_ref, ...), custom_call_target="tpu_custom_call" | custom-call | flops 1150000000 | tf_op jit(solution)/shard_map/gather_up/pallas_call | solution.py:798
  267.4 3.8 collective-permute-start.34
  272.3 11.6 %attend_back.3 = (bf16[4,512,768]{2,1,0:T(8,128)(2,1)}, f32[2,1,768]{2,1,0:T(1,128)}) custom-call(bf16[512,1024]{1,0:T(8,128)(2,1)} %get-tuple-element.213.refs_4_.mg_ref, bf16[4,256,1024]{2,1,0:T(8,128)(2,1)} %bitcast.79, bf16[4,512,768]{2,1,0:T(8,128)(2,1)} %get-tuple-element.205.qkv, ...), custom_call_target="tpu_custom_call", output_to_operand_aliasing={{0}: (4, {})} | custom-call | flops 1150000000 | tf_op jit(solution)/shard_map/attend_back/pallas_call | solution.py:598
  286.1 3.8 pass_on.4
  290.8 8.7 %input_back.1 = (bf16[512,1024]{1,0:T(8,128)(2,1)}, f32[1,1024]{1,0:T(1,128)}) custom-call(s32[1]{0:T(128)} %bitcast.place_ref, bf16[4,512,768]{2,1,0:T(8,128)(2,1)} %get-tuple-element.220.pg_ref.refs_2_, f32[512,1024]{1,0:T(8,128)} %get-tuple-element.218.gf_hbm, bf16[3,8,128,256]{3,2,1,0:T(8,128)(2,1)} %bitcast.85, ...), custom_call_target="tpu_custom_call" | custom-call | flops 1150000000 | tf_op jit(solution)/shard_map/input_back/pallas_call | solution.py:661
  299.4 4.2 %all-to-all-start.3 = ((bf16[4,128,1024]{2,1,0:T(8,128)(2,1)}), bf16[4,128,1024]{2,1,0:T(8,128)(2,1)}, u32[]{:S(2)}, u32[]{:S(2)}) async-start(bf16[4,128,1024]{2,1,0:T(8,128)(2,1)} %bitcast.86), calls=%async_computation.3 | async-start | bytes 2097152 | tf_op jit(solution)/shard_map/all_to_all | solution.py:904
  303.8 9.0 %weight_grad.5 = (bf16[2,4,128,768]{3,2,1,0:T(8,128)(2,1)}, bf16[2,4,128,768]{3,2,1,0:T(8,128)(2,1)}) custom-call(s32[1]{0:T(128)} %bitcast.place_ref, bf16[512,1024]{1,0:T(8,128)(2,1)} %add_convert_fusion.x_hbm.refs_0_, bf16[512,1024]{1,0:T(8,128)(2,1)} %collective-permute-done.21.refs_1_, bf16[4,512,768]{2,1,0:T(8,128)(2,1)} %get-tuple-element.220.pg_ref.refs_2_, ...), custom_call_target="tpu_custom_call" | custom-call | flops 344999985152 | tf_op jit(solution)/shard_map/weight_grad/pallas_call | solution.py:734
  312.9 1.6 collective-permute-start.32
  316.5 4.4 %gather_up.4 = (f32[128,1280]{1,0:T(8,128)}, bf16[128,1280]{1,0:T(8,128)(2,1)}, bf16[128,1280]{1,0:T(8,128)(2,1)}, bf16[128,1280]{1,0:T(8,128)(2,1)}) custom-call(bf16[2,4,128,1280]{3,2,1,0:T(8,128)(2,1)} %get-tuple-element.202.keep_ref, bf16[2,4,128,1280]{3,2,1,0:T(8,128)(2,1)} %collective-permute-done.30.came_ref, ...), custom_call_target="tpu_custom_call" | custom-call | flops 344999985152 | tf_op jit(solution)/shard_map/gather_up/pallas_call | solution.py:798
  320.9 3.8 collective-permute-start.41
  325.8 7.8 %collective-permute-done.32.came_ref = bf16[2,4,128,768]{3,2,1,0:T(8,128)(2,1)} collective-permute-done((bf16[2,4,128,768]{3,2,1,0:T(8,128)(2,1)}, bf16[2,4,128,768]{3,2,1,0:T(8,128)(2,1)}, u32[]{:S(2)}, u32[]{:S(2)}) %collective-permute-start.32) | collective-permute-done | bytes 1572896 | tf_op jit(solution)/shard_map/ppermute | solution.py:885
  333.6 3.6 pass_on.5
  339.1 9.8 %all-to-all-start.4 = ((f32[32,1,418]{2,1,0:T(1,128)}), f32[32,1,418]{2,1,0:T(1,128)}, u32[]{:S(2)}, u32[]{:S(2)}) async-start(f32[32,1,418]{2,1,0:T(1,128)} %copy.66), calls=%async_computation.4 | async-start | bytes 131072 | tf_op jit(solution)/shard_map/all_to_all | solution.py:1071
  348.9 2.3 finish.3
  351.2 8.1 %collective-permute-done.42.refs_2_ = bf16[128,1280]{1,0:T(8,128)(2,1)} collective-permute-done((bf16[128,1280]{1,0:T(8,128)(2,1)}, bf16[128,1280]{1,0:T(8,128)(2,1)}, u32[]{:S(2)}, u32[]{:S(2)}) %collective-permute-start.42) | collective-permute-done | bytes 327712 | tf_op jit(solution)/shard_map/ppermute | solution.py:897
  360.5 1.5 copy.75
  361.9 3.8 gather_up.5
  366.9 2.2 collective-permute-start.38
  372.3 2.7 copy.68
  375.0 3.0 copy.67
  379.8 2.4 finish.5
  382.3 1.6 convolution_multiply_fusion.1
  383.9 2.9 collective-permute-done.39.refs_2_
  386.8 2.1 finish.4
  (212 shorter events, 47.5 us)
Async XLA Ops:
  0.6 64.4 %copy-start = (f32[32,1024]{1,0:T(8,128)S(1)}, f32[32,1024]{1,0:T(8,128)}, u32[]{:S(2)}) copy-start(f32[32,1024]{1,0:T(8,128)} %param.24) | copy-start | bytes 393220
  3.7 12.4 %collective-permute-start = (bf16[3,136,256]{2,1,0:T(8,128)(2,1)S(1)}, bf16[3,136,256]{2,1,0:T(8,128)(2,1)S(1)}, u32[]{:S(2)}, u32[]{:S(2)}) collective-permute-start(bf16[3,136,256]{2,1,0:T(8,128)(2,1)S(1)} %concatenate.65), channel_id=1, source_target_pairs={{0,1},{1,2},{2,3},{3,0},{4,5},{5,6},{6,7},{7,4},{8,9},{9,10},{10,1... | collective-permute-start | bytes 626696 | tf_op jit(solution)/shard_map/ppermute | solution.py:897
  6.8 16.3 %collective-permute-start.1 = (bf16[3,136,256]{2,1,0:T(8,128)(2,1)S(1)}, bf16[3,136,256]{2,1,0:T(8,128)(2,1)S(1)}, u32[]{:S(2)}, u32[]{:S(2)}) collective-permute-start(bf16[3,136,256]{2,1,0:T(8,128)(2,1)S(1)} %concatenate.65), channel_id=1, source_target_pairs={{0,2},{1,3},{2,0},{3,1},{4,6},{5,7},{6,4},{7,5},{8,10},{9,11},{10,... | collective-permute-start | bytes 626696 | tf_op jit(solution)/shard_map/ppermute | solution.py:897
  9.4 13.7 %collective-permute-start.2 = (bf16[3,136,256]{2,1,0:T(8,128)(2,1)S(1)}, bf16[3,136,256]{2,1,0:T(8,128)(2,1)S(1)}, u32[]{:S(2)}, u32[]{:S(2)}) collective-permute-start(bf16[3,136,256]{2,1,0:T(8,128)(2,1)S(1)} %concatenate.65), channel_id=1, source_target_pairs={{0,3},{1,0},{2,1},{3,2},{4,7},{5,4},{6,5},{7,6},{8,11},{9,8},{10,9... | collective-permute-start | bytes 626696 | tf_op jit(solution)/shard_map/ppermute | solution.py:897
  23.8 11.6 %copy-start.2 = (bf16[128,4,1024]{2,1,0:T(4,128)(2,1)S(1)}, bf16[128,4,1024]{2,1,0:T(4,128)(2,1)}, u32[]{:S(2)}) copy-start(bf16[128,4,1024]{2,1,0:T(4,128)(2,1)} %param.19) | copy-start | bytes 3145732
  25.9 15.0 %collective-permute-start.6 = (bf16[3,3,128,256]{3,2,1,0:T(8,128)(2,1)}, bf16[3,3,128,256]{3,2,1,0:T(8,128)(2,1)S(1)}, u32[]{:S(2)}, u32[]{:S(2)}) collective-permute-start(bf16[3,3,128,256]{3,2,1,0:T(8,128)(2,1)} %get-tuple-element.141.refs_0_), channel_id=1, source_target_pairs={{0,8},{4,20},{8,0},{12,28},{16,24},{20,4},{24,16},{28,12},{1,9},{5... | collective-permute-start | bytes 1769480 | tf_op jit(solution)/shard_map/ppermute | solution.py:885
  28.2 17.5 %collective-permute-start.3 = (bf16[168,1024]{1,0:T(8,128)(2,1)}, bf16[168,1024]{1,0:T(8,128)(2,1)}, u32[]{:S(2)}, u32[]{:S(2)}) collective-permute-start(bf16[168,1024]{1,0:T(8,128)(2,1)} %concatenate.63), channel_id=1, source_target_pairs={{0,1},{1,2},{2,3},{3,0},{4,5},{5,6},{6,7},{7,4},{8,9},{9,10},{10,1... | collective-permute-start | bytes 1032200 | tf_op jit(solution)/shard_map/ppermute | solution.py:897
  33.0 25.3 %collective-permute-start.4 = (bf16[168,1024]{1,0:T(8,128)(2,1)}, bf16[168,1024]{1,0:T(8,128)(2,1)}, u32[]{:S(2)}, u32[]{:S(2)}) collective-permute-start(bf16[168,1024]{1,0:T(8,128)(2,1)} %concatenate.63), channel_id=1, source_target_pairs={{0,2},{1,3},{2,0},{3,1},{4,6},{5,7},{6,4},{7,5},{8,10},{9,11},{10,... | collective-permute-start | bytes 1032200 | tf_op jit(solution)/shard_map/ppermute | solution.py:897
  34.7 23.7 %collective-permute-start.5 = (bf16[168,1024]{1,0:T(8,128)(2,1)}, bf16[168,1024]{1,0:T(8,128)(2,1)}, u32[]{:S(2)}, u32[]{:S(2)}) collective-permute-start(bf16[168,1024]{1,0:T(8,128)(2,1)} %concatenate.63), channel_id=1, source_target_pairs={{0,3},{1,0},{2,1},{3,2},{4,7},{5,4},{6,5},{7,6},{8,11},{9,8},{10,9... | collective-permute-start | bytes 1032200 | tf_op jit(solution)/shard_map/ppermute | solution.py:897
  36.7 49.4 %all-to-all-start = ((bf16[4,128,1024]{2,1,0:T(8,128)(2,1)}), bf16[4,128,1024]{2,1,0:T(8,128)(2,1)}, u32[]{:S(2)}, u32[]{:S(2)}) async-start(bf16[4,128,1024]{2,1,0:T(8,128)(2,1)} %bitcast.76), calls=%async_computation | async-start | bytes 2097152 | tf_op jit(solution)/shard_map/all_to_all | solution.py:900
  44.1 21.6 %collective-permute-start.8 = (bf16[2,3,3,128,256]{4,3,2,1,0:T(8,128)(2,1)}, bf16[2,3,3,128,256]{4,3,2,1,0:T(8,128)(2,1)}, u32[]{:S(2)}, u32[]{:S(2)}) collective-permute-start(bf16[2,3,3,128,256]{4,3,2,1,0:T(8,128)(2,1)} %pack.7.refs_1_), channel_id=1, source_target_pairs={{0,16},{4,12},{8,24},{12,4},{16,0},{20,28},{24,8},{28,20},{1,17},{... | collective-permute-start | bytes 3538952 | tf_op jit(solution)/shard_map/ppermute | solution.py:885
  45.7 29.4 %collective-permute-start.10 = (bf16[2,3,3,128,256]{4,3,2,1,0:T(8,128)(2,1)}, bf16[2,3,3,128,256]{4,3,2,1,0:T(8,128)(2,1)}, u32[]{:S(2)}, u32[]{:S(2)}) collective-permute-start(bf16[2,3,3,128,256]{4,3,2,1,0:T(8,128)(2,1)} %pack.7.refs_1_), channel_id=1, source_target_pairs={{0,4},{4,0},{8,12},{12,8},{16,20},{20,16},{24,28},{28,24},{1,5},{5... | collective-permute-start | bytes 3538952 | tf_op jit(solution)/shard_map/ppermute | solution.py:885
  60.6 14.5 %collective-permute-start.7 = (bf16[3,160,1024]{2,1,0:T(8,128)(2,1)}, bf16[3,160,1024]{2,1,0:T(8,128)(2,1)}, u32[]{:S(2)}, u32[]{:S(2)}) collective-permute-start(bf16[3,160,1024]{2,1,0:T(8,128)(2,1)} %get-tuple-element.146.refs_0_), channel_id=1, source_target_pairs={{0,8},{4,20},{8,0},{12,28},{16,24},{20,4},{24,16},{28,12},{1,9},{5... | collective-permute-start | bytes 2949128 | tf_op jit(solution)/shard_map/ppermute | solution.py:885
  65.7 9.4 %collective-permute-start.9 = (bf16[2,3,3,128,256]{4,3,2,1,0:T(8,128)(2,1)}, bf16[2,3,3,128,256]{4,3,2,1,0:T(8,128)(2,1)}, u32[]{:S(2)}, u32[]{:S(2)}) collective-permute-start(bf16[2,3,3,128,256]{4,3,2,1,0:T(8,128)(2,1)} %collective-permute-done.8.refs_2_), channel_id=1, source_target_pairs={{0,4},{4,0},{8,12},{12,8},{16,20},{20,16},{24,28},{28,24},{1,5},{5... | collective-permute-start | bytes 3538952 | tf_op jit(solution)/shard_map/ppermute | solution.py:885
  77.9 31.3 %collective-permute-start.14 = (bf16[2,3,160,1024]{3,2,1,0:T(8,128)(2,1)}, bf16[2,3,160,1024]{3,2,1,0:T(8,128)(2,1)}, u32[]{:S(2)}, u32[]{:S(2)}) collective-permute-start(bf16[2,3,160,1024]{3,2,1,0:T(8,128)(2,1)} %pack.9.refs_1_.refs_6_), channel_id=1, source_target_pairs={{0,4},{4,0},{8,12},{12,8},{16,20},{20,16},{24,28},{28,24},{1,5},{5... | collective-permute-start | bytes 5898248 | tf_op jit(solution)/shard_map/ppermute | solution.py:885
  78.0 38.4 %collective-permute-start.15 = (bf16[2,3,160,1024]{3,2,1,0:T(8,128)(2,1)}, bf16[2,3,160,1024]{3,2,1,0:T(8,128)(2,1)}, u32[]{:S(2)}, u32[]{:S(2)}) collective-permute-start(bf16[2,3,160,1024]{3,2,1,0:T(8,128)(2,1)} %pack.9.refs_1_.refs_6_), channel_id=1, source_target_pairs={{0,16},{4,12},{8,24},{12,4},{16,0},{20,28},{24,8},{28,20},{1,17},{... | collective-permute-start | bytes 5898248 | tf_op jit(solution)/shard_map/ppermute | solution.py:885
  88.5 35.1 %collective-permute-start.11 = (bf16[128,1024]{1,0:T(8,128)(2,1)}, bf16[128,1024]{1,0:T(8,128)(2,1)}, u32[]{:S(2)}, u32[]{:S(2)}) collective-permute-start(bf16[128,1024]{1,0:T(8,128)(2,1)} %get-tuple-element.154), channel_id=1, source_target_pairs={{0,1},{1,2},{2,3},{3,0},{4,5},{5,6},{6,7},{7,4},{8,9},{9,10},{10,1... | collective-permute-start | bytes 786440 | tf_op jit(solution)/shard_map/ppermute | solution.py:897
  98.9 24.7 %collective-permute-start.12 = (bf16[128,1024]{1,0:T(8,128)(2,1)}, bf16[128,1024]{1,0:T(8,128)(2,1)}, u32[]{:S(2)}, u32[]{:S(2)}) collective-permute-start(bf16[128,1024]{1,0:T(8,128)(2,1)} %get-tuple-element.154), channel_id=1, source_target_pairs={{0,2},{1,3},{2,0},{3,1},{4,6},{5,7},{6,4},{7,5},{8,10},{9,11},{10,... | collective-permute-start | bytes 786440 | tf_op jit(solution)/shard_map/ppermute | solution.py:897
  102.3 21.3 %collective-permute-start.13 = (bf16[128,1024]{1,0:T(8,128)(2,1)}, bf16[128,1024]{1,0:T(8,128)(2,1)}, u32[]{:S(2)}, u32[]{:S(2)}) collective-permute-start(bf16[128,1024]{1,0:T(8,128)(2,1)} %get-tuple-element.154), channel_id=1, source_target_pairs={{0,3},{1,0},{2,1},{3,2},{4,7},{5,4},{6,5},{7,6},{8,11},{9,8},{10,9... | collective-permute-start | bytes 786440 | tf_op jit(solution)/shard_map/ppermute | solution.py:897
  116.4 7.2 %collective-permute-start.16 = (bf16[2,3,160,1024]{3,2,1,0:T(8,128)(2,1)}, bf16[2,3,160,1024]{3,2,1,0:T(8,128)(2,1)}, u32[]{:S(2)}, u32[]{:S(2)}) collective-permute-start(bf16[2,3,160,1024]{3,2,1,0:T(8,128)(2,1)} %collective-permute-done.15.refs_2_.refs_7_), channel_id=1, source_target_pairs={{0,4},{4,0},{8,12},{12,8},{16,20},{20,16},{24,28},{28,24},{1,5},{5... | collective-permute-start | bytes 5898248 | tf_op jit(solution)/shard_map/ppermute | solution.py:885
  125.7 16.6 %collective-permute-start.17 = (bf16[3,128,1024]{2,1,0:T(8,128)(2,1)}, bf16[3,128,1024]{2,1,0:T(8,128)(2,1)}, u32[]{:S(2)}, u32[]{:S(2)}) collective-permute-start(bf16[3,128,1024]{2,1,0:T(8,128)(2,1)} %pack.10.refs_0_), channel_id=1, source_target_pairs={{0,8},{4,20},{8,0},{12,28},{16,24},{20,4},{24,16},{28,12},{1,9},{5... | collective-permute-start | bytes 2359304 | tf_op jit(solution)/shard_map/ppermute | solution.py:885
  134.6 34.9 %all-to-all-start.1 = ((bf16[4,128,1024]{2,1,0:T(8,128)(2,1)}), bf16[4,128,1024]{2,1,0:T(8,128)(2,1)}, u32[]{:S(2)}, u32[]{:S(2)}) async-start(bf16[4,128,1024]{2,1,0:T(8,128)(2,1)} %bitcast.75), calls=%async_computation.1 | async-start | bytes 2097152 | tf_op jit(solution)/shard_map/all_to_all | solution.py:900
  144.9 22.3 %collective-permute-start.18 = (bf16[2,3,128,1024]{3,2,1,0:T(8,128)(2,1)}, bf16[2,3,128,1024]{3,2,1,0:T(8,128)(2,1)}, u32[]{:S(2)}, u32[]{:S(2)}) collective-permute-start(bf16[2,3,128,1024]{3,2,1,0:T(8,128)(2,1)} %pack.11.refs_1_), channel_id=1, source_target_pairs={{0,16},{4,12},{8,24},{12,4},{16,0},{20,28},{24,8},{28,20},{1,17},{... | collective-permute-start | bytes 4718600 | tf_op jit(solution)/shard_map/ppermute | solution.py:885
  146.4 20.7 %collective-permute-start.19 = (bf16[2,3,128,1024]{3,2,1,0:T(8,128)(2,1)}, bf16[2,3,128,1024]{3,2,1,0:T(8,128)(2,1)}, u32[]{:S(2)}, u32[]{:S(2)}) collective-permute-start(bf16[2,3,128,1024]{3,2,1,0:T(8,128)(2,1)} %pack.11.refs_1_), channel_id=1, source_target_pairs={{0,4},{4,0},{8,12},{12,8},{16,20},{20,16},{24,28},{28,24},{1,5},{5... | collective-permute-start | bytes 4718600 | tf_op jit(solution)/shard_map/ppermute | solution.py:885
  146.4 20.7 %collective-permute-start.21 = (bf16[512,1024]{1,0:T(8,128)(2,1)}, bf16[512,1024]{1,0:T(8,128)(2,1)}, u32[]{:S(2)}, u32[]{:S(2)}) collective-permute-start(bf16[512,1024]{1,0:T(8,128)(2,1)} %add_convert_fusion.x_hbm.refs_0_), channel_id=1, source_target_pairs={{0,4},{4,0},{8,12},{12,8},{16,20},{20,16},{24,28},{28,24},{1,5},{5... | collective-permute-start | bytes 3145736 | tf_op jit(solution)/shard_map/ppermute | solution.py:885
  147.0 20.2 %collective-permute-start.20 = (bf16[4,512,256]{2,1,0:T(8,128)(2,1)}, bf16[4,512,256]{2,1,0:T(8,128)(2,1)}, u32[]{:S(2)}, u32[]{:S(2)}) collective-permute-start(bf16[4,512,256]{2,1,0:T(8,128)(2,1)} %get-tuple-element.200.ctx_ref.refs_6_), channel_id=1, source_target_pairs={{0,4},{4,0},{8,12},{12,8},{16,20},{20,16},{24,28},{28,24},{1,5},{5... | collective-permute-start | bytes 3145736 | tf_op jit(solution)/shard_map/ppermute | solution.py:885
  147.0 20.8 %copy-start.37 = (s32[8]{0:T(128)S(1)}, s32[8]{0:T(128)}, u32[]{:S(2)}) copy-start(s32[8]{0:T(128)} %param.22) | copy-start | bytes 100
  167.2 3.8 collective-permute-start.22
  169.0 23.2 %collective-permute-start.24 = (bf16[4,512,1024]{2,1,0:T(8,128)(2,1)}, bf16[4,512,1024]{2,1,0:T(8,128)(2,1)}, u32[]{:S(2)}, u32[]{:S(2)}) collective-permute-start(bf16[4,512,1024]{2,1,0:T(8,128)(2,1)} %get-tuple-element.175.act_ref.refs_2_), channel_id=1, source_target_pairs={{0,4},{4,0},{8,12},{12,8},{16,20},{20,16},{24,28},{28,24},{1,5},{5... | collective-permute-start | bytes 12582920 | tf_op jit(solution)/shard_map/ppermute | solution.py:885
  172.1 14.6 %copy-start.38 = (s32[8]{0:T(128)S(1)}, s32[8]{0:T(128)}, u32[]{:S(2)}) copy-start(s32[8]{0:T(128)} %param.22) | copy-start | bytes 100
  185.7 6.5 %collective-permute-start.23 = (bf16[512,1024]{1,0:T(8,128)(2,1)}, bf16[512,1024]{1,0:T(8,128)(2,1)S(1)}, u32[]{:S(2)}, u32[]{:S(2)}) collective-permute-start(bf16[512,1024]{1,0:T(8,128)(2,1)} %get-tuple-element.185.refs_0_.bg_ref), channel_id=1, source_target_pairs={{0,4},{4,0},{8,12},{12,8},{16,20},{20,16},{24,28},{28,24},{1,5},{5... | collective-permute-start | bytes 3145736 | tf_op jit(solution)/shard_map/ppermute | solution.py:885
  202.5 32.0 %collective-permute-start.26 = (bf16[512,1024]{1,0:T(8,128)(2,1)}, bf16[512,1024]{1,0:T(8,128)(2,1)}, u32[]{:S(2)}, u32[]{:S(2)}) collective-permute-start(bf16[512,1024]{1,0:T(8,128)(2,1)} %get-tuple-element.194.refs_0_), channel_id=1, source_target_pairs={{0,4},{4,0},{8,12},{12,8},{16,20},{20,16},{24,28},{28,24},{1,5},{5... | collective-permute-start | bytes 3145736 | tf_op jit(solution)/shard_map/ppermute | solution.py:885
  202.7 31.9 %collective-permute-start.25 = (bf16[2,4,128,1024]{3,2,1,0:T(8,128)(2,1)}, bf16[2,4,128,1024]{3,2,1,0:T(8,128)(2,1)}, u32[]{:S(2)}, u32[]{:S(2)}) collective-permute-start(bf16[2,4,128,1024]{3,2,1,0:T(8,128)(2,1)} %get-tuple-element.190), channel_id=1, source_target_pairs={{0,8},{4,20},{8,0},{12,28},{16,24},{20,4},{24,16},{28,12},{1,9},{5... | collective-permute-start | bytes 6291464 | tf_op jit(solution)/shard_map/ppermute | solution.py:885
  226.1 12.5 %collective-permute-start.28 = (bf16[4,512,1024]{2,1,0:T(8,128)(2,1)}, bf16[4,512,1024]{2,1,0:T(8,128)(2,1)}, u32[]{:S(2)}, u32[]{:S(2)}) collective-permute-start(bf16[4,512,1024]{2,1,0:T(8,128)(2,1)} %get-tuple-element.196.refs_2_), channel_id=1, source_target_pairs={{0,4},{4,0},{8,12},{12,8},{16,20},{20,16},{24,28},{28,24},{1,5},{5... | collective-permute-start | bytes 12582920 | tf_op jit(solution)/shard_map/ppermute | solution.py:885
  226.2 12.4 %collective-permute-start.29 = (bf16[512,1024]{1,0:T(8,128)(2,1)}, bf16[512,1024]{1,0:T(8,128)(2,1)}, u32[]{:S(2)}, u32[]{:S(2)}) collective-permute-start(bf16[512,1024]{1,0:T(8,128)(2,1)} %get-tuple-element.213.refs_4_.mg_ref), channel_id=1, source_target_pairs={{0,4},{4,0},{8,12},{12,8},{16,20},{20,16},{24,28},{28,24},{1,5},{5... | collective-permute-start | bytes 3145736 | tf_op jit(solution)/shard_map/ppermute | solution.py:885
  226.7 45.6 %all-to-all-start.2 = ((bf16[4,128,1024]{2,1,0:T(8,128)(2,1)}), bf16[4,128,1024]{2,1,0:T(8,128)(2,1)}, u32[]{:S(2)}, u32[]{:S(2)}) async-start(bf16[4,128,1024]{2,1,0:T(8,128)(2,1)} %bitcast.26), calls=%async_computation.2 | async-start | bytes 2097152 | tf_op jit(solution)/shard_map/all_to_all | solution.py:904
  238.2 25.2 %collective-permute-start.27 = (bf16[4,128,1024]{2,1,0:T(8,128)(2,1)}, bf16[4,128,1024]{2,1,0:T(8,128)(2,1)}, u32[]{:S(2)}, u32[]{:S(2)}) collective-permute-start(bf16[4,128,1024]{2,1,0:T(8,128)(2,1)} %pass_on.3), channel_id=1, source_target_pairs={{0,16},{4,12},{8,24},{12,4},{16,0},{20,28},{24,8},{28,20},{1,17},{... | collective-permute-start | bytes 3145736 | tf_op jit(solution)/shard_map/ppermute | solution.py:885
  250.6 35.6 %collective-permute-start.30 = (bf16[2,4,128,1280]{3,2,1,0:T(8,128)(2,1)}, bf16[2,4,128,1280]{3,2,1,0:T(8,128)(2,1)}, u32[]{:S(2)}, u32[]{:S(2)}) collective-permute-start(bf16[2,4,128,1280]{3,2,1,0:T(8,128)(2,1)} %get-tuple-element.215), channel_id=1, source_target_pairs={{0,8},{4,20},{8,0},{12,28},{16,24},{20,4},{24,16},{28,12},{1,9},{5... | collective-permute-start | bytes 7864328 | tf_op jit(solution)/shard_map/ppermute | solution.py:885
  267.4 49.1 %collective-permute-start.34 = (bf16[128,1024]{1,0:T(8,128)(2,1)}, bf16[128,1024]{1,0:T(8,128)(2,1)}, u32[]{:S(2)}, u32[]{:S(2)}) collective-permute-start(bf16[128,1024]{1,0:T(8,128)(2,1)} %get-tuple-element.210), channel_id=1, source_target_pairs={{0,3},{1,0},{2,1},{3,2},{4,7},{5,4},{6,5},{7,6},{8,11},{9,8},{10,9... | collective-permute-start | bytes 786440 | tf_op jit(solution)/shard_map/ppermute | solution.py:897
  271.2 45.3 %collective-permute-start.35 = (bf16[128,1024]{1,0:T(8,128)(2,1)}, bf16[128,1024]{1,0:T(8,128)(2,1)}, u32[]{:S(2)}, u32[]{:S(2)}) collective-permute-start(bf16[128,1024]{1,0:T(8,128)(2,1)} %get-tuple-element.211), channel_id=1, source_target_pairs={{0,2},{1,3},{2,0},{3,1},{4,6},{5,7},{6,4},{7,5},{8,10},{9,11},{10,... | collective-permute-start | bytes 786440 | tf_op jit(solution)/shard_map/ppermute | solution.py:897
  271.2 45.3 %collective-permute-start.36 = (bf16[128,1024]{1,0:T(8,128)(2,1)}, bf16[128,1024]{1,0:T(8,128)(2,1)}, u32[]{:S(2)}, u32[]{:S(2)}) collective-permute-start(bf16[128,1024]{1,0:T(8,128)(2,1)} %get-tuple-element.212), channel_id=1, source_target_pairs={{0,1},{1,2},{2,3},{3,0},{4,5},{5,6},{6,7},{7,4},{8,9},{9,10},{10,1... | collective-permute-start | bytes 786440 | tf_op jit(solution)/shard_map/ppermute | solution.py:897
  272.3 12.3 %copy-start.24 = (f32[2,1,768]{2,1,0:T(1,128)S(1)}, f32[2,1,768]{2,1,0:T(1,128)}, u32[]{:S(2)}) copy-start(f32[2,1,768]{2,1,0:T(1,128)} %get-tuple-element.241) | copy-start | bytes 18436
  283.9 19.8 %collective-permute-start.31 = (bf16[4,512,768]{2,1,0:T(8,128)(2,1)}, bf16[4,512,768]{2,1,0:T(8,128)(2,1)}, u32[]{:S(2)}, u32[]{:S(2)}) collective-permute-start(bf16[4,512,768]{2,1,0:T(8,128)(2,1)} %get-tuple-element.220.pg_ref.refs_2_), channel_id=1, source_target_pairs={{0,4},{4,0},{8,12},{12,8},{16,20},{20,16},{24,28},{28,24},{1,5},{5... | collective-permute-start | bytes 9437192 | tf_op jit(solution)/shard_map/ppermute | solution.py:885
  290.0 26.6 %collective-permute-start.33 = (bf16[4,128,1280]{2,1,0:T(8,128)(2,1)}, bf16[4,128,1280]{2,1,0:T(8,128)(2,1)}, u32[]{:S(2)}, u32[]{:S(2)}) collective-permute-start(bf16[4,128,1280]{2,1,0:T(8,128)(2,1)} %pass_on.4), channel_id=1, source_target_pairs={{0,16},{4,12},{8,24},{12,4},{16,0},{20,28},{24,8},{28,20},{1,17},{... | collective-permute-start | bytes 3932168 | tf_op jit(solution)/shard_map/ppermute | solution.py:885
  299.4 39.0 %all-to-all-start.3 = ((bf16[4,128,1024]{2,1,0:T(8,128)(2,1)}), bf16[4,128,1024]{2,1,0:T(8,128)(2,1)}, u32[]{:S(2)}, u32[]{:S(2)}) async-start(bf16[4,128,1024]{2,1,0:T(8,128)(2,1)} %bitcast.86), calls=%async_computation.3 | async-start | bytes 2097152 | tf_op jit(solution)/shard_map/all_to_all | solution.py:904
  303.7 12.0 %copy-start.28 = (f32[2]{0:T(128)S(1)}, f32[2]{0:T(128)}, u32[]{:S(2)}) copy-start(f32[2]{0:T(128)} %pad_maximum_fusion.5) | copy-start | bytes 28
  303.7 12.0 %copy-start.6 = (f32[32,32]{1,0:T(8,128)S(1)}, f32[32,32]{1,0:T(8,128)}, u32[]{:S(2)}) copy-start(f32[32,32]{1,0:T(8,128)} %reshape_squeeze.21) | copy-start | bytes 12292
  303.7 12.0 %copy-start.7 = (f32[32,32]{1,0:T(8,128)S(1)}, f32[32,32]{1,0:T(8,128)}, u32[]{:S(2)}) copy-start(f32[32,32]{1,0:T(8,128)} %reshape_squeeze.22) | copy-start | bytes 12292
  303.7 12.0 %copy-start.8 = (f32[32,32]{1,0:T(8,128)S(1)}, f32[32,32]{1,0:T(8,128)}, u32[]{:S(2)}) copy-start(f32[32,32]{1,0:T(8,128)} %reshape_squeeze.23) | copy-start | bytes 12292
  303.8 12.0 %copy-start.9 = (f32[32,32]{1,0:T(8,128)S(1)}, f32[32,32]{1,0:T(8,128)}, u32[]{:S(2)}) copy-start(f32[32,32]{1,0:T(8,128)} %reshape_squeeze.18) | copy-start | bytes 12292
  303.8 12.0 %copy-start.10 = (f32[32,32]{1,0:T(8,128)S(1)}, f32[32,32]{1,0:T(8,128)}, u32[]{:S(2)}) copy-start(f32[32,32]{1,0:T(8,128)} %reshape_squeeze.19) | copy-start | bytes 12292
  303.8 12.0 %copy-start.11 = (f32[32,32]{1,0:T(8,128)S(1)}, f32[32,32]{1,0:T(8,128)}, u32[]{:S(2)}) copy-start(f32[32,32]{1,0:T(8,128)} %reshape_squeeze.20) | copy-start | bytes 12292
  303.8 12.0 %copy-start.12 = (f32[32,32]{1,0:T(8,128)S(1)}, f32[32,32]{1,0:T(8,128)}, u32[]{:S(2)}) copy-start(f32[32,32]{1,0:T(8,128)} %reshape_reshape.10) | copy-start | bytes 12292
  303.8 12.0 %copy-start.13 = (f32[32,32]{1,0:T(8,128)S(1)}, f32[32,32]{1,0:T(8,128)}, u32[]{:S(2)}) copy-start(f32[32,32]{1,0:T(8,128)} %reshape_reshape.9) | copy-start | bytes 12292
  303.8 12.0 %copy-start.14 = (f32[32,128]{1,0:T(8,128)S(1)}, f32[32,128]{1,0:T(8,128)}, u32[]{:S(2)}) copy-start(f32[32,128]{1,0:T(8,128)} %reshape_reshape.11) | copy-start | bytes 49156
  312.9 20.7 %collective-permute-start.32 = (bf16[2,4,128,768]{3,2,1,0:T(8,128)(2,1)}, bf16[2,4,128,768]{3,2,1,0:T(8,128)(2,1)}, u32[]{:S(2)}, u32[]{:S(2)}) collective-permute-start(bf16[2,4,128,768]{3,2,1,0:T(8,128)(2,1)} %get-tuple-element.222), channel_id=1, source_target_pairs={{0,8},{4,20},{8,0},{12,28},{16,24},{20,4},{24,16},{28,12},{1,9},{5... | collective-permute-start | bytes 4718600 | tf_op jit(solution)/shard_map/ppermute | solution.py:885
  320.9 30.3 %collective-permute-start.41 = (bf16[128,1280]{1,0:T(8,128)(2,1)}, bf16[128,1280]{1,0:T(8,128)(2,1)}, u32[]{:S(2)}, u32[]{:S(2)}) collective-permute-start(bf16[128,1280]{1,0:T(8,128)(2,1)} %get-tuple-element.225), channel_id=1, source_target_pairs={{0,3},{1,0},{2,1},{3,2},{4,7},{5,4},{6,5},{7,6},{8,11},{9,8},{10,9... | collective-permute-start | bytes 983048 | tf_op jit(solution)/shard_map/ppermute | solution.py:897
  324.7 34.7 %collective-permute-start.42 = (bf16[128,1280]{1,0:T(8,128)(2,1)}, bf16[128,1280]{1,0:T(8,128)(2,1)}, u32[]{:S(2)}, u32[]{:S(2)}) collective-permute-start(bf16[128,1280]{1,0:T(8,128)(2,1)} %get-tuple-element.226), channel_id=1, source_target_pairs={{0,2},{1,3},{2,0},{3,1},{4,6},{5,7},{6,4},{7,5},{8,10},{9,11},{10,... | collective-permute-start | bytes 983048 | tf_op jit(solution)/shard_map/ppermute | solution.py:897
  324.7 34.6 %collective-permute-start.43 = (bf16[128,1280]{1,0:T(8,128)(2,1)}, bf16[128,1280]{1,0:T(8,128)(2,1)}, u32[]{:S(2)}, u32[]{:S(2)}) collective-permute-start(bf16[128,1280]{1,0:T(8,128)(2,1)} %get-tuple-element.227), channel_id=1, source_target_pairs={{0,1},{1,2},{2,3},{3,0},{4,5},{5,6},{6,7},{7,4},{8,9},{9,10},{10,1... | collective-permute-start | bytes 983048 | tf_op jit(solution)/shard_map/ppermute | solution.py:897
  337.2 24.7 %collective-permute-start.37 = (bf16[4,128,768]{2,1,0:T(8,128)(2,1)}, bf16[4,128,768]{2,1,0:T(8,128)(2,1)}, u32[]{:S(2)}, u32[]{:S(2)}) collective-permute-start(bf16[4,128,768]{2,1,0:T(8,128)(2,1)} %pass_on.5), channel_id=1, source_target_pairs={{0,16},{4,12},{8,24},{12,4},{16,0},{20,28},{24,8},{28,20},{1,17},{... | collective-permute-start | bytes 2359304 | tf_op jit(solution)/shard_map/ppermute | solution.py:885
  339.1 21.3 %all-to-all-start.4 = ((f32[32,1,418]{2,1,0:T(1,128)}), f32[32,1,418]{2,1,0:T(1,128)}, u32[]{:S(2)}, u32[]{:S(2)}) async-start(f32[32,1,418]{2,1,0:T(1,128)} %copy.66), calls=%async_computation.4 | async-start | bytes 131072 | tf_op jit(solution)/shard_map/all_to_all | solution.py:1071
  366.9 16.9 %collective-permute-start.38 = (bf16[128,768]{1,0:T(8,128)(2,1)}, bf16[128,768]{1,0:T(8,128)(2,1)}, u32[]{:S(2)}, u32[]{:S(2)}) collective-permute-start(bf16[128,768]{1,0:T(8,128)(2,1)} %get-tuple-element.235), channel_id=1, source_target_pairs={{0,3},{1,0},{2,1},{3,2},{4,7},{5,4},{6,5},{7,6},{8,11},{9,8},{10,9... | collective-permute-start | bytes 589832 | tf_op jit(solution)/shard_map/ppermute | solution.py:897
  369.2 17.6 %collective-permute-start.39 = (bf16[128,768]{1,0:T(8,128)(2,1)}, bf16[128,768]{1,0:T(8,128)(2,1)}, u32[]{:S(2)}, u32[]{:S(2)}) collective-permute-start(bf16[128,768]{1,0:T(8,128)(2,1)} %get-tuple-element.236), channel_id=1, source_target_pairs={{0,2},{1,3},{2,0},{3,1},{4,6},{5,7},{6,4},{7,5},{8,10},{9,11},{10,... | collective-permute-start | bytes 589832 | tf_op jit(solution)/shard_map/ppermute | solution.py:897
  369.2 17.6 %collective-permute-start.40 = (bf16[128,768]{1,0:T(8,128)(2,1)}, bf16[128,768]{1,0:T(8,128)(2,1)}, u32[]{:S(2)}, u32[]{:S(2)}) collective-permute-start(bf16[128,768]{1,0:T(8,128)(2,1)} %get-tuple-element.237), channel_id=1, source_target_pairs={{0,1},{1,2},{2,3},{3,0},{4,5},{5,6},{6,7},{7,4},{8,9},{9,10},{10,1... | collective-permute-start | bytes 589832 | tf_op jit(solution)/shard_map/ppermute | solution.py:897
  (24 other events, 93.6 us)

commit v2 on v0

--- a/solution.py
+++ b/solution.py
@@ -289,18 +289,15 @@
 
     g_up.wait(up_refs, place, wu, u_sems, s)
     units = wu.shape[-1]
-
-    def columns(n, _):
-        span = pl.ds(pl.multiple_of(n * 256, 256), 256)
+    for n in range(units // 256):
+        span = slice(n * 256, (n + 1) * 256)
         u = dot(low_ref[...], wu[s, :, :, span].reshape(width, 256), ((1,), (0,)))
         u = u + bias_ref[0, :, span]
         phi = 0.5 + 0.5 * lax.erf(u * (2.0**-0.5))
         act_ref[0, :, span] = (u * phi).astype(bf16)
-        slope = phi + u * jnp.exp(-0.5 * u * u) * (2.0 * math.pi) ** -0.5
-        slope_ref[0, :, span] = slope.astype(bf16)
-        return 0
-
-    lax.fori_loop(0, units // 256, columns, 0)
+        slope_ref[0, :, span] = (
+            phi + u * jnp.exp(-0.5 * u * u) * (2.0 * math.pi) ** -0.5
+        ).astype(bf16)
 
     @pl.when(s == shards - 1)
     def _():

time: 392 us -> 390 us (level)
  transfers between devices with their start and end apart: 49 -> 49, of which waited for: 9 -> 10; matrix products, arithmetic and copies ran while one was open for 10% -> 10% of each run, Pallas kernels for 45% -> 44%
where the time goes in v2:
time: 390 us; the launch traced here: 388 us
  Pallas kernels  192 us (49%)
  starting transfers between devices  89.8 us (23%)
  waiting for transfers between devices  52.7 us (14%)
  local copies, waits for them, and re-layouts  36.3 us (9%)
  other arithmetic  8.93 us (2%)
  between operations  5.93 us (2%)
    ppermute x18, starting transfers between devices, shift(): return lax.ppermute(x, 'mp', [(i, (i + s) % mpn) for i in range(mpn)])  41.1 us
    ppermute x18, waiting for transfers between devices, shift(): return lax.ppermute(x, 'mp', [(i, (i + s) % mpn) for i in range(mpn)])  30.9 us
    pallas_call x3, Pallas kernels, weight_grad(): pl.pallas_call(functools.partial(weight_grad_body, len(groups), looped),...  30.3 us
    pallas_call x4, Pallas kernels, attend(): pl.pallas_call(functools.partial(attend_body, shard, gathered), grid=(pai...  28.3 us
    pallas_call x2, Pallas kernels, attend_back(): pl.pallas_call(attend_back_body, grid=(count, pairs), out_shape=[jax.Shap...  23.1 us
    pallas_call x1, Pallas kernels, up_back(): pl.pallas_call(functools.partial(up_back_body, shards, g_down, g_up), gri...  21.8 us
    pallas_call x1, Pallas kernels, up_project(): pl.pallas_call(functools.partial(up_body, shards, g_out, g_up), grid=(sha...  19.4 us
    ppermute x26, starting transfers between devices, exchange(): return lax.ppermute(x, 'dp', pairs)  17.6 us
  transfers between devices with their start and end apart: 49, of which 10 were waited for; matrix products, arithmetic and copies ran while one was open for 10% of the time, Pallas kernels for 44%

profile of v2, /device:TPU:0, one launch (start us, length us, event | category | flops | bytes accessed | tf_op | source)
XLA Modules:
  0.0 388.2 jit_solution(13748084739077292982)
XLA Ops:
  3.7 3.1 collective-permute-start
  6.8 2.6 collective-permute-start.1
  12.3 1.8 dynamic-slice_bitcast_fusion
  14.1 2.0 concatenate.63
  16.1 7.0 %collective-permute-done.1.refs_1_ = bf16[3,136,256]{2,1,0:T(8,128)(2,1)S(1)} collective-permute-done((bf16[3,136,256]{2,1,0:T(8,128)(2,1)S(1)}, bf16[3,136,256]{2,1,0:T(8,128)(2,1)S(1)}, u32[]{:S(2)}, u32[]{:S(2)}) %collective-permute-start.1) | collective-permute-done | bytes 208928 | tf_op jit(solution)/shard_map/ppermute | solution.py:894
  23.8 2.1 pack.6
  25.9 1.5 collective-permute-start.6
  28.2 4.9 %collective-permute-start.3 = (bf16[168,1024]{1,0:T(8,128)(2,1)}, bf16[168,1024]{1,0:T(8,128)(2,1)}, u32[]{:S(2)}, u32[]{:S(2)}) collective-permute-start(bf16[168,1024]{1,0:T(8,128)(2,1)} %concatenate.63), channel_id=1, source_target_pairs={{0,1},{1,2},{2,3},{3,0},{4,5},{5,6},{6,7},{7,4},{8,9},{9,10},{10,1... | collective-permute-start | bytes 1032200 | tf_op jit(solution)/shard_map/ppermute | solution.py:894
  33.0 1.7 collective-permute-start.4
  36.7 4.3 %all-to-all-start = ((bf16[4,128,1024]{2,1,0:T(8,128)(2,1)}), bf16[4,128,1024]{2,1,0:T(8,128)(2,1)}, u32[]{:S(2)}, u32[]{:S(2)}) async-start(bf16[4,128,1024]{2,1,0:T(8,128)(2,1)} %bitcast.76), calls=%async_computation | async-start | bytes 2097152 | tf_op jit(solution)/shard_map/all_to_all | solution.py:897
  41.8 2.3 pack.7.refs_1_
  44.1 1.6 collective-permute-start.8
  45.7 12.7 %collective-permute-done.4.refs_1_ = bf16[168,1024]{1,0:T(8,128)(2,1)} collective-permute-done((bf16[168,1024]{1,0:T(8,128)(2,1)}, bf16[168,1024]{1,0:T(8,128)(2,1)}, u32[]{:S(2)}, u32[]{:S(2)}) %collective-permute-start.4) | collective-permute-done | bytes 344096 | tf_op jit(solution)/shard_map/ppermute | solution.py:894
  58.4 2.2 pack.8
  66.7 2.6 embed.1.te_ref
  70.0 5.1 %collective-permute-done.7.refs_1_ = bf16[3,160,1024]{2,1,0:T(8,128)(2,1)} collective-permute-done((bf16[3,160,1024]{2,1,0:T(8,128)(2,1)}, bf16[3,160,1024]{2,1,0:T(8,128)(2,1)}, u32[]{:S(2)}, u32[]{:S(2)}) %collective-permute-start.7) | collective-permute-done | bytes 983072 | tf_op jit(solution)/shard_map/ppermute | solution.py:882
  75.1 2.8 pack.9.refs_1_.refs_6_
  78.0 2.1 collective-permute-start.15
  80.2 5.9 %all-to-all-done = bf16[4,128,1024]{2,1,0:T(8,128)(2,1)} async-done(((bf16[4,128,1024]{2,1,0:T(8,128)(2,1)}), bf16[4,128,1024]{2,1,0:T(8,128)(2,1)}, u32[]{:S(2)}, u32[]{:S(2)}) %all-to-all-start) | async-done | bytes 1048608 | tf_op jit(solution)/shard_map/all_to_all | solution.py:897
  86.1 2.4 add_convert_fusion.x_hbm.refs_0_
  88.5 10.4 %collective-permute-start.11 = (bf16[128,1024]{1,0:T(8,128)(2,1)}, bf16[128,1024]{1,0:T(8,128)(2,1)}, u32[]{:S(2)}, u32[]{:S(2)}) collective-permute-start(bf16[128,1024]{1,0:T(8,128)(2,1)} %get-tuple-element.154), channel_id=1, source_target_pairs={{0,1},{1,2},{2,3},{3,0},{4,5},{5,6},{6,7},{7,4},{8,9},{9,10},{10,1... | collective-permute-start | bytes 786440 | tf_op jit(solution)/shard_map/ppermute | solution.py:894
  98.9 3.4 collective-permute-start.12
  102.3 7.0 %attend.4 = (bf16[4,512,768]{2,1,0:T(8,128)(2,1)}, bf16[4,4,512,512]{3,2,1,0:T(8,128)(2,1)}, bf16[4,512,256]{2,1,0:T(8,128)(2,1)}) custom-call(s32[1]{0:T(128)} %bitcast.place_ref, bf16[512,1024]{1,0:T(8,128)(2,1)} %add_convert_fusion.x_hbm.refs_0_, f32[1,3,1,256]{3,2,1,0:T(1,128)} %broadcast_in_dim_broadcast_in_dim.3.bias_ref, bf16[3,8,128,256]{3,2,1,0:T(8,128)(2,1)} %bitcast.81), custom_call_target="tpu_custom_call" | custom-call | flops 344999985152 | tf_op jit(solution)/shard_map/attend/pallas_call | solution.py:218
  109.3 7.1 %attend.5 = (bf16[4,512,768]{2,1,0:T(8,128)(2,1)}, bf16[4,4,512,512]{3,2,1,0:T(8,128)(2,1)}, bf16[4,512,256]{2,1,0:T(8,128)(2,1)}) custom-call(s32[1]{0:T(128)} %bitcast.place_ref, bf16[512,1024]{1,0:T(8,128)(2,1)} %add_convert_fusion.x_hbm.refs_0_, ...), custom_call_target="tpu_custom_call", output_to_operand_aliasing={{0}: (8, {}), {1}: (9, {}), {2}: (10, {})} | custom-call | flops 344999985152 | tf_op jit(solution)/shard_map/attend/pallas_call | solution.py:218
  116.5 7.1 %attend.6 = (bf16[4,512,768]{2,1,0:T(8,128)(2,1)}, bf16[4,4,512,512]{3,2,1,0:T(8,128)(2,1)}, bf16[4,512,256]{2,1,0:T(8,128)(2,1)}) custom-call(s32[1]{0:T(128)} %bitcast.place_ref, bf16[512,1024]{1,0:T(8,128)(2,1)} %add_convert_fusion.x_hbm.refs_0_, ...), custom_call_target="tpu_custom_call", output_to_operand_aliasing={{0}: (8, {}), {1}: (9, {}), {2}: (10, {})} | custom-call | flops 344999985152 | tf_op jit(solution)/shard_map/attend/pallas_call | solution.py:218
  123.6 2.0 pack.10.refs_0_
  126.2 7.1 %attend.7 = (bf16[4,512,768]{2,1,0:T(8,128)(2,1)}, bf16[4,4,512,512]{3,2,1,0:T(8,128)(2,1)}, bf16[4,512,256]{2,1,0:T(8,128)(2,1)}) custom-call(s32[1]{0:T(128)} %bitcast.place_ref, bf16[512,1024]{1,0:T(8,128)(2,1)} %add_convert_fusion.x_hbm.refs_0_, ...), custom_call_target="tpu_custom_call", output_to_operand_aliasing={{0}: (8, {}), {1}: (9, {}), {2}: (10, {})} | custom-call | flops 344999985152 | tf_op jit(solution)/shard_map/attend/pallas_call | solution.py:218
  134.6 7.6 %all-to-all-start.1 = ((bf16[4,128,1024]{2,1,0:T(8,128)(2,1)}), bf16[4,128,1024]{2,1,0:T(8,128)(2,1)}, u32[]{:S(2)}, u32[]{:S(2)}) async-start(bf16[4,128,1024]{2,1,0:T(8,128)(2,1)} %bitcast.75), calls=%async_computation.1 | async-start | bytes 2097152 | tf_op jit(solution)/shard_map/all_to_all | solution.py:897
  142.3 2.6 pack.11.refs_1_
  144.9 1.6 collective-permute-start.18
  147.0 19.4 %up_project.1 = (f32[512,1024]{1,0:T(8,128)}, f32[512,128]{1,0:T(8,128)}, bf16[512,1024]{1,0:T(8,128)(2,1)}, bf16[4,512,1024]{2,1,0:T(8,128)(2,1)}, bf16[4,512,1...) custom-call(s32[1]{0:T(128)} %bitcast.place_ref, bf16[4,512,256]{2,1,0:T(8,128)(2,1)} %get-tuple-element.200.ctx_ref.refs_6_, ...), custom_call_target="tpu_custom_call" | custom-call | flops 344999985152 | tf_op jit(solution)/shard_map/up_project/pallas_call | solution.py:314
  171.4 13.6 %down_project.1 = (bf16[512,1024]{1,0:T(8,128)(2,1)}, bf16[512,1024]{1,0:T(8,128)(2,1)}, f32[3,1024]{1,0:T(4,128)}) custom-call(s32[1]{0:T(128)} %bitcast.place_ref, f32[1]{0:T(128)S(6)} %convert_element_type.37.live_ref, bf16[4,512,1024]{2,1,0:T(8,128)(2,1)} %get-tuple-element.175.act_ref.refs_2_, f32[1,1024]{1,0:T(1,128)} %bitcast.105, ...), custom_call_target="tpu_custom_call" | custom-call | flops 344999985152 | tf_op jit(solution)/shard_map/down_project/pallas_call | solution.py:425
  192.5 9.4 %weight_grad.3 = (bf16[2,4,128,1024]{3,2,1,0:T(8,128)(2,1)}, bf16[2,4,128,1024]{3,2,1,0:T(8,128)(2,1)}) custom-call(s32[1]{0:T(128)} %bitcast.place_ref, bf16[512,1024]{1,0:T(8,128)(2,1)} %get-tuple-element.185.refs_0_.bg_ref, bf16[512,1024]{1,0:T(8,128)(2,1)} %copy-done.30, bf16[4,512,1024]{2,1,0:T(8,128)(2,1)} %get-tuple-element.175.act_ref.refs_2_, ...), custom_call_target="tpu_custom_call" | custom-call | flops 344999985152 | tf_op jit(solution)/shard_map/weight_grad/pallas_call | solution.py:731
  202.0 1.6 collective-permute-start.25
  203.5 21.8 %up_back.1 = (bf16[4,512,1024]{2,1,0:T(8,128)(2,1)}, f32[4,1,1024]{2,1,0:T(1,128)}, f32[512,1024]{1,0:T(8,128)}, bf16[512,1024]{1,0:T(8,128)(2,1)}, f32[3,1024]{1,0:T(4,128)}) custom-call(s32[1]{0:T(128)} %bitcast.place_ref, bf16[512,1024]{1,0:T(8,128)(2,1)} %get-tuple-element.185.refs_0_.bg_ref, bf16[4,512,1024]{2,1,0:T(8,128)(2,1)} %get-tuple-element.186.slope_ref, ...), custom_call_target="tpu_custom_call" | custom-call | flops 344999985152 | tf_op jit(solution)/shard_map/up_back/pallas_call | solution.py:522
  226.0 5.1 %all-to-all-start.2 = ((bf16[4,128,1024]{2,1,0:T(8,128)(2,1)}), bf16[4,128,1024]{2,1,0:T(8,128)(2,1)}, u32[]{:S(2)}, u32[]{:S(2)}) async-start(bf16[4,128,1024]{2,1,0:T(8,128)(2,1)} %bitcast.26), calls=%async_computation.2 | async-start | bytes 2097152 | tf_op jit(solution)/shard_map/all_to_all | solution.py:901
  233.9 3.7 pass_on.3
  238.0 11.9 %weight_grad.4 = (bf16[2,4,128,1280]{3,2,1,0:T(8,128)(2,1)}, bf16[2,4,128,1280]{3,2,1,0:T(8,128)(2,1)}) custom-call(s32[1]{0:T(128)} %bitcast.place_ref, bf16[512,1024]{1,0:T(8,128)(2,1)} %get-tuple-element.194.refs_0_, bf16[512,1024]{1,0:T(8,128)(2,1)} %collective-permute-done.26.refs_1_, bf16[4,512,1024]{2,1,0:T(8,128)(2,1)} %get-tuple-element.196.refs_2_, ...), custom_call_target="tpu_custom_call" | custom-call | flops 344999985152 | tf_op jit(solution)/shard_map/weight_grad/pallas_call | solution.py:731
  251.1 11.5 %attend_back.2 = (bf16[4,512,768]{2,1,0:T(8,128)(2,1)}, f32[2,1,768]{2,1,0:T(1,128)}) custom-call(bf16[512,1024]{1,0:T(8,128)(2,1)} %get-tuple-element.213.refs_4_.mg_ref, bf16[4,256,1024]{2,1,0:T(8,128)(2,1)} %bitcast.78, bf16[4,512,768]{2,1,0:T(8,128)(2,1)} %get-tuple-element.205.qkv, bf16[4,4,512,512]{3,2,1,0:T(8,128)(2,1)} %get-tuple-element.206.p_of), custom_call_target="tpu_custom_call" | custom-call | flops 344999985152 | tf_op jit(solution)/shard_map/attend_back/pallas_call | solution.py:595
  262.7 4.0 %gather_up.3 = (f32[128,1024]{1,0:T(8,128)}, bf16[128,1024]{1,0:T(8,128)(2,1)}, bf16[128,1024]{1,0:T(8,128)(2,1)}, bf16[128,1024]{1,0:T(8,128)(2,1)}) custom-call(bf16[2,4,128,1024]{3,2,1,0:T(8,128)(2,1)} %get-tuple-element.184.keep_ref, bf16[2,4,128,1024]{3,2,1,0:T(8,128)(2,1)} %collective-permute-done.25.came_ref, ...), custom_call_target="tpu_custom_call" | custom-call | flops 1150000000 | tf_op jit(solution)/shard_map/gather_up/pallas_call | solution.py:795
  266.7 3.8 collective-permute-start.34
  271.6 11.6 %attend_back.3 = (bf16[4,512,768]{2,1,0:T(8,128)(2,1)}, f32[2,1,768]{2,1,0:T(1,128)}) custom-call(bf16[512,1024]{1,0:T(8,128)(2,1)} %get-tuple-element.213.refs_4_.mg_ref, bf16[4,256,1024]{2,1,0:T(8,128)(2,1)} %bitcast.79, bf16[4,512,768]{2,1,0:T(8,128)(2,1)} %get-tuple-element.205.qkv, ...), custom_call_target="tpu_custom_call", output_to_operand_aliasing={{0}: (4, {})} | custom-call | flops 1150000000 | tf_op jit(solution)/shard_map/attend_back/pallas_call | solution.py:595
  285.4 3.8 pass_on.4
  290.1 8.7 %input_back.1 = (bf16[512,1024]{1,0:T(8,128)(2,1)}, f32[1,1024]{1,0:T(1,128)}) custom-call(s32[1]{0:T(128)} %bitcast.place_ref, bf16[4,512,768]{2,1,0:T(8,128)(2,1)} %get-tuple-element.220.pg_ref.refs_2_, f32[512,1024]{1,0:T(8,128)} %get-tuple-element.218.gf_hbm, bf16[3,8,128,256]{3,2,1,0:T(8,128)(2,1)} %bitcast.85, ...), custom_call_target="tpu_custom_call" | custom-call | flops 1150000000 | tf_op jit(solution)/shard_map/input_back/pallas_call | solution.py:658
  298.7 4.2 %all-to-all-start.3 = ((bf16[4,128,1024]{2,1,0:T(8,128)(2,1)}), bf16[4,128,1024]{2,1,0:T(8,128)(2,1)}, u32[]{:S(2)}, u32[]{:S(2)}) async-start(bf16[4,128,1024]{2,1,0:T(8,128)(2,1)} %bitcast.86), calls=%async_computation.3 | async-start | bytes 2097152 | tf_op jit(solution)/shard_map/all_to_all | solution.py:901
  303.1 9.0 %weight_grad.5 = (bf16[2,4,128,768]{3,2,1,0:T(8,128)(2,1)}, bf16[2,4,128,768]{3,2,1,0:T(8,128)(2,1)}) custom-call(s32[1]{0:T(128)} %bitcast.place_ref, bf16[512,1024]{1,0:T(8,128)(2,1)} %add_convert_fusion.x_hbm.refs_0_, bf16[512,1024]{1,0:T(8,128)(2,1)} %collective-permute-done.21.refs_1_, bf16[4,512,768]{2,1,0:T(8,128)(2,1)} %get-tuple-element.220.pg_ref.refs_2_, ...), custom_call_target="tpu_custom_call" | custom-call | flops 344999985152 | tf_op jit(solution)/shard_map/weight_grad/pallas_call | solution.py:731
  312.2 1.6 collective-permute-start.32
  315.8 4.4 %gather_up.4 = (f32[128,1280]{1,0:T(8,128)}, bf16[128,1280]{1,0:T(8,128)(2,1)}, bf16[128,1280]{1,0:T(8,128)(2,1)}, bf16[128,1280]{1,0:T(8,128)(2,1)}) custom-call(bf16[2,4,128,1280]{3,2,1,0:T(8,128)(2,1)} %get-tuple-element.202.keep_ref, bf16[2,4,128,1280]{3,2,1,0:T(8,128)(2,1)} %collective-permute-done.30.came_ref, ...), custom_call_target="tpu_custom_call" | custom-call | flops 344999985152 | tf_op jit(solution)/shard_map/gather_up/pallas_call | solution.py:795
  320.2 3.8 collective-permute-start.41
  325.1 7.8 %collective-permute-done.32.came_ref = bf16[2,4,128,768]{3,2,1,0:T(8,128)(2,1)} collective-permute-done((bf16[2,4,128,768]{3,2,1,0:T(8,128)(2,1)}, bf16[2,4,128,768]{3,2,1,0:T(8,128)(2,1)}, u32[]{:S(2)}, u32[]{:S(2)}) %collective-permute-start.32) | collective-permute-done | bytes 1572896 | tf_op jit(solution)/shard_map/ppermute | solution.py:882
  332.9 3.6 pass_on.5
  338.4 9.8 %all-to-all-start.4 = ((f32[32,1,418]{2,1,0:T(1,128)}), f32[32,1,418]{2,1,0:T(1,128)}, u32[]{:S(2)}, u32[]{:S(2)}) async-start(f32[32,1,418]{2,1,0:T(1,128)} %copy.66), calls=%async_computation.4 | async-start | bytes 131072 | tf_op jit(solution)/shard_map/all_to_all | solution.py:1068
  348.2 2.3 finish.3
  350.5 8.2 %collective-permute-done.42.refs_2_ = bf16[128,1280]{1,0:T(8,128)(2,1)} collective-permute-done((bf16[128,1280]{1,0:T(8,128)(2,1)}, bf16[128,1280]{1,0:T(8,128)(2,1)}, u32[]{:S(2)}, u32[]{:S(2)}) %collective-permute-start.42) | collective-permute-done | bytes 327712 | tf_op jit(solution)/shard_map/ppermute | solution.py:894
  359.8 1.5 copy.75
  361.2 3.8 gather_up.5
  366.2 2.2 collective-permute-start.38
  370.1 1.5 convert_bitcast_fusion
  371.6 2.7 copy.68
  374.3 3.0 copy.67
  379.1 2.4 finish.5
  381.6 1.6 convolution_multiply_fusion.1
  383.2 2.9 collective-permute-done.39.refs_2_
  386.1 2.1 finish.4
  (212 shorter events, 47.4 us)
Async XLA Ops:
  0.6 64.4 %copy-start = (f32[32,1024]{1,0:T(8,128)S(1)}, f32[32,1024]{1,0:T(8,128)}, u32[]{:S(2)}) copy-start(f32[32,1024]{1,0:T(8,128)} %param.24) | copy-start | bytes 393220
  3.7 12.4 %collective-permute-start = (bf16[3,136,256]{2,1,0:T(8,128)(2,1)S(1)}, bf16[3,136,256]{2,1,0:T(8,128)(2,1)S(1)}, u32[]{:S(2)}, u32[]{:S(2)}) collective-permute-start(bf16[3,136,256]{2,1,0:T(8,128)(2,1)S(1)} %concatenate.65), channel_id=1, source_target_pairs={{0,1},{1,2},{2,3},{3,0},{4,5},{5,6},{6,7},{7,4},{8,9},{9,10},{10,1... | collective-permute-start | bytes 626696 | tf_op jit(solution)/shard_map/ppermute | solution.py:894
  6.8 16.3 %collective-permute-start.1 = (bf16[3,136,256]{2,1,0:T(8,128)(2,1)S(1)}, bf16[3,136,256]{2,1,0:T(8,128)(2,1)S(1)}, u32[]{:S(2)}, u32[]{:S(2)}) collective-permute-start(bf16[3,136,256]{2,1,0:T(8,128)(2,1)S(1)} %concatenate.65), channel_id=1, source_target_pairs={{0,2},{1,3},{2,0},{3,1},{4,6},{5,7},{6,4},{7,5},{8,10},{9,11},{10,... | collective-permute-start | bytes 626696 | tf_op jit(solution)/shard_map/ppermute | solution.py:894
  9.4 13.7 %collective-permute-start.2 = (bf16[3,136,256]{2,1,0:T(8,128)(2,1)S(1)}, bf16[3,136,256]{2,1,0:T(8,128)(2,1)S(1)}, u32[]{:S(2)}, u32[]{:S(2)}) collective-permute-start(bf16[3,136,256]{2,1,0:T(8,128)(2,1)S(1)} %concatenate.65), channel_id=1, source_target_pairs={{0,3},{1,0},{2,1},{3,2},{4,7},{5,4},{6,5},{7,6},{8,11},{9,8},{10,9... | collective-permute-start | bytes 626696 | tf_op jit(solution)/shard_map/ppermute | solution.py:894
  23.8 11.6 %copy-start.2 = (bf16[128,4,1024]{2,1,0:T(4,128)(2,1)S(1)}, bf16[128,4,1024]{2,1,0:T(4,128)(2,1)}, u32[]{:S(2)}) copy-start(bf16[128,4,1024]{2,1,0:T(4,128)(2,1)} %param.19) | copy-start | bytes 3145732
  25.9 15.0 %collective-permute-start.6 = (bf16[3,3,128,256]{3,2,1,0:T(8,128)(2,1)}, bf16[3,3,128,256]{3,2,1,0:T(8,128)(2,1)S(1)}, u32[]{:S(2)}, u32[]{:S(2)}) collective-permute-start(bf16[3,3,128,256]{3,2,1,0:T(8,128)(2,1)} %get-tuple-element.141.refs_0_), channel_id=1, source_target_pairs={{0,8},{4,20},{8,0},{12,28},{16,24},{20,4},{24,16},{28,12},{1,9},{5... | collective-permute-start | bytes 1769480 | tf_op jit(solution)/shard_map/ppermute | solution.py:882
  28.2 17.5 %collective-permute-start.3 = (bf16[168,1024]{1,0:T(8,128)(2,1)}, bf16[168,1024]{1,0:T(8,128)(2,1)}, u32[]{:S(2)}, u32[]{:S(2)}) collective-permute-start(bf16[168,1024]{1,0:T(8,128)(2,1)} %concatenate.63), channel_id=1, source_target_pairs={{0,1},{1,2},{2,3},{3,0},{4,5},{5,6},{6,7},{7,4},{8,9},{9,10},{10,1... | collective-permute-start | bytes 1032200 | tf_op jit(solution)/shard_map/ppermute | solution.py:894
  33.0 25.3 %collective-permute-start.4 = (bf16[168,1024]{1,0:T(8,128)(2,1)}, bf16[168,1024]{1,0:T(8,128)(2,1)}, u32[]{:S(2)}, u32[]{:S(2)}) collective-permute-start(bf16[168,1024]{1,0:T(8,128)(2,1)} %concatenate.63), channel_id=1, source_target_pairs={{0,2},{1,3},{2,0},{3,1},{4,6},{5,7},{6,4},{7,5},{8,10},{9,11},{10,... | collective-permute-start | bytes 1032200 | tf_op jit(solution)/shard_map/ppermute | solution.py:894
  34.7 23.7 %collective-permute-start.5 = (bf16[168,1024]{1,0:T(8,128)(2,1)}, bf16[168,1024]{1,0:T(8,128)(2,1)}, u32[]{:S(2)}, u32[]{:S(2)}) collective-permute-start(bf16[168,1024]{1,0:T(8,128)(2,1)} %concatenate.63), channel_id=1, source_target_pairs={{0,3},{1,0},{2,1},{3,2},{4,7},{5,4},{6,5},{7,6},{8,11},{9,8},{10,9... | collective-permute-start | bytes 1032200 | tf_op jit(solution)/shard_map/ppermute | solution.py:894
  36.7 49.4 %all-to-all-start = ((bf16[4,128,1024]{2,1,0:T(8,128)(2,1)}), bf16[4,128,1024]{2,1,0:T(8,128)(2,1)}, u32[]{:S(2)}, u32[]{:S(2)}) async-start(bf16[4,128,1024]{2,1,0:T(8,128)(2,1)} %bitcast.76), calls=%async_computation | async-start | bytes 2097152 | tf_op jit(solution)/shard_map/all_to_all | solution.py:897
  44.1 21.6 %collective-permute-start.8 = (bf16[2,3,3,128,256]{4,3,2,1,0:T(8,128)(2,1)}, bf16[2,3,3,128,256]{4,3,2,1,0:T(8,128)(2,1)}, u32[]{:S(2)}, u32[]{:S(2)}) collective-permute-start(bf16[2,3,3,128,256]{4,3,2,1,0:T(8,128)(2,1)} %pack.7.refs_1_), channel_id=1, source_target_pairs={{0,16},{4,12},{8,24},{12,4},{16,0},{20,28},{24,8},{28,20},{1,17},{... | collective-permute-start | bytes 3538952 | tf_op jit(solution)/shard_map/ppermute | solution.py:882
  45.7 29.4 %collective-permute-start.10 = (bf16[2,3,3,128,256]{4,3,2,1,0:T(8,128)(2,1)}, bf16[2,3,3,128,256]{4,3,2,1,0:T(8,128)(2,1)}, u32[]{:S(2)}, u32[]{:S(2)}) collective-permute-start(bf16[2,3,3,128,256]{4,3,2,1,0:T(8,128)(2,1)} %pack.7.refs_1_), channel_id=1, source_target_pairs={{0,4},{4,0},{8,12},{12,8},{16,20},{20,16},{24,28},{28,24},{1,5},{5... | collective-permute-start | bytes 3538952 | tf_op jit(solution)/shard_map/ppermute | solution.py:882
  60.6 14.5 %collective-permute-start.7 = (bf16[3,160,1024]{2,1,0:T(8,128)(2,1)}, bf16[3,160,1024]{2,1,0:T(8,128)(2,1)}, u32[]{:S(2)}, u32[]{:S(2)}) collective-permute-start(bf16[3,160,1024]{2,1,0:T(8,128)(2,1)} %get-tuple-element.146.refs_0_), channel_id=1, source_target_pairs={{0,8},{4,20},{8,0},{12,28},{16,24},{20,4},{24,16},{28,12},{1,9},{5... | collective-permute-start | bytes 2949128 | tf_op jit(solution)/shard_map/ppermute | solution.py:882
  65.7 9.4 %collective-permute-start.9 = (bf16[2,3,3,128,256]{4,3,2,1,0:T(8,128)(2,1)}, bf16[2,3,3,128,256]{4,3,2,1,0:T(8,128)(2,1)}, u32[]{:S(2)}, u32[]{:S(2)}) collective-permute-start(bf16[2,3,3,128,256]{4,3,2,1,0:T(8,128)(2,1)} %collective-permute-done.8.refs_2_), channel_id=1, source_target_pairs={{0,4},{4,0},{8,12},{12,8},{16,20},{20,16},{24,28},{28,24},{1,5},{5... | collective-permute-start | bytes 3538952 | tf_op jit(solution)/shard_map/ppermute | solution.py:882
  77.9 31.3 %collective-permute-start.14 = (bf16[2,3,160,1024]{3,2,1,0:T(8,128)(2,1)}, bf16[2,3,160,1024]{3,2,1,0:T(8,128)(2,1)}, u32[]{:S(2)}, u32[]{:S(2)}) collective-permute-start(bf16[2,3,160,1024]{3,2,1,0:T(8,128)(2,1)} %pack.9.refs_1_.refs_6_), channel_id=1, source_target_pairs={{0,4},{4,0},{8,12},{12,8},{16,20},{20,16},{24,28},{28,24},{1,5},{5... | collective-permute-start | bytes 5898248 | tf_op jit(solution)/shard_map/ppermute | solution.py:882
  78.0 38.4 %collective-permute-start.15 = (bf16[2,3,160,1024]{3,2,1,0:T(8,128)(2,1)}, bf16[2,3,160,1024]{3,2,1,0:T(8,128)(2,1)}, u32[]{:S(2)}, u32[]{:S(2)}) collective-permute-start(bf16[2,3,160,1024]{3,2,1,0:T(8,128)(2,1)} %pack.9.refs_1_.refs_6_), channel_id=1, source_target_pairs={{0,16},{4,12},{8,24},{12,4},{16,0},{20,28},{24,8},{28,20},{1,17},{... | collective-permute-start | bytes 5898248 | tf_op jit(solution)/shard_map/ppermute | solution.py:882
  88.5 35.1 %collective-permute-start.11 = (bf16[128,1024]{1,0:T(8,128)(2,1)}, bf16[128,1024]{1,0:T(8,128)(2,1)}, u32[]{:S(2)}, u32[]{:S(2)}) collective-permute-start(bf16[128,1024]{1,0:T(8,128)(2,1)} %get-tuple-element.154), channel_id=1, source_target_pairs={{0,1},{1,2},{2,3},{3,0},{4,5},{5,6},{6,7},{7,4},{8,9},{9,10},{10,1... | collective-permute-start | bytes 786440 | tf_op jit(solution)/shard_map/ppermute | solution.py:894
  98.9 24.7 %collective-permute-start.12 = (bf16[128,1024]{1,0:T(8,128)(2,1)}, bf16[128,1024]{1,0:T(8,128)(2,1)}, u32[]{:S(2)}, u32[]{:S(2)}) collective-permute-start(bf16[128,1024]{1,0:T(8,128)(2,1)} %get-tuple-element.154), channel_id=1, source_target_pairs={{0,2},{1,3},{2,0},{3,1},{4,6},{5,7},{6,4},{7,5},{8,10},{9,11},{10,... | collective-permute-start | bytes 786440 | tf_op jit(solution)/shard_map/ppermute | solution.py:894
  102.3 21.3 %collective-permute-start.13 = (bf16[128,1024]{1,0:T(8,128)(2,1)}, bf16[128,1024]{1,0:T(8,128)(2,1)}, u32[]{:S(2)}, u32[]{:S(2)}) collective-permute-start(bf16[128,1024]{1,0:T(8,128)(2,1)} %get-tuple-element.154), channel_id=1, source_target_pairs={{0,3},{1,0},{2,1},{3,2},{4,7},{5,4},{6,5},{7,6},{8,11},{9,8},{10,9... | collective-permute-start | bytes 786440 | tf_op jit(solution)/shard_map/ppermute | solution.py:894
  116.4 7.2 %collective-permute-start.16 = (bf16[2,3,160,1024]{3,2,1,0:T(8,128)(2,1)}, bf16[2,3,160,1024]{3,2,1,0:T(8,128)(2,1)}, u32[]{:S(2)}, u32[]{:S(2)}) collective-permute-start(bf16[2,3,160,1024]{3,2,1,0:T(8,128)(2,1)} %collective-permute-done.15.refs_2_.refs_7_), channel_id=1, source_target_pairs={{0,4},{4,0},{8,12},{12,8},{16,20},{20,16},{24,28},{28,24},{1,5},{5... | collective-permute-start | bytes 5898248 | tf_op jit(solution)/shard_map/ppermute | solution.py:882
  125.7 16.6 %collective-permute-start.17 = (bf16[3,128,1024]{2,1,0:T(8,128)(2,1)}, bf16[3,128,1024]{2,1,0:T(8,128)(2,1)}, u32[]{:S(2)}, u32[]{:S(2)}) collective-permute-start(bf16[3,128,1024]{2,1,0:T(8,128)(2,1)} %pack.10.refs_0_), channel_id=1, source_target_pairs={{0,8},{4,20},{8,0},{12,28},{16,24},{20,4},{24,16},{28,12},{1,9},{5... | collective-permute-start | bytes 2359304 | tf_op jit(solution)/shard_map/ppermute | solution.py:882
  134.6 34.9 %all-to-all-start.1 = ((bf16[4,128,1024]{2,1,0:T(8,128)(2,1)}), bf16[4,128,1024]{2,1,0:T(8,128)(2,1)}, u32[]{:S(2)}, u32[]{:S(2)}) async-start(bf16[4,128,1024]{2,1,0:T(8,128)(2,1)} %bitcast.75), calls=%async_computation.1 | async-start | bytes 2097152 | tf_op jit(solution)/shard_map/all_to_all | solution.py:897
  144.9 21.6 %collective-permute-start.18 = (bf16[2,3,128,1024]{3,2,1,0:T(8,128)(2,1)}, bf16[2,3,128,1024]{3,2,1,0:T(8,128)(2,1)}, u32[]{:S(2)}, u32[]{:S(2)}) collective-permute-start(bf16[2,3,128,1024]{3,2,1,0:T(8,128)(2,1)} %pack.11.refs_1_), channel_id=1, source_target_pairs={{0,16},{4,12},{8,24},{12,4},{16,0},{20,28},{24,8},{28,20},{1,17},{... | collective-permute-start | bytes 4718600 | tf_op jit(solution)/shard_map/ppermute | solution.py:882
  146.4 20.0 %collective-permute-start.19 = (bf16[2,3,128,1024]{3,2,1,0:T(8,128)(2,1)}, bf16[2,3,128,1024]{3,2,1,0:T(8,128)(2,1)}, u32[]{:S(2)}, u32[]{:S(2)}) collective-permute-start(bf16[2,3,128,1024]{3,2,1,0:T(8,128)(2,1)} %pack.11.refs_1_), channel_id=1, source_target_pairs={{0,4},{4,0},{8,12},{12,8},{16,20},{20,16},{24,28},{28,24},{1,5},{5... | collective-permute-start | bytes 4718600 | tf_op jit(solution)/shard_map/ppermute | solution.py:882
  146.4 20.0 %collective-permute-start.21 = (bf16[512,1024]{1,0:T(8,128)(2,1)}, bf16[512,1024]{1,0:T(8,128)(2,1)}, u32[]{:S(2)}, u32[]{:S(2)}) collective-permute-start(bf16[512,1024]{1,0:T(8,128)(2,1)} %add_convert_fusion.x_hbm.refs_0_), channel_id=1, source_target_pairs={{0,4},{4,0},{8,12},{12,8},{16,20},{20,16},{24,28},{28,24},{1,5},{5... | collective-permute-start | bytes 3145736 | tf_op jit(solution)/shard_map/ppermute | solution.py:882
  147.0 19.5 %collective-permute-start.20 = (bf16[4,512,256]{2,1,0:T(8,128)(2,1)}, bf16[4,512,256]{2,1,0:T(8,128)(2,1)}, u32[]{:S(2)}, u32[]{:S(2)}) collective-permute-start(bf16[4,512,256]{2,1,0:T(8,128)(2,1)} %get-tuple-element.200.ctx_ref.refs_6_), channel_id=1, source_target_pairs={{0,4},{4,0},{8,12},{12,8},{16,20},{20,16},{24,28},{28,24},{1,5},{5... | collective-permute-start | bytes 3145736 | tf_op jit(solution)/shard_map/ppermute | solution.py:882
  147.0 20.1 %copy-start.37 = (s32[8]{0:T(128)S(1)}, s32[8]{0:T(128)}, u32[]{:S(2)}) copy-start(s32[8]{0:T(128)} %param.22) | copy-start | bytes 100
  166.5 3.8 collective-permute-start.22
  168.3 23.2 %collective-permute-start.24 = (bf16[4,512,1024]{2,1,0:T(8,128)(2,1)}, bf16[4,512,1024]{2,1,0:T(8,128)(2,1)}, u32[]{:S(2)}, u32[]{:S(2)}) collective-permute-start(bf16[4,512,1024]{2,1,0:T(8,128)(2,1)} %get-tuple-element.175.act_ref.refs_2_), channel_id=1, source_target_pairs={{0,4},{4,0},{8,12},{12,8},{16,20},{20,16},{24,28},{28,24},{1,5},{5... | collective-permute-start | bytes 12582920 | tf_op jit(solution)/shard_map/ppermute | solution.py:882
  171.4 14.6 %copy-start.38 = (s32[8]{0:T(128)S(1)}, s32[8]{0:T(128)}, u32[]{:S(2)}) copy-start(s32[8]{0:T(128)} %param.22) | copy-start | bytes 100
  185.0 6.5 %collective-permute-start.23 = (bf16[512,1024]{1,0:T(8,128)(2,1)}, bf16[512,1024]{1,0:T(8,128)(2,1)S(1)}, u32[]{:S(2)}, u32[]{:S(2)}) collective-permute-start(bf16[512,1024]{1,0:T(8,128)(2,1)} %get-tuple-element.185.refs_0_.bg_ref), channel_id=1, source_target_pairs={{0,4},{4,0},{8,12},{12,8},{16,20},{20,16},{24,28},{28,24},{1,5},{5... | collective-permute-start | bytes 3145736 | tf_op jit(solution)/shard_map/ppermute | solution.py:882
  201.8 32.0 %collective-permute-start.26 = (bf16[512,1024]{1,0:T(8,128)(2,1)}, bf16[512,1024]{1,0:T(8,128)(2,1)}, u32[]{:S(2)}, u32[]{:S(2)}) collective-permute-start(bf16[512,1024]{1,0:T(8,128)(2,1)} %get-tuple-element.194.refs_0_), channel_id=1, source_target_pairs={{0,4},{4,0},{8,12},{12,8},{16,20},{20,16},{24,28},{28,24},{1,5},{5... | collective-permute-start | bytes 3145736 | tf_op jit(solution)/shard_map/ppermute | solution.py:882
  202.0 31.9 %collective-permute-start.25 = (bf16[2,4,128,1024]{3,2,1,0:T(8,128)(2,1)}, bf16[2,4,128,1024]{3,2,1,0:T(8,128)(2,1)}, u32[]{:S(2)}, u32[]{:S(2)}) collective-permute-start(bf16[2,4,128,1024]{3,2,1,0:T(8,128)(2,1)} %get-tuple-element.190), channel_id=1, source_target_pairs={{0,8},{4,20},{8,0},{12,28},{16,24},{20,4},{24,16},{28,12},{1,9},{5... | collective-permute-start | bytes 6291464 | tf_op jit(solution)/shard_map/ppermute | solution.py:882
  225.4 12.6 %collective-permute-start.28 = (bf16[4,512,1024]{2,1,0:T(8,128)(2,1)}, bf16[4,512,1024]{2,1,0:T(8,128)(2,1)}, u32[]{:S(2)}, u32[]{:S(2)}) collective-permute-start(bf16[4,512,1024]{2,1,0:T(8,128)(2,1)} %get-tuple-element.196.refs_2_), channel_id=1, source_target_pairs={{0,4},{4,0},{8,12},{12,8},{16,20},{20,16},{24,28},{28,24},{1,5},{5... | collective-permute-start | bytes 12582920 | tf_op jit(solution)/shard_map/ppermute | solution.py:882
  225.5 12.5 %collective-permute-start.29 = (bf16[512,1024]{1,0:T(8,128)(2,1)}, bf16[512,1024]{1,0:T(8,128)(2,1)}, u32[]{:S(2)}, u32[]{:S(2)}) collective-permute-start(bf16[512,1024]{1,0:T(8,128)(2,1)} %get-tuple-element.213.refs_4_.mg_ref), channel_id=1, source_target_pairs={{0,4},{4,0},{8,12},{12,8},{16,20},{20,16},{24,28},{28,24},{1,5},{5... | collective-permute-start | bytes 3145736 | tf_op jit(solution)/shard_map/ppermute | solution.py:882
  226.0 45.6 %all-to-all-start.2 = ((bf16[4,128,1024]{2,1,0:T(8,128)(2,1)}), bf16[4,128,1024]{2,1,0:T(8,128)(2,1)}, u32[]{:S(2)}, u32[]{:S(2)}) async-start(bf16[4,128,1024]{2,1,0:T(8,128)(2,1)} %bitcast.26), calls=%async_computation.2 | async-start | bytes 2097152 | tf_op jit(solution)/shard_map/all_to_all | solution.py:901
  237.5 25.1 %collective-permute-start.27 = (bf16[4,128,1024]{2,1,0:T(8,128)(2,1)}, bf16[4,128,1024]{2,1,0:T(8,128)(2,1)}, u32[]{:S(2)}, u32[]{:S(2)}) collective-permute-start(bf16[4,128,1024]{2,1,0:T(8,128)(2,1)} %pass_on.3), channel_id=1, source_target_pairs={{0,16},{4,12},{8,24},{12,4},{16,0},{20,28},{24,8},{28,20},{1,17},{... | collective-permute-start | bytes 3145736 | tf_op jit(solution)/shard_map/ppermute | solution.py:882
  250.0 35.4 %collective-permute-start.30 = (bf16[2,4,128,1280]{3,2,1,0:T(8,128)(2,1)}, bf16[2,4,128,1280]{3,2,1,0:T(8,128)(2,1)}, u32[]{:S(2)}, u32[]{:S(2)}) collective-permute-start(bf16[2,4,128,1280]{3,2,1,0:T(8,128)(2,1)} %get-tuple-element.215), channel_id=1, source_target_pairs={{0,8},{4,20},{8,0},{12,28},{16,24},{20,4},{24,16},{28,12},{1,9},{5... | collective-permute-start | bytes 7864328 | tf_op jit(solution)/shard_map/ppermute | solution.py:882
  266.7 49.2 %collective-permute-start.34 = (bf16[128,1024]{1,0:T(8,128)(2,1)}, bf16[128,1024]{1,0:T(8,128)(2,1)}, u32[]{:S(2)}, u32[]{:S(2)}) collective-permute-start(bf16[128,1024]{1,0:T(8,128)(2,1)} %get-tuple-element.210), channel_id=1, source_target_pairs={{0,3},{1,0},{2,1},{3,2},{4,7},{5,4},{6,5},{7,6},{8,11},{9,8},{10,9... | collective-permute-start | bytes 786440 | tf_op jit(solution)/shard_map/ppermute | solution.py:894
  270.5 45.3 %collective-permute-start.35 = (bf16[128,1024]{1,0:T(8,128)(2,1)}, bf16[128,1024]{1,0:T(8,128)(2,1)}, u32[]{:S(2)}, u32[]{:S(2)}) collective-permute-start(bf16[128,1024]{1,0:T(8,128)(2,1)} %get-tuple-element.211), channel_id=1, source_target_pairs={{0,2},{1,3},{2,0},{3,1},{4,6},{5,7},{6,4},{7,5},{8,10},{9,11},{10,... | collective-permute-start | bytes 786440 | tf_op jit(solution)/shard_map/ppermute | solution.py:894
  270.5 45.3 %collective-permute-start.36 = (bf16[128,1024]{1,0:T(8,128)(2,1)}, bf16[128,1024]{1,0:T(8,128)(2,1)}, u32[]{:S(2)}, u32[]{:S(2)}) collective-permute-start(bf16[128,1024]{1,0:T(8,128)(2,1)} %get-tuple-element.212), channel_id=1, source_target_pairs={{0,1},{1,2},{2,3},{3,0},{4,5},{5,6},{6,7},{7,4},{8,9},{9,10},{10,1... | collective-permute-start | bytes 786440 | tf_op jit(solution)/shard_map/ppermute | solution.py:894
  271.6 12.3 %copy-start.24 = (f32[2,1,768]{2,1,0:T(1,128)S(1)}, f32[2,1,768]{2,1,0:T(1,128)}, u32[]{:S(2)}) copy-start(f32[2,1,768]{2,1,0:T(1,128)} %get-tuple-element.241) | copy-start | bytes 18436
  283.2 19.8 %collective-permute-start.31 = (bf16[4,512,768]{2,1,0:T(8,128)(2,1)}, bf16[4,512,768]{2,1,0:T(8,128)(2,1)}, u32[]{:S(2)}, u32[]{:S(2)}) collective-permute-start(bf16[4,512,768]{2,1,0:T(8,128)(2,1)} %get-tuple-element.220.pg_ref.refs_2_), channel_id=1, source_target_pairs={{0,4},{4,0},{8,12},{12,8},{16,20},{20,16},{24,28},{28,24},{1,5},{5... | collective-permute-start | bytes 9437192 | tf_op jit(solution)/shard_map/ppermute | solution.py:882
  289.2 26.6 %collective-permute-start.33 = (bf16[4,128,1280]{2,1,0:T(8,128)(2,1)}, bf16[4,128,1280]{2,1,0:T(8,128)(2,1)}, u32[]{:S(2)}, u32[]{:S(2)}) collective-permute-start(bf16[4,128,1280]{2,1,0:T(8,128)(2,1)} %pass_on.4), channel_id=1, source_target_pairs={{0,16},{4,12},{8,24},{12,4},{16,0},{20,28},{24,8},{28,20},{1,17},{... | collective-permute-start | bytes 3932168 | tf_op jit(solution)/shard_map/ppermute | solution.py:882
  298.7 39.0 %all-to-all-start.3 = ((bf16[4,128,1024]{2,1,0:T(8,128)(2,1)}), bf16[4,128,1024]{2,1,0:T(8,128)(2,1)}, u32[]{:S(2)}, u32[]{:S(2)}) async-start(bf16[4,128,1024]{2,1,0:T(8,128)(2,1)} %bitcast.86), calls=%async_computation.3 | async-start | bytes 2097152 | tf_op jit(solution)/shard_map/all_to_all | solution.py:901
  303.0 12.0 %copy-start.28 = (f32[2]{0:T(128)S(1)}, f32[2]{0:T(128)}, u32[]{:S(2)}) copy-start(f32[2]{0:T(128)} %pad_maximum_fusion.5) | copy-start | bytes 28
  303.0 12.0 %copy-start.6 = (f32[32,32]{1,0:T(8,128)S(1)}, f32[32,32]{1,0:T(8,128)}, u32[]{:S(2)}) copy-start(f32[32,32]{1,0:T(8,128)} %reshape_squeeze.21) | copy-start | bytes 12292
  303.0 12.0 %copy-start.7 = (f32[32,32]{1,0:T(8,128)S(1)}, f32[32,32]{1,0:T(8,128)}, u32[]{:S(2)}) copy-start(f32[32,32]{1,0:T(8,128)} %reshape_squeeze.22) | copy-start | bytes 12292
  303.1 12.0 %copy-start.8 = (f32[32,32]{1,0:T(8,128)S(1)}, f32[32,32]{1,0:T(8,128)}, u32[]{:S(2)}) copy-start(f32[32,32]{1,0:T(8,128)} %reshape_squeeze.23) | copy-start | bytes 12292
  303.1 12.0 %copy-start.9 = (f32[32,32]{1,0:T(8,128)S(1)}, f32[32,32]{1,0:T(8,128)}, u32[]{:S(2)}) copy-start(f32[32,32]{1,0:T(8,128)} %reshape_squeeze.18) | copy-start | bytes 12292
  303.1 12.0 %copy-start.10 = (f32[32,32]{1,0:T(8,128)S(1)}, f32[32,32]{1,0:T(8,128)}, u32[]{:S(2)}) copy-start(f32[32,32]{1,0:T(8,128)} %reshape_squeeze.19) | copy-start | bytes 12292
  303.1 12.0 %copy-start.11 = (f32[32,32]{1,0:T(8,128)S(1)}, f32[32,32]{1,0:T(8,128)}, u32[]{:S(2)}) copy-start(f32[32,32]{1,0:T(8,128)} %reshape_squeeze.20) | copy-start | bytes 12292
  303.1 12.0 %copy-start.12 = (f32[32,32]{1,0:T(8,128)S(1)}, f32[32,32]{1,0:T(8,128)}, u32[]{:S(2)}) copy-start(f32[32,32]{1,0:T(8,128)} %reshape_reshape.10) | copy-start | bytes 12292
  303.1 12.0 %copy-start.13 = (f32[32,32]{1,0:T(8,128)S(1)}, f32[32,32]{1,0:T(8,128)}, u32[]{:S(2)}) copy-start(f32[32,32]{1,0:T(8,128)} %reshape_reshape.9) | copy-start | bytes 12292
  303.1 12.0 %copy-start.14 = (f32[32,128]{1,0:T(8,128)S(1)}, f32[32,128]{1,0:T(8,128)}, u32[]{:S(2)}) copy-start(f32[32,128]{1,0:T(8,128)} %reshape_reshape.11) | copy-start | bytes 49156
  312.2 20.7 %collective-permute-start.32 = (bf16[2,4,128,768]{3,2,1,0:T(8,128)(2,1)}, bf16[2,4,128,768]{3,2,1,0:T(8,128)(2,1)}, u32[]{:S(2)}, u32[]{:S(2)}) collective-permute-start(bf16[2,4,128,768]{3,2,1,0:T(8,128)(2,1)} %get-tuple-element.222), channel_id=1, source_target_pairs={{0,8},{4,20},{8,0},{12,28},{16,24},{20,4},{24,16},{28,12},{1,9},{5... | collective-permute-start | bytes 4718600 | tf_op jit(solution)/shard_map/ppermute | solution.py:882
  320.2 30.3 %collective-permute-start.41 = (bf16[128,1280]{1,0:T(8,128)(2,1)}, bf16[128,1280]{1,0:T(8,128)(2,1)}, u32[]{:S(2)}, u32[]{:S(2)}) collective-permute-start(bf16[128,1280]{1,0:T(8,128)(2,1)} %get-tuple-element.225), channel_id=1, source_target_pairs={{0,3},{1,0},{2,1},{3,2},{4,7},{5,4},{6,5},{7,6},{8,11},{9,8},{10,9... | collective-permute-start | bytes 983048 | tf_op jit(solution)/shard_map/ppermute | solution.py:894
  324.0 34.7 %collective-permute-start.42 = (bf16[128,1280]{1,0:T(8,128)(2,1)}, bf16[128,1280]{1,0:T(8,128)(2,1)}, u32[]{:S(2)}, u32[]{:S(2)}) collective-permute-start(bf16[128,1280]{1,0:T(8,128)(2,1)} %get-tuple-element.226), channel_id=1, source_target_pairs={{0,2},{1,3},{2,0},{3,1},{4,6},{5,7},{6,4},{7,5},{8,10},{9,11},{10,... | collective-permute-start | bytes 983048 | tf_op jit(solution)/shard_map/ppermute | solution.py:894
  324.0 34.7 %collective-permute-start.43 = (bf16[128,1280]{1,0:T(8,128)(2,1)}, bf16[128,1280]{1,0:T(8,128)(2,1)}, u32[]{:S(2)}, u32[]{:S(2)}) collective-permute-start(bf16[128,1280]{1,0:T(8,128)(2,1)} %get-tuple-element.227), channel_id=1, source_target_pairs={{0,1},{1,2},{2,3},{3,0},{4,5},{5,6},{6,7},{7,4},{8,9},{9,10},{10,1... | collective-permute-start | bytes 983048 | tf_op jit(solution)/shard_map/ppermute | solution.py:894
  336.5 24.7 %collective-permute-start.37 = (bf16[4,128,768]{2,1,0:T(8,128)(2,1)}, bf16[4,128,768]{2,1,0:T(8,128)(2,1)}, u32[]{:S(2)}, u32[]{:S(2)}) collective-permute-start(bf16[4,128,768]{2,1,0:T(8,128)(2,1)} %pass_on.5), channel_id=1, source_target_pairs={{0,16},{4,12},{8,24},{12,4},{16,0},{20,28},{24,8},{28,20},{1,17},{... | collective-permute-start | bytes 2359304 | tf_op jit(solution)/shard_map/ppermute | solution.py:882
  338.4 21.3 %all-to-all-start.4 = ((f32[32,1,418]{2,1,0:T(1,128)}), f32[32,1,418]{2,1,0:T(1,128)}, u32[]{:S(2)}, u32[]{:S(2)}) async-start(f32[32,1,418]{2,1,0:T(1,128)} %copy.66), calls=%async_computation.4 | async-start | bytes 131072 | tf_op jit(solution)/shard_map/all_to_all | solution.py:1068
  366.2 16.9 %collective-permute-start.38 = (bf16[128,768]{1,0:T(8,128)(2,1)}, bf16[128,768]{1,0:T(8,128)(2,1)}, u32[]{:S(2)}, u32[]{:S(2)}) collective-permute-start(bf16[128,768]{1,0:T(8,128)(2,1)} %get-tuple-element.235), channel_id=1, source_target_pairs={{0,3},{1,0},{2,1},{3,2},{4,7},{5,4},{6,5},{7,6},{8,11},{9,8},{10,9... | collective-permute-start | bytes 589832 | tf_op jit(solution)/shard_map/ppermute | solution.py:894
  368.5 17.6 %collective-permute-start.39 = (bf16[128,768]{1,0:T(8,128)(2,1)}, bf16[128,768]{1,0:T(8,128)(2,1)}, u32[]{:S(2)}, u32[]{:S(2)}) collective-permute-start(bf16[128,768]{1,0:T(8,128)(2,1)} %get-tuple-element.236), channel_id=1, source_target_pairs={{0,2},{1,3},{2,0},{3,1},{4,6},{5,7},{6,4},{7,5},{8,10},{9,11},{10,... | collective-permute-start | bytes 589832 | tf_op jit(solution)/shard_map/ppermute | solution.py:894
  368.5 17.6 %collective-permute-start.40 = (bf16[128,768]{1,0:T(8,128)(2,1)}, bf16[128,768]{1,0:T(8,128)(2,1)}, u32[]{:S(2)}, u32[]{:S(2)}) collective-permute-start(bf16[128,768]{1,0:T(8,128)(2,1)} %get-tuple-element.237), channel_id=1, source_target_pairs={{0,1},{1,2},{2,3},{3,0},{4,5},{5,6},{6,7},{7,4},{8,9},{9,10},{10,1... | collective-permute-start | bytes 589832 | tf_op jit(solution)/shard_map/ppermute | solution.py:894
  (24 other events, 93.6 us)
